TPU v7x, 128 devices: a whole 4x4x4 slice. The times are simulated.
128 devices in a mesh: outer: 4 (over x), inner: 32 (over z, y, core).
Axes of the slice: x: 4, y: 4, z: 4, core: 2. Of those that a mesh axis runs over, the one named last changes fastest.
Arguments:
- events: bfloat16 [16, 1048576], P(None, ('outer', 'inner')), may hold values from -6 to 6
- coeffs: bfloat16 [64, 1048576], P(None, ('outer', 'inner')), may hold values from -6 to 6
- tree_perm: int32 [128, 8192], P(('outer', 'inner')), may hold values from 0 to 8191, each once within a row
- near_list: int32 [2048, 32], P(('outer', 'inner')), may hold values from 0 to 2047, as said below
- near_count: int32 [2048], P(('outer', 'inner')), may hold values from 1 to 32, as said below
- far_list: int32 [2048, 16], P(('outer', 'inner')), may hold values from 0 to 31, as said below
- skel_low: int32 [128, 128], P(('outer', 'inner')), may hold values from 0 to 8191, as said below
- skel_high: int32 [4, 128], P('outer'), may hold values from 0 to 4095, as said below
Outputs:
- product: bfloat16 [64, 1048576], P(None, ('outer', 'inner'))
Inputs may be any that keep to these rules, and one draw needn't show every extreme that they name: `near_list`: slot 0 of leaf i is i; the first near_count[i] slots are distinct leaves within 8 leaves of the leaf's own lower node (i // 16) on either side; the other slots repeat i. `near_count`: some leaf has all 32 slots live. `far_list`: distinct within a leaf, never the leaf's own lower node nor the ones next to it. `skel_low`: distinct within a row. `skel_high`: distinct within a row.
All inputs are finite; a program needn't handle non-finite values.
Results may differ from a plain program's by a relative error of at most 0.006.
Values may be sent and summed in bfloat16 or wider, within the bound.
No kernel may reach another device: no remote copies, remote signals or barrier semaphores. Data moves between devices by JAX's collectives and lax.ppermute only.
A program may use at most 64 MiB of HBM per device.

v0:
```python
import functools

import jax
import jax.numpy as jnp
from jax import lax
from jax.experimental import pallas as pl
from jax.experimental.pallas import tpu as pltpu
from jax.sharding import PartitionSpec as P

LEAF = 512
RANK = 128
NEAR = 32
LEAF_DEV = 16
COLS = 64
FEAT = 16
LANES = 128
REACH = 8
LOW_ROUNDS = ((1,), (2,), (4,), (8, 16, 24))
NT = (((1,), (1,)), ((), ()))
NN = (((1,), (0,)), ((), ()))
VMEM_LIMIT = 24 << 20
LAST_LIMIT = 32 << 20

X0 = COLS
N0 = X0 + FEAT
O0 = N0 + 3


def dot(a, b, dims=NN):
    return lax.dot_general(a, b, dims, preferred_element_type=jnp.float32)


def target_map():
    k = lax.broadcasted_iota(jnp.int32, (LANES, LANES), 0)
    m = lax.broadcasted_iota(jnp.int32, (LANES, LANES), 1)
    quarter = (k == m) & (k >= X0) & (k < N0)
    ones = (k == m + 3) & (m >= N0) & (m < O0)
    pieces = (k + 3 == m) & (k >= N0) & (k < O0)
    return jnp.where(quarter, 0.25, jnp.where(ones | pieces, 1.0, 0.0)).astype(jnp.bfloat16)


def targets(rows):
    return dot(rows, target_map()).astype(jnp.bfloat16)


def weight_map():
    k = lax.broadcasted_iota(jnp.int32, (COLS, LANES), 0)
    m = lax.broadcasted_iota(jnp.int32, (COLS, LANES), 1)
    return jnp.where(k == m, 1.0, 0.0).astype(jnp.bfloat16)


def weights(rows):
    return dot(weight_map(), rows, NT).astype(jnp.bfloat16)


def block(i, size):
    return pl.ds(pl.multiple_of(i * size, size), size)


def cost(pairs):
    return pl.CostEstimate(
        flops=pairs * 2 * LEAF * LEAF * 384, bytes_accessed=4 << 20, transcendentals=pairs * LEAF * LEAF
    )


def features(xb):
    x = xb.astype(jnp.float32)
    n = jnp.sum(x * x, axis=0, keepdims=True) * -0.125
    n1 = n.astype(jnp.bfloat16).astype(jnp.float32)
    n2 = (n - n1).astype(jnp.bfloat16).astype(jnp.float32)
    n3 = (n - n1 - n2).astype(jnp.bfloat16).astype(jnp.float32)
    r = lax.broadcasted_iota(jnp.int32, xb.shape, 0)
    one = jnp.where(r < 6, 1.0, 0.0)
    ext = jnp.where(r == 0, n1, jnp.where(r == 1, n2, jnp.where(r == 2, n3, one)))
    pad = jnp.zeros((LANES - COLS - 2 * FEAT, xb.shape[1]), jnp.bfloat16)
    return [xb, ext.astype(jnp.bfloat16), pad]


def tree_kernel(
    perm_hbm, skel_hbm, events_hbm, coeffs_hbm, lo_out, hi_out, w_out, t_out, own_out,
    table, picked, spick, perm, skel, events, coeffs, sems,
):
    moves = [
        pltpu.make_async_copy(src, dst, sems.at[i])
        for i, (src, dst) in enumerate(
            [(events_hbm, events), (coeffs_hbm, coeffs), (perm_hbm, perm), (skel_hbm, skel)]
        )
    ]
    for m in moves:
        m.start()
    for m in moves:
        m.wait()
    chunks = events.shape[1] // LEAF

    def build(c, _):
        at = block(c, LEAF)
        full = jnp.concatenate([coeffs[:, at]] + features(events[:, at]), axis=0)
        table[at, :] = full.T.astype(jnp.float32)
        return 0

    lax.fori_loop(0, chunks, build, 0)

    def fetch(ids):
        return jnp.concatenate([table[pl.ds(i, 1), :] for i in ids], axis=0)

    for j in range(0, RANK, 8):
        spick[j : j + 8, :] = fetch([perm[0, skel[0, j + u]] for u in range(8)])

    step = 64

    def gather(rows_out, base, c, _):
        def some(b, _):
            for v in range(0, step, 8):
                e = (base + c) * LEAF + b * step + v
                picked[block(b * (step // 8) + v // 8, 8), :] = fetch(
                    [perm[0, e + u] for u in range(8)]
                )
            return 0

        lax.fori_loop(0, LEAF // step, some, 0)
        at = block(base + c, LEAF)
        r = picked[...]
        rb = r.astype(jnp.bfloat16)
        rows_out[block(c, LEAF), :] = rb
        w_out[:, at] = r.T[:COLS].astype(jnp.bfloat16)
        t_out[at, :] = targets(rb)
        return 0

    half = chunks // 2
    lax.fori_loop(0, half, functools.partial(gather, lo_out, 0), 0)
    lax.fori_loop(0, half, functools.partial(gather, hi_out, half), 0)

    s = spick[...]
    ts = targets(s.astype(jnp.bfloat16))
    su = halves_dot(lo_out, hi_out, w_out, ts) / events.shape[1] ** 0.5
    own_out[:COLS, :] = su.astype(jnp.bfloat16)
    own_out[COLS:, :] = s.T[X0:N0].astype(jnp.bfloat16)


def halves_dot(lo, hi, w, ts):
    half = lo.shape[0]
    ka = jnp.exp(dot(lo[...], ts, NT)).astype(jnp.bfloat16)
    kb = jnp.exp(dot(hi[...], ts, NT)).astype(jnp.bfloat16)
    return dot(w[:, :half], ka) + dot(w[:, half:], kb)


SMEM = pl.BlockSpec(memory_space=pltpu.SMEM)
VMEM = pl.BlockSpec(memory_space=pltpu.VMEM)
ANY = pl.BlockSpec(memory_space=pl.ANY)
HBM = pl.BlockSpec(memory_space=pltpu.HBM)


def params(limit=VMEM_LIMIT):
    return pltpu.CompilerParams(vmem_limit_bytes=limit)


def tree_call(perm, skel, events, coeffs):
    n = events.shape[1]
    return pl.pallas_call(
        tree_kernel,
        out_shape=(
            jax.ShapeDtypeStruct((n // 2, LANES), jnp.bfloat16),
            jax.ShapeDtypeStruct((n // 2, LANES), jnp.bfloat16),
            jax.ShapeDtypeStruct((COLS, n), jnp.bfloat16),
            jax.ShapeDtypeStruct((n, LANES), jnp.bfloat16),
            jax.ShapeDtypeStruct((COLS + FEAT, RANK), jnp.bfloat16),
        ),
        in_specs=[HBM] * 4,
        out_specs=(VMEM,) * 5,
        scratch_shapes=[
            pltpu.VMEM((n, LANES), jnp.float32),
            pltpu.VMEM((LEAF, LANES), jnp.float32),
            pltpu.VMEM((RANK, LANES), jnp.float32),
            pltpu.SMEM(perm.shape, jnp.int32),
            pltpu.SMEM(skel.shape, jnp.int32),
            pltpu.VMEM(events.shape, jnp.bfloat16),
            pltpu.VMEM(coeffs.shape, jnp.bfloat16),
            pltpu.SemaphoreType.DMA((4,)),
        ],
        compiler_params=params(),
        name="tree_rows",
    )(perm, skel, events, coeffs)


def event_rows(xb):
    none = jnp.zeros((COLS, xb.shape[1]), jnp.bfloat16)
    return jnp.concatenate([none] + features(xb), axis=0).T


def term_kernel(scale, parts, me, picks, *refs):
    pieces, (lo, hi, w, term_out, low_out, low_w, low_x) = refs[:parts], refs[parts:]
    each = COLS + FEAT
    blocks = pieces[0].shape[0] // each
    size = blocks * RANK
    for i, piece in enumerate(pieces):
        for b in range(blocks):
            at = slice((i * blocks + b) * RANK, (i * blocks + b + 1) * RANK)
            low_w[:, at] = piece[b * each : b * each + COLS, :]
            low_x[:, at] = piece[b * each + COLS : (b + 1) * each, :]
        at = slice(i * size, (i + 1) * size)
        low_out[at, :] = event_rows(low_x[:, at])
    p = picks[...]
    p = ((p // RANK) ^ me[0]) * RANK + p % RANK
    hit = lax.broadcasted_iota(jnp.int32, (parts * size, RANK), 0) == p
    hx = dot(low_x[...], jnp.where(hit, 1.0, 0.0).astype(jnp.bfloat16)).astype(jnp.bfloat16)
    term_out[COLS:, :] = hx
    term = halves_dot(lo, hi, w, targets(event_rows(hx))) * scale
    term_out[:COLS, :] = term.astype(jnp.bfloat16)


def term_call(scale, me, picks, pieces, lo, hi, w):
    total = len(pieces) * pieces[0].shape[0] // (COLS + FEAT) * RANK
    return pl.pallas_call(
        lambda *refs: term_kernel(scale, len(pieces), *refs),
        out_shape=(
            jax.ShapeDtypeStruct((COLS + FEAT, RANK), jnp.bfloat16),
            jax.ShapeDtypeStruct((total, LANES), jnp.bfloat16),
            jax.ShapeDtypeStruct((COLS, total), jnp.bfloat16),
        ),
        in_specs=[SMEM] + [VMEM] * (4 + len(pieces)),
        out_specs=(VMEM,) * 3,
        scratch_shapes=[pltpu.VMEM((FEAT, total), jnp.bfloat16)],
        compiler_params=params(),
        cost_estimate=cost(4),
        name="high_term",
    )(me, picks, *pieces, lo, hi, w)


def low_kernel(far, me, low, low_w, t, part):
    groups = far.shape[1] // 4
    both = 2

    def some(b, _):
        ks = []
        for j in range(both):
            leaf = b * both + j
            tl = t[block(leaf, LEAF), :]
            for g in range(groups):
                spots = [block(far[leaf, 4 * g + i] ^ me[0], RANK) for i in range(4)]
                r = jnp.concatenate([low[s, :] for s in spots], axis=0)
                ks.append((spots, jnp.exp(dot(r, tl, NT)).astype(jnp.bfloat16)))
        for j in range(both):
            total = None
            for spots, k in ks[j * groups : (j + 1) * groups]:
                p = dot(jnp.concatenate([low_w[:, s] for s in spots], axis=1), k)
                total = p if total is None else total + p
            part[b * both + j] = total
        return 0

    lax.fori_loop(0, LEAF_DEV // both, some, 0)


def low_call(far, me, low, low_w, t):
    return pl.pallas_call(
        low_kernel,
        out_shape=jax.ShapeDtypeStruct((LEAF_DEV, COLS, LEAF), jnp.float32),
        in_specs=[SMEM, SMEM, VMEM, VMEM, VMEM],
        out_specs=VMEM,
        compiler_params=params(),
        cost_estimate=cost(64),
        name="far_low",
    )(far, me, low, low_w, t)


def near_kernel(scales, near, count, first, lo, hi, left, right, w_own, t, low, out, rows, w, acc, pairs, sems):
    near_scale, low_scale = scales
    side = REACH * LEAF
    own = LEAF_DEV * LEAF
    moves = [
        pltpu.make_async_copy(left, rows.at[pl.ds(0, side), :], sems.at[0]),
        pltpu.make_async_copy(right, rows.at[pl.ds(side + own, side), :], sems.at[1]),
        pltpu.make_async_copy(lo, rows.at[pl.ds(side, own // 2), :], sems.at[2]),
        pltpu.make_async_copy(hi, rows.at[pl.ds(side + own // 2, own // 2), :], sems.at[3]),
        pltpu.make_async_copy(w_own, w.at[:, pl.ds(side, own)], sems.at[4]),
    ]
    for m in moves:
        m.start()

    def leaf_slots(leaf, n):
        def slot(s, n):
            pairs[n] = leaf * 64 + (near[leaf, s] - first[0] + REACH)
            return n + 1

        return lax.fori_loop(0, count[leaf], slot, n)

    n = lax.fori_loop(0, LEAF_DEV, leaf_slots, jnp.int32(0))
    for u in range(8):
        pairs[n + u] = LEAF_DEV * 64

    acc[...] = jnp.zeros_like(acc)
    moves[0].wait()
    moves[1].wait()

    def flip(b, _):
        at = block(b, LEAF)
        there = block(b + REACH + LEAF_DEV, LEAF)
        w[:, at] = weights(rows[at, :])
        w[:, there] = weights(rows[there, :])
        return 0

    lax.fori_loop(0, REACH, flip, 0)
    for m in moves[2:]:
        m.wait()

    def step(begin, many):
        ks = []
        for u in range(many):
            e = pairs[begin + u]
            leaf, at = e // 64, e % 64
            tl = t[block(jnp.minimum(leaf, LEAF_DEV - 1), LEAF), :]
            k = jnp.exp(dot(rows[block(at, LEAF), :], tl, NT)).astype(jnp.bfloat16)
            ks.append((leaf, at, k))
        for leaf, at, k in ks:
            acc[leaf] = acc[leaf] + dot(w[:, block(at, LEAF)], k)

    def eight(s, _):
        step(s * 8, 8)
        return 0

    lax.fori_loop(0, n // 8, eight, 0)

    def four(s, _):
        step(n // 8 * 8 + s * 4, 4)
        return 0

    lax.fori_loop(0, (n % 8 + 3) // 4, four, 0)

    for leaf in range(LEAF_DEV):
        at = slice(leaf * LEAF, (leaf + 1) * LEAF)
        out[:, at] = acc[leaf] * near_scale + low[leaf] * low_scale


def near_call(scales, near, count, first, lo, hi, left, right, w, t, low):
    n = (LEAF_DEV + 2 * REACH) * LEAF
    return pl.pallas_call(
        lambda *refs: near_kernel(scales, *refs),
        out_shape=jax.ShapeDtypeStruct((COLS, LEAF_DEV * LEAF), jnp.float32),
        in_specs=[SMEM] * 3 + [ANY] * 5 + [VMEM] * 2,
        out_specs=VMEM,
        scratch_shapes=[
            pltpu.VMEM((n, LANES), jnp.bfloat16),
            pltpu.VMEM((COLS, n), jnp.bfloat16),
            pltpu.VMEM((LEAF_DEV + 1, COLS, LEAF), jnp.float32),
            pltpu.SMEM((LEAF_DEV * NEAR + 8,), jnp.int32),
            pltpu.SemaphoreType.DMA((5,)),
        ],
        compiler_params=params(LAST_LIMIT),
        cost_estimate=cost(150),
        name="near_sum",
    )(near, count, first, lo, hi, left, right, w, t, low)


def high_kernel(scale, ratio, group_count, own_group, terms, t, part, out):
    each = COLS + FEAT
    members = terms.shape[0] // each // group_count
    ws, xs = [], []
    for k in range(1, group_count):
        group = (own_group[0] + k) % group_count
        base = group * (members * each)
        total = jnp.zeros((COLS, RANK), jnp.float32)
        for m in range(members):
            at = pl.ds(pl.multiple_of(base + m * each, 16), COLS)
            total = total + terms[at, :].astype(jnp.float32)
        ws.append(total.astype(jnp.bfloat16) * jnp.bfloat16(ratio))
        xs.append(terms[pl.ds(pl.multiple_of(base + COLS, 16), FEAT), :])
    high_w = jnp.concatenate(ws, axis=1)
    high_x = event_rows(jnp.concatenate(xs, axis=1))
    many = 8

    def some(b, _):
        ats = [block(b * many + j, LEAF) for j in range(many)]
        ks = [jnp.exp(dot(high_x, t[at, :], NT)).astype(jnp.bfloat16) for at in ats]
        for at, k in zip(ats, ks):
            out[:, at] = (part[:, at] + dot(high_w, k) * scale).astype(jnp.bfloat16)
        return 0

    lax.fori_loop(0, LEAF_DEV // many, some, 0)


def high_call(scale, ratio, group_count, own_group, terms, t, part):
    return pl.pallas_call(
        lambda *refs: high_kernel(scale, ratio, group_count, *refs),
        out_shape=jax.ShapeDtypeStruct(part.shape, jnp.bfloat16),
        in_specs=[SMEM] + [VMEM] * 3,
        out_specs=VMEM,
        compiler_params=params(),
        cost_estimate=cost(12),
        name="high_out",
    )(own_group, terms, t, part)


def swap(x, axis, mask):
    count = lax.axis_size(axis)
    return lax.ppermute(x, axis, [(i, i ^ mask) for i in range(count)])


def after(x, *others):
    return lax.optimization_barrier((x, *others))[0]


def per_device(events, coeffs, tree_perm, near_list, near_count, far_list, skel_low, skel_high):
    group_devs = lax.axis_size("inner")
    group_count = lax.axis_size("outer")
    far_count = far_list.shape[1]
    ev_dev = events.shape[1]
    inner = lax.axis_index("inner").astype(jnp.int32)
    device = lax.axis_index("outer").astype(jnp.int32) * group_devs + inner
    devices = group_devs * group_count
    first = (device * LEAF_DEV).reshape(1)
    me = inner.reshape(1)
    lo, hi, w, t, own = tree_call(tree_perm, skel_low, events, coeffs)

    low = own
    for masks in LOW_ROUNDS:
        pieces = [low] + [swap(low, "inner", m) for m in masks]
        low = jnp.concatenate(pieces, axis=0) if masks is not LOW_ROUNDS[-1] else low

    both = ("outer", "inner")
    left = lax.ppermute(after(hi, low), both, [(i, i + 1) for i in range(devices - 1)])
    right = lax.ppermute(after(lo, low), both, [(i + 1, i) for i in range(devices - 1)])

    scale = 1.0 / (ev_dev * group_devs) ** 0.5
    term, low, low_w = term_call(scale, me, skel_high, pieces, lo, hi, w)
    terms = lax.all_gather(term, both, axis=0, tiled=True)
    far = low_call(far_list, me, low, low_w, t)
    near_scale = 16.0 / (LEAF * NEAR) ** 0.5
    low_scale = 128.0 / (far_count * RANK) ** 0.5
    ratio = (far_count / group_count) ** 0.5
    part = near_call(
        (near_scale, low_scale), near_list, near_count, first, lo, hi, left, right, w, t, far
    )
    group = lax.axis_index("outer").astype(jnp.int32).reshape(1)
    return high_call(low_scale, ratio, group_count, group, after(terms, part), t, part)


def solution(mesh):
    return jax.shard_map(
        per_device,
        mesh=mesh,
        in_specs=(
            P(None, ("outer", "inner")),
            P(None, ("outer", "inner")),
            P(("outer", "inner"), None),
            P(("outer", "inner"), None),
            P(("outer", "inner")),
            P(("outer", "inner"), None),
            P(("outer", "inner"), None),
            P("outer", None),
        ),
        out_specs=P(None, ("outer", "inner")),
        check_vma=False,
    )
```

profile of v0, /device:TPU:7, one launch (start us, length us, event | category | flops | bytes accessed | tf_op | source)
XLA Modules:
  0.0 142.4 jit_solution(6941783268150163391)
XLA Ops:
  6.5 1.2 copy-done
  7.8 0.9 copy-done.1
  8.7 0.8 copy-done.2
  9.5 0.7 copy-done.3
  10.1 14.1 %tree_rows.1 = (bf16[4096,128]{1,0:T(8,128)(2,1)S(1)}, bf16[4096,128]{1,0:T(8,128)(2,1)S(1)}, bf16[64,8192]{1,0:T(8,128)(2,1)S(1)}, bf16[8192,128]{1,0:T(8,128)(2,1)S(1)}, bf16[80,128]{1,0:T(8,128)(2,1)S(1)}) custom-call(s32[1,8192]{1,0:T(1,128)S(1)} %copy-done.2, s32[1,128]{1,0:T(1,128)S(1)} %copy-done.3, bf16[16,8192]{1,0:T(8,128)(2,1)S(1)} %copy-done.1, ...), custom_call_target="tpu_custom_call" | custom-call | tf_op jit(solution)/shard_map/tree_rows/pallas_call | solution.py:159
  24.2 1.4 copy-done.6
  25.6 0.7 collective-permute-start
  26.3 0.8 collective-permute-done
  27.1 1.3 collective-permute-start.1
  28.4 1.5 %collective-permute-done.1 = bf16[160,128]{1,0:T(8,128)(2,1)S(1)} collective-permute-done((bf16[160,128]{1,0:T(8,128)(2,1)S(1)}, bf16[160,128]{1,0:T(8,128)(2,1)S(1)}, u32[]{:S(2)}, u32[]{:S(2)}) %collective-permute-start.1) | collective-permute-done | bytes 40992 | tf_op jit(solution)/shard_map/ppermute | solution.py:394
  30.0 2.9 %collective-permute-start.2 = (bf16[320,128]{1,0:T(8,128)(2,1)S(1)}, bf16[320,128]{1,0:T(8,128)(2,1)S(1)}, u32[]{:S(2)}, u32[]{:S(2)}) collective-permute-start(bf16[320,128]{1,0:T(8,128)(2,1)S(1)} %pad_maximum_fusion), channel_id=1, source_target_pairs={{0,4},{1,5},{2,6},{3,7},{4,0},{5,1},{6,2},{7,3},{8,12},{9,13},{10,... | collective-permute-start | bytes 245768 | tf_op jit(solution)/shard_map/ppermute | solution.py:394
  32.9 1.9 %collective-permute-done.2 = bf16[320,128]{1,0:T(8,128)(2,1)S(1)} collective-permute-done((bf16[320,128]{1,0:T(8,128)(2,1)S(1)}, bf16[320,128]{1,0:T(8,128)(2,1)S(1)}, u32[]{:S(2)}, u32[]{:S(2)}) %collective-permute-start.2) | collective-permute-done | bytes 81952 | tf_op jit(solution)/shard_map/ppermute | solution.py:394
  34.8 1.7 %collective-permute-start.3 = (bf16[640,128]{1,0:T(8,128)(2,1)S(1)}, bf16[640,128]{1,0:T(8,128)(2,1)S(1)}, u32[]{:S(2)}, u32[]{:S(2)}) collective-permute-start(bf16[640,128]{1,0:T(8,128)(2,1)S(1)} %constant_dynamic-update-slice_fusion.refs_2_), channel_id=1, source_target_pairs={{0,8},{1,9},{2,10},{3,11},{4,12},{5,13},{6,14},{7,15},{8,0},{9,1},... | collective-permute-start | bytes 491528 | tf_op jit(solution)/shard_map/ppermute | solution.py:394
  36.5 3.3 %collective-permute-start.4 = (bf16[640,128]{1,0:T(8,128)(2,1)S(1)}, bf16[640,128]{1,0:T(8,128)(2,1)}, u32[]{:S(2)}, u32[]{:S(2)}) collective-permute-start(bf16[640,128]{1,0:T(8,128)(2,1)S(1)} %constant_dynamic-update-slice_fusion.refs_2_), channel_id=1, source_target_pairs={{0,16},{1,17},{2,18},{3,19},{4,20},{5,21},{6,22},{7,23},{8,24},{9,... | collective-permute-start | bytes 491528 | tf_op jit(solution)/shard_map/ppermute | solution.py:394
  39.8 4.9 %collective-permute-done.4.refs_4_ = bf16[640,128]{1,0:T(8,128)(2,1)} collective-permute-done((bf16[640,128]{1,0:T(8,128)(2,1)S(1)}, bf16[640,128]{1,0:T(8,128)(2,1)}, u32[]{:S(2)}, u32[]{:S(2)}) %collective-permute-start.4) | collective-permute-done | bytes 163872 | tf_op jit(solution)/shard_map/ppermute | solution.py:394
  44.7 1.4 collective-permute-done.5.refs_5_
  46.1 0.7 copy-done.4
  46.8 3.3 %high_term.1 = (bf16[80,128]{1,0:T(8,128)(2,1)}, bf16[4096,128]{1,0:T(8,128)(2,1)S(1)}, bf16[64,4096]{1,0:T(8,128)(2,1)S(1)}) custom-call(s32[1]{0:T(128)} %bitcast.1.refs_0_.me, s32[1,128]{1,0:T(1,128)S(1)} %copy-done.4, bf16[640,128]{1,0:T(8,128)(2,1)S(1)} %constant_dynamic-update-slice_fusion.refs_2_, ...), custom_call_target="tpu_custom_call" | custom-call | flops 805306368 | bytes 4194304 | tf_op jit(solution)/shard_map/high_term/pallas_call | solution.py:213
  50.0 1.0 copy-done.10
  51.0 0.8 copy-done.12
  51.8 6.1 %collective-permute-start.7 = (bf16[4096,128]{1,0:T(8,128)(2,1)S(1)}, bf16[4096,128]{1,0:T(8,128)(2,1)S(1)}, u32[]{:S(2)}, u32[]{:S(2)}) collective-permute-start(bf16[4096,128]{1,0:T(8,128)(2,1)S(1)} %get-tuple-element.22.refs_6_.refs_3_), channel_id=1, source_target_pairs={{1,0},{2,1},{3,2},{4,3},{5,4},{6,5},{7,6},{8,7},{9,8},{10,9},{11,1... | collective-permute-start | bytes 3145736 | tf_op jit(solution)/shard_map/ppermute | solution.py:420
  58.0 3.1 %collective-permute-start.6 = (bf16[4096,128]{1,0:T(8,128)(2,1)S(1)}, bf16[4096,128]{1,0:T(8,128)(2,1)S(1)}, u32[]{:S(2)}, u32[]{:S(2)}) collective-permute-start(bf16[4096,128]{1,0:T(8,128)(2,1)S(1)} %get-tuple-element.21.refs_7_.refs_4_), channel_id=1, source_target_pairs={{0,1},{1,2},{2,3},{3,4},{4,5},{5,6},{6,7},{7,8},{8,9},{9,10},{10,1... | collective-permute-start | bytes 3145736 | tf_op jit(solution)/shard_map/ppermute | solution.py:419
  61.1 1.6 %copy-done.7 = bf16[8192,128]{1,0:T(8,128)(2,1)S(1)} copy-done((bf16[8192,128]{1,0:T(8,128)(2,1)S(1)}, bf16[8192,128]{1,0:T(8,128)(2,1)}, u32[]{:S(2)}) %copy-start.7) | copy-done | bytes 2097176
  62.7 1.2 copy-done.11
  63.9 1.0 copy-done.13
  65.0 16.9 %far_low.1.refs_9_ = f32[16,64,512]{2,1,0:T(8,128)S(1)} custom-call(s32[16,16]{1,0:T(8,128)S(1)} %copy-done.14, s32[1]{0:T(128)} %bitcast.1.refs_0_.me, bf16[4096,128]{1,0:T(8,128)(2,1)S(1)} %copy-done.11, bf16[64,4096]{1,0:T(8,128)(2,1)S(1)} %copy-done.13, bf16[8192,128]{1,0:T(8,128)(2,1)S(1)} %copy-done.7), custom_call_target="tpu_custom_call" | custom-call | flops 12884901888 | bytes 4194304 | tf_op jit(solution)/shard_map/far_low/pallas_call | solution.py:254
  81.9 43.1 %near_sum.1.refs_3_ = f32[64,8192]{1,0:T(8,128)S(1)} custom-call(s32[16,32]{1,0:T(8,128)S(1)} %copy-done.15, s32[16]{0:T(128)S(1)} %copy-done.16, s32[1]{0:T(128)} %bitcast.2.refs_2_, bf16[4096,128]{1,0:T(8,128)(2,1)S(1)} %get-tuple-element.22.refs_6_.refs_3_, bf16[4096,128]{1,0:T(8,128)(2,1)S(1)} %get-tuple-element.21.refs_7_.refs_4_, ...), custom_call_target="tpu_custom_call" | custom-call | flops 30198988800 | bytes 4194304 | tf_op jit(solution)/shard_map/near_sum/pallas_call | solution.py:335
  125.0 1.4 copy-done.17
  126.4 1.7 %copy-done.5 = bf16[10240,128]{1,0:T(8,128)(2,1)S(1)} copy-done((bf16[10240,128]{1,0:T(8,128)(2,1)S(1)}, bf16[10240,128]{1,0:T(8,128)(2,1)}, u32[]{:S(2)}) %copy-start.5) | copy-done | bytes 2621464
  128.1 1.6 %copy-done.9 = bf16[8192,128]{1,0:T(8,128)(2,1)S(1)} copy-done((bf16[8192,128]{1,0:T(8,128)(2,1)S(1)}, bf16[8192,128]{1,0:T(8,128)(2,1)}, u32[]{:S(2)}) %copy-start.9) | copy-done | bytes 2097176
  129.7 1.6 %copy-done.18 = f32[64,8192]{1,0:T(8,128)S(1)} copy-done((f32[64,8192]{1,0:T(8,128)S(1)}, f32[64,8192]{1,0:T(8,128)}, u32[]{:S(2)}) %copy-start.18) | copy-done | bytes 2097176
  131.3 4.3 %high_out.1 = bf16[64,8192]{1,0:T(8,128)(2,1)} custom-call(s32[1]{0:T(128)} %bitcast.refs_0_, bf16[10240,128]{1,0:T(8,128)(2,1)S(1)} %copy-done.5, bf16[8192,128]{1,0:T(8,128)(2,1)S(1)} %copy-done.9, f32[64,8192]{1,0:T(8,128)S(1)} %copy-done.18), custom_call_target="tpu_custom_call" | custom-call | flops 2415919104 | bytes 4194304 | tf_op jit(solution)/shard_map/high_out/pallas_call | solution.py:381
  (36 shorter events, 0.1 us)
Async XLA Ops:
  6.5 119.8 %all-gather.2.cloned.1.call-start = ((), (), s32[]{:S(2)}) async-start(), calls=%async_computation | async-start | bytes 2641920 | tf_op jit(solution)/shard_map/all_gather | solution.py:424
  6.5 1.2 copy-start
  7.8 0.9 copy-start.1
  8.7 0.8 copy-start.2
  9.5 0.7 copy-start.3
  24.2 1.4 copy-start.6
  25.6 1.5 %collective-permute-start = (bf16[80,128]{1,0:T(8,128)(2,1)S(1)}, bf16[80,128]{1,0:T(8,128)(2,1)S(1)}, u32[]{:S(2)}, u32[]{:S(2)}) collective-permute-start(bf16[80,128]{1,0:T(8,128)(2,1)S(1)} %get-tuple-element.16), channel_id=1, source_target_pairs={{0,1},{1,0},{2,3},{3,2},{4,5},{5,4},{6,7},{7,6},{8,9},{9,8},{10,11... | collective-permute-start | bytes 61448 | tf_op jit(solution)/shard_map/ppermute | solution.py:394
  27.1 2.9 %collective-permute-start.1 = (bf16[160,128]{1,0:T(8,128)(2,1)S(1)}, bf16[160,128]{1,0:T(8,128)(2,1)S(1)}, u32[]{:S(2)}, u32[]{:S(2)}) collective-permute-start(bf16[160,128]{1,0:T(8,128)(2,1)S(1)} %pad_maximum_fusion.1), channel_id=1, source_target_pairs={{0,2},{1,3},{2,0},{3,1},{4,6},{5,7},{6,4},{7,5},{8,10},{9,11},{10,... | collective-permute-start | bytes 122888 | tf_op jit(solution)/shard_map/ppermute | solution.py:394
  28.4 32.7 %copy-start.14 = (s32[16,16]{1,0:T(8,128)S(1)}, s32[16,16]{1,0:T(8,128)}, u32[]{:S(2)}) copy-start(s32[16,16]{1,0:T(8,128)} %far.1) | copy-start | bytes 3076
  30.0 4.8 %collective-permute-start.2 = (bf16[320,128]{1,0:T(8,128)(2,1)S(1)}, bf16[320,128]{1,0:T(8,128)(2,1)S(1)}, u32[]{:S(2)}, u32[]{:S(2)}) collective-permute-start(bf16[320,128]{1,0:T(8,128)(2,1)S(1)} %pad_maximum_fusion), channel_id=1, source_target_pairs={{0,4},{1,5},{2,6},{3,7},{4,0},{5,1},{6,2},{7,3},{8,12},{9,13},{10,... | collective-permute-start | bytes 245768 | tf_op jit(solution)/shard_map/ppermute | solution.py:394
  34.8 5.0 %collective-permute-start.3 = (bf16[640,128]{1,0:T(8,128)(2,1)S(1)}, bf16[640,128]{1,0:T(8,128)(2,1)S(1)}, u32[]{:S(2)}, u32[]{:S(2)}) collective-permute-start(bf16[640,128]{1,0:T(8,128)(2,1)S(1)} %constant_dynamic-update-slice_fusion.refs_2_), channel_id=1, source_target_pairs={{0,8},{1,9},{2,10},{3,11},{4,12},{5,13},{6,14},{7,15},{8,0},{9,1},... | collective-permute-start | bytes 491528 | tf_op jit(solution)/shard_map/ppermute | solution.py:394
  36.5 8.2 %collective-permute-start.4 = (bf16[640,128]{1,0:T(8,128)(2,1)S(1)}, bf16[640,128]{1,0:T(8,128)(2,1)}, u32[]{:S(2)}, u32[]{:S(2)}) collective-permute-start(bf16[640,128]{1,0:T(8,128)(2,1)S(1)} %constant_dynamic-update-slice_fusion.refs_2_), channel_id=1, source_target_pairs={{0,16},{1,17},{2,18},{3,19},{4,20},{5,21},{6,22},{7,23},{8,24},{9,... | collective-permute-start | bytes 491528 | tf_op jit(solution)/shard_map/ppermute | solution.py:394
  39.8 6.3 %collective-permute-start.5 = (bf16[640,128]{1,0:T(8,128)(2,1)S(1)}, bf16[640,128]{1,0:T(8,128)(2,1)}, u32[]{:S(2)}, u32[]{:S(2)}) collective-permute-start(bf16[640,128]{1,0:T(8,128)(2,1)S(1)} %constant_dynamic-update-slice_fusion.refs_2_), channel_id=1, source_target_pairs={{0,24},{1,25},{2,26},{3,27},{4,28},{5,29},{6,30},{7,31},{8,16},{9,... | collective-permute-start | bytes 491528 | tf_op jit(solution)/shard_map/ppermute | solution.py:394
  46.1 0.7 copy-start.4
  50.0 1.0 copy-start.10
  51.0 0.8 copy-start.12
  51.8 30.0 %collective-permute-start.7 = (bf16[4096,128]{1,0:T(8,128)(2,1)S(1)}, bf16[4096,128]{1,0:T(8,128)(2,1)S(1)}, u32[]{:S(2)}, u32[]{:S(2)}) collective-permute-start(bf16[4096,128]{1,0:T(8,128)(2,1)S(1)} %get-tuple-element.22.refs_6_.refs_3_), channel_id=1, source_target_pairs={{1,0},{2,1},{3,2},{4,3},{5,4},{6,5},{7,6},{8,7},{9,8},{10,9},{11,1... | collective-permute-start | bytes 3145736 | tf_op jit(solution)/shard_map/ppermute | solution.py:420
  58.0 23.9 %collective-permute-start.6 = (bf16[4096,128]{1,0:T(8,128)(2,1)S(1)}, bf16[4096,128]{1,0:T(8,128)(2,1)S(1)}, u32[]{:S(2)}, u32[]{:S(2)}) collective-permute-start(bf16[4096,128]{1,0:T(8,128)(2,1)S(1)} %get-tuple-element.21.refs_7_.refs_4_), channel_id=1, source_target_pairs={{0,1},{1,2},{2,3},{3,4},{4,5},{5,6},{6,7},{7,8},{8,9},{9,10},{10,1... | collective-permute-start | bytes 3145736 | tf_op jit(solution)/shard_map/ppermute | solution.py:419
  61.1 1.6 %copy-start.7 = (bf16[8192,128]{1,0:T(8,128)(2,1)S(1)}, bf16[8192,128]{1,0:T(8,128)(2,1)}, u32[]{:S(2)}) copy-start(bf16[8192,128]{1,0:T(8,128)(2,1)} %copy-done.6) | copy-start | bytes 6291460
  62.7 1.2 copy-start.11
  63.9 1.0 copy-start.13
  65.0 16.9 %copy-start.8 = (bf16[8192,128]{1,0:T(8,128)(2,1)S(1)}, bf16[8192,128]{1,0:T(8,128)(2,1)}, u32[]{:S(2)}) copy-start(bf16[8192,128]{1,0:T(8,128)(2,1)} %copy-done.6) | copy-start | bytes 6291460
  65.0 16.9 %copy-start.15 = (s32[16,32]{1,0:T(8,128)S(1)}, s32[16,32]{1,0:T(8,128)}, u32[]{:S(2)}) copy-start(s32[16,32]{1,0:T(8,128)} %refs_0_.1) | copy-start | bytes 6148
  65.0 16.9 %copy-start.16 = (s32[16]{0:T(128)S(1)}, s32[16]{0:T(128)}, u32[]{:S(2)}) copy-start(s32[16]{0:T(128)} %refs_1_.3) | copy-start | bytes 196
  125.0 1.4 copy-start.17
  126.4 1.7 %copy-start.5 = (bf16[10240,128]{1,0:T(8,128)(2,1)S(1)}, bf16[10240,128]{1,0:T(8,128)(2,1)}, u32[]{:S(2)}) copy-start(bf16[10240,128]{1,0:T(8,128)(2,1)} %all-gather.2.cloned.1.call-done.refs_1_) | copy-start | bytes 7864324
  128.1 1.6 %copy-start.9 = (bf16[8192,128]{1,0:T(8,128)(2,1)S(1)}, bf16[8192,128]{1,0:T(8,128)(2,1)}, u32[]{:S(2)}) copy-start(bf16[8192,128]{1,0:T(8,128)(2,1)} %copy-done.6) | copy-start | bytes 6291460
  129.7 1.6 %copy-start.18 = (f32[64,8192]{1,0:T(8,128)S(1)}, f32[64,8192]{1,0:T(8,128)}, u32[]{:S(2)}) copy-start(f32[64,8192]{1,0:T(8,128)} %copy-done.17) | copy-start | bytes 6291460
Sparse Core Ops, SparseCore 0:
  52.0 66.8 all-gather.1
where the time goes:
time: 143 us; the launch traced here: 142 us
  Pallas kernels  81.6 us (57%)
  starting transfers between devices  19.1 us (13%)
  local copies, waits for them, and re-layouts  17.6 us (12%)
  between operations  13.5 us (9%)
  waiting for transfers between devices  10.6 us (7%)
    pallas_call x1, Pallas kernels, near_call(): pl.pallas_call(lambda *refs: near_kernel(scales, *refs), out_shape=jax.Sh...  43.1 us
    unnamed x41, local copies, waits for them, and re-layouts  17.5 us
    pallas_call x1, Pallas kernels, low_call(): pl.pallas_call(low_kernel, out_shape=jax.ShapeDtypeStruct((LEAF_DEV, COLS...  16.9 us
    pallas_call x1, Pallas kernels, tree_call(): pl.pallas_call(tree_kernel, out_shape=(jax.ShapeDtypeStruct((n // 2, LANE...  14.1 us
    ppermute x6, waiting for transfers between devices, swap(): return lax.ppermute(x, axis, [(i, i ^ mask) for i in range(count)])  10.6 us
    ppermute x6, starting transfers between devices, swap(): return lax.ppermute(x, axis, [(i, i ^ mask) for i in range(count)])  9.91 us
    ppermute x1, starting transfers between devices, per_device(): lax.ppermute(after(lo, low), both, [(i + 1, i) for i in range(devices - 1)])  6.12 us
    pallas_call x1, Pallas kernels, high_call(): pl.pallas_call(lambda *refs: high_kernel(scale, ratio, group_count, *refs...  4.28 us
  transfers between devices with their start and end apart: 9, of which 5 were waited for; matrix products, arithmetic and copies ran while one was open for 0% of the time, Pallas kernels for 42%

commit v1 on v0

--- a/solution.py
+++ b/solution.py
@@ -16,10 +16,10 @@
 LANES = 128
 REACH = 8
 LOW_ROUNDS = ((1,), (2,), (4,), (8, 16, 24))
+SELF_SPANS = ((0, 2), (2, 2), (4, 4), (8, 8))
 NT = (((1,), (1,)), ((), ()))
 NN = (((1,), (0,)), ((), ()))
-VMEM_LIMIT = 24 << 20
-LAST_LIMIT = 32 << 20
+VMEM_LIMIT = 60 << 20
 
 X0 = COLS
 N0 = X0 + FEAT
@@ -77,8 +77,8 @@
 
 
 def tree_kernel(
-    perm_hbm, skel_hbm, events_hbm, coeffs_hbm, lo_out, hi_out, w_out, t_out, own_out,
-    table, picked, spick, perm, skel, events, coeffs, sems,
+    perm_hbm, skel_hbm, events_hbm, coeffs_hbm, lo_hbm, hi_hbm, w_hbm, t_hbm, own_out,
+    lo_out, hi_out, w_out, t_out, table, picked, spick, perm, skel, events, coeffs, sems,
 ):
     moves = [
         pltpu.make_async_copy(src, dst, sems.at[i])
@@ -88,8 +88,8 @@
     ]
     for m in moves:
         m.start()
-    for m in moves:
-        m.wait()
+    moves[0].wait()
+    moves[1].wait()
     chunks = events.shape[1] // LEAF
 
     def build(c, _):
@@ -99,6 +99,8 @@
         return 0
 
     lax.fori_loop(0, chunks, build, 0)
+    moves[2].wait()
+    moves[3].wait()
 
     def fetch(ids):
         return jnp.concatenate([table[pl.ds(i, 1), :] for i in ids], axis=0)
@@ -128,13 +130,24 @@
 
     half = chunks // 2
     lax.fori_loop(0, half, functools.partial(gather, lo_out, 0), 0)
+    outs = [
+        pltpu.make_async_copy(src, dst, sems.at[4 + i])
+        for i, (src, dst) in enumerate(
+            [(lo_out, lo_hbm), (hi_out, hi_hbm), (w_out, w_hbm), (t_out, t_hbm)]
+        )
+    ]
+    outs[0].start()
     lax.fori_loop(0, half, functools.partial(gather, hi_out, half), 0)
+    for m in outs[1:]:
+        m.start()
 
     s = spick[...]
     ts = targets(s.astype(jnp.bfloat16))
     su = halves_dot(lo_out, hi_out, w_out, ts) / events.shape[1] ** 0.5
     own_out[:COLS, :] = su.astype(jnp.bfloat16)
     own_out[COLS:, :] = s.T[X0:N0].astype(jnp.bfloat16)
+    for m in outs:
+        m.wait()
 
 
 def halves_dot(lo, hi, w, ts):
@@ -147,7 +160,6 @@
 SMEM = pl.BlockSpec(memory_space=pltpu.SMEM)
 VMEM = pl.BlockSpec(memory_space=pltpu.VMEM)
 ANY = pl.BlockSpec(memory_space=pl.ANY)
-HBM = pl.BlockSpec(memory_space=pltpu.HBM)
 
 
 def params(limit=VMEM_LIMIT):
@@ -165,9 +177,13 @@
             jax.ShapeDtypeStruct((n, LANES), jnp.bfloat16),
             jax.ShapeDtypeStruct((COLS + FEAT, RANK), jnp.bfloat16),
         ),
-        in_specs=[HBM] * 4,
-        out_specs=(VMEM,) * 5,
+        in_specs=[ANY] * 4,
+        out_specs=(ANY,) * 4 + (VMEM,),
         scratch_shapes=[
+            pltpu.VMEM((n // 2, LANES), jnp.bfloat16),
+            pltpu.VMEM((n // 2, LANES), jnp.bfloat16),
+            pltpu.VMEM((COLS, n), jnp.bfloat16),
+            pltpu.VMEM((n, LANES), jnp.bfloat16),
             pltpu.VMEM((n, LANES), jnp.float32),
             pltpu.VMEM((LEAF, LANES), jnp.float32),
             pltpu.VMEM((RANK, LANES), jnp.float32),
@@ -175,20 +191,55 @@
             pltpu.SMEM(skel.shape, jnp.int32),
             pltpu.VMEM(events.shape, jnp.bfloat16),
             pltpu.VMEM(coeffs.shape, jnp.bfloat16),
-            pltpu.SemaphoreType.DMA((4,)),
+            pltpu.SemaphoreType.DMA((8,)),
         ],
         compiler_params=params(),
         name="tree_rows",
     )(perm, skel, events, coeffs)
 
 
+def self_kernel(leaves, rows, w, t, part):
+    for leaf in range(leaves):
+        at = slice(leaf * LEAF, (leaf + 1) * LEAF)
+        k = jnp.exp(dot(rows[at, :], t[at, :], NT)).astype(jnp.bfloat16)
+        part[leaf] = dot(w[:, at], k)
+
+
+def self_call(lo, hi, w, t, first, leaves):
+    spot = first // leaves
+    halves = LEAF_DEV // 2 // leaves
+    rows, row_spot = (lo, spot) if spot < halves else (hi, spot - halves)
+    size = leaves * LEAF
+    return pl.pallas_call(
+        lambda *refs: self_kernel(leaves, *refs),
+        out_shape=jax.ShapeDtypeStruct((leaves, COLS, LEAF), jnp.float32),
+        grid=(1,),
+        in_specs=[
+            pl.BlockSpec((size, LANES), lambda i: (row_spot, 0)),
+            pl.BlockSpec((COLS, size), lambda i: (0, spot)),
+            pl.BlockSpec((size, LANES), lambda i: (spot, 0)),
+        ],
+        out_specs=pl.BlockSpec((leaves, COLS, LEAF), lambda i: (0, 0, 0)),
+        compiler_params=params(),
+        cost_estimate=cost(leaves),
+        name="near_self",
+    )(rows, w, t)
+
+
 def event_rows(xb):
     none = jnp.zeros((COLS, xb.shape[1]), jnp.bfloat16)
     return jnp.concatenate([none] + features(xb), axis=0).T
 
 
 def term_kernel(scale, parts, me, picks, *refs):
-    pieces, (lo, hi, w, term_out, low_out, low_w, low_x) = refs[:parts], refs[parts:]
+    pieces, refs = refs[:parts], refs[parts:]
+    sources, (term_out, low_out, low_w, low_x, lo, hi, w, sems) = refs[:3], refs[3:]
+    moves = [
+        pltpu.make_async_copy(src, dst, sems.at[i])
+        for i, (src, dst) in enumerate(zip(sources, (lo, hi, w)))
+    ]
+    for m in moves:
+        m.start()
     each = COLS + FEAT
     blocks = pieces[0].shape[0] // each
     size = blocks * RANK
@@ -204,6 +255,8 @@
     hit = lax.broadcasted_iota(jnp.int32, (parts * size, RANK), 0) == p
     hx = dot(low_x[...], jnp.where(hit, 1.0, 0.0).astype(jnp.bfloat16)).astype(jnp.bfloat16)
     term_out[COLS:, :] = hx
+    for m in moves:
+        m.wait()
     term = halves_dot(lo, hi, w, targets(event_rows(hx))) * scale
     term_out[:COLS, :] = term.astype(jnp.bfloat16)
 
@@ -217,9 +270,15 @@
             jax.ShapeDtypeStruct((total, LANES), jnp.bfloat16),
             jax.ShapeDtypeStruct((COLS, total), jnp.bfloat16),
         ),
-        in_specs=[SMEM] + [VMEM] * (4 + len(pieces)),
+        in_specs=[SMEM] + [VMEM] * (1 + len(pieces)) + [ANY] * 3,
         out_specs=(VMEM,) * 3,
-        scratch_shapes=[pltpu.VMEM((FEAT, total), jnp.bfloat16)],
+        scratch_shapes=[
+            pltpu.VMEM((FEAT, total), jnp.bfloat16),
+            pltpu.VMEM(lo.shape, jnp.bfloat16),
+            pltpu.VMEM(hi.shape, jnp.bfloat16),
+            pltpu.VMEM(w.shape, jnp.bfloat16),
+            pltpu.SemaphoreType.DMA((3,)),
+        ],
         compiler_params=params(),
         cost_estimate=cost(4),
         name="high_term",
@@ -228,42 +287,46 @@
 
 def low_kernel(far, me, low, low_w, t, part):
     groups = far.shape[1] // 4
-    both = 2
-
-    def some(b, _):
-        ks = []
-        for j in range(both):
-            leaf = b * both + j
-            tl = t[block(leaf, LEAF), :]
-            for g in range(groups):
-                spots = [block(far[leaf, 4 * g + i] ^ me[0], RANK) for i in range(4)]
-                r = jnp.concatenate([low[s, :] for s in spots], axis=0)
-                ks.append((spots, jnp.exp(dot(r, tl, NT)).astype(jnp.bfloat16)))
-        for j in range(both):
-            total = None
-            for spots, k in ks[j * groups : (j + 1) * groups]:
-                p = dot(jnp.concatenate([low_w[:, s] for s in spots], axis=1), k)
-                total = p if total is None else total + p
-            part[b * both + j] = total
-        return 0
-
-    lax.fori_loop(0, LEAF_DEV // both, some, 0)
+    leaves = part.shape[0]
+    ks = []
+    for j in range(leaves):
+        leaf = pl.program_id(0) * leaves + j
+        tl = t[j * LEAF : (j + 1) * LEAF, :]
+        for g in range(groups):
+            spots = [block(far[leaf, 4 * g + i] ^ me[0], RANK) for i in range(4)]
+            r = jnp.concatenate([low[s, :] for s in spots], axis=0)
+            ks.append((spots, jnp.exp(dot(r, tl, NT)).astype(jnp.bfloat16)))
+    for j in range(leaves):
+        total = None
+        for spots, k in ks[j * groups : (j + 1) * groups]:
+            p = dot(jnp.concatenate([low_w[:, s] for s in spots], axis=1), k)
+            total = p if total is None else total + p
+        part[j] = total
 
 
 def low_call(far, me, low, low_w, t):
+    leaves = 2
     return pl.pallas_call(
         low_kernel,
         out_shape=jax.ShapeDtypeStruct((LEAF_DEV, COLS, LEAF), jnp.float32),
-        in_specs=[SMEM, SMEM, VMEM, VMEM, VMEM],
-        out_specs=VMEM,
+        grid=(LEAF_DEV // leaves,),
+        in_specs=[
+            SMEM,
+            SMEM,
+            pl.BlockSpec(low.shape, lambda i: (0, 0)),
+            pl.BlockSpec(low_w.shape, lambda i: (0, 0)),
+            pl.BlockSpec((leaves * LEAF, LANES), lambda i: (i, 0)),
+        ],
+        out_specs=pl.BlockSpec((leaves, COLS, LEAF), lambda i: (i, 0, 0)),
         compiler_params=params(),
         cost_estimate=cost(64),
         name="far_low",
     )(far, me, low, low_w, t)
 
 
-def near_kernel(scales, near, count, first, lo, hi, left, right, w_own, t, low, out, rows, w, acc, pairs, sems):
+def near_kernel(scales, near, count, first, lo, hi, left, right, w_own, t_hbm, low_hbm, *refs):
     near_scale, low_scale = scales
+    selfs, (out, rows, w, t, low, acc, pairs, sems) = refs[:-8], refs[-8:]
     side = REACH * LEAF
     own = LEAF_DEV * LEAF
     moves = [
@@ -272,22 +335,30 @@
         pltpu.make_async_copy(lo, rows.at[pl.ds(side, own // 2), :], sems.at[2]),
         pltpu.make_async_copy(hi, rows.at[pl.ds(side + own // 2, own // 2), :], sems.at[3]),
         pltpu.make_async_copy(w_own, w.at[:, pl.ds(side, own)], sems.at[4]),
+        pltpu.make_async_copy(t_hbm, t, sems.at[5]),
     ]
+    leaf = 0
+    for part in selfs:
+        there = acc.at[pl.ds(leaf, part.shape[0])]
+        moves.append(pltpu.make_async_copy(part, there, sems.at[len(moves)]))
+        leaf += part.shape[0]
+    low_move = pltpu.make_async_copy(low_hbm, low, sems.at[len(moves)])
     for m in moves:
         m.start()
+    low_move.start()
 
     def leaf_slots(leaf, n):
         def slot(s, n):
             pairs[n] = leaf * 64 + (near[leaf, s] - first[0] + REACH)
             return n + 1
 
-        return lax.fori_loop(0, count[leaf], slot, n)
+        return lax.fori_loop(1, count[leaf], slot, n)
 
     n = lax.fori_loop(0, LEAF_DEV, leaf_slots, jnp.int32(0))
     for u in range(8):
         pairs[n + u] = LEAF_DEV * 64
 
-    acc[...] = jnp.zeros_like(acc)
+    acc[LEAF_DEV] = jnp.zeros((COLS, LEAF), jnp.float32)
     moves[0].wait()
     moves[1].wait()
 
@@ -325,64 +396,77 @@
 
     lax.fori_loop(0, (n % 8 + 3) // 4, four, 0)
 
+    low_move.wait()
     for leaf in range(LEAF_DEV):
         at = slice(leaf * LEAF, (leaf + 1) * LEAF)
         out[:, at] = acc[leaf] * near_scale + low[leaf] * low_scale
 
 
-def near_call(scales, near, count, first, lo, hi, left, right, w, t, low):
+def near_call(scales, near, count, first, lo, hi, left, right, w, t, low, selfs):
     n = (LEAF_DEV + 2 * REACH) * LEAF
     return pl.pallas_call(
         lambda *refs: near_kernel(scales, *refs),
         out_shape=jax.ShapeDtypeStruct((COLS, LEAF_DEV * LEAF), jnp.float32),
-        in_specs=[SMEM] * 3 + [ANY] * 5 + [VMEM] * 2,
+        in_specs=[SMEM] * 3 + [ANY] * (7 + len(selfs)),
         out_specs=VMEM,
         scratch_shapes=[
             pltpu.VMEM((n, LANES), jnp.bfloat16),
             pltpu.VMEM((COLS, n), jnp.bfloat16),
+            pltpu.VMEM(t.shape, jnp.bfloat16),
+            pltpu.VMEM(low.shape, jnp.float32),
             pltpu.VMEM((LEAF_DEV + 1, COLS, LEAF), jnp.float32),
             pltpu.SMEM((LEAF_DEV * NEAR + 8,), jnp.int32),
-            pltpu.SemaphoreType.DMA((5,)),
-        ],
-        compiler_params=params(LAST_LIMIT),
+            pltpu.SemaphoreType.DMA((7 + len(selfs),)),
+        ],
+        compiler_params=params(),
         cost_estimate=cost(150),
         name="near_sum",
-    )(near, count, first, lo, hi, left, right, w, t, low)
-
-
-def high_kernel(scale, ratio, group_count, own_group, terms, t, part, out):
-    each = COLS + FEAT
-    members = terms.shape[0] // each // group_count
-    ws, xs = [], []
-    for k in range(1, group_count):
-        group = (own_group[0] + k) % group_count
-        base = group * (members * each)
-        total = jnp.zeros((COLS, RANK), jnp.float32)
-        for m in range(members):
-            at = pl.ds(pl.multiple_of(base + m * each, 16), COLS)
-            total = total + terms[at, :].astype(jnp.float32)
-        ws.append(total.astype(jnp.bfloat16) * jnp.bfloat16(ratio))
-        xs.append(terms[pl.ds(pl.multiple_of(base + COLS, 16), FEAT), :])
-    high_w = jnp.concatenate(ws, axis=1)
-    high_x = event_rows(jnp.concatenate(xs, axis=1))
-    many = 8
-
-    def some(b, _):
-        ats = [block(b * many + j, LEAF) for j in range(many)]
-        ks = [jnp.exp(dot(high_x, t[at, :], NT)).astype(jnp.bfloat16) for at in ats]
-        for at, k in zip(ats, ks):
-            out[:, at] = (part[:, at] + dot(high_w, k) * scale).astype(jnp.bfloat16)
-        return 0
-
-    lax.fori_loop(0, LEAF_DEV // many, some, 0)
+    )(near, count, first, lo, hi, left, right, w, t, low, *selfs)
+
+
+def high_kernel(scale, ratio, group_count, own_group, terms, t, part, out, high_w, high_x):
+    @pl.when(pl.program_id(0) == 0)
+    def _():
+        each = COLS + FEAT
+        members = terms.shape[0] // each // group_count
+        xs = []
+        for k in range(1, group_count):
+            group = (own_group[0] + k) % group_count
+            base = group * (members * each)
+            total = jnp.zeros((COLS, RANK), jnp.float32)
+            for m in range(members):
+                at = pl.ds(pl.multiple_of(base + m * each, 16), COLS)
+                total = total + terms[at, :].astype(jnp.float32)
+            spot = slice((k - 1) * RANK, k * RANK)
+            high_w[:, spot] = total.astype(jnp.bfloat16) * jnp.bfloat16(ratio)
+            xs.append(terms[pl.ds(pl.multiple_of(base + COLS, 16), FEAT), :])
+        high_x[...] = event_rows(jnp.concatenate(xs, axis=1))
+
+    many = out.shape[1] // LEAF
+    ats = [slice(j * LEAF, (j + 1) * LEAF) for j in range(many)]
+    ks = [jnp.exp(dot(high_x[...], t[at, :], NT)).astype(jnp.bfloat16) for at in ats]
+    for at, k in zip(ats, ks):
+        out[:, at] = (part[:, at] + dot(high_w[...], k) * scale).astype(jnp.bfloat16)
 
 
 def high_call(scale, ratio, group_count, own_group, terms, t, part):
+    many = 4
+    total = (group_count - 1) * RANK
     return pl.pallas_call(
         lambda *refs: high_kernel(scale, ratio, group_count, *refs),
         out_shape=jax.ShapeDtypeStruct(part.shape, jnp.bfloat16),
-        in_specs=[SMEM] + [VMEM] * 3,
-        out_specs=VMEM,
+        grid=(LEAF_DEV // many,),
+        in_specs=[
+            SMEM,
+            pl.BlockSpec(terms.shape, lambda i: (0, 0)),
+            pl.BlockSpec((many * LEAF, LANES), lambda i: (i, 0)),
+            pl.BlockSpec((COLS, many * LEAF), lambda i: (0, i)),
+        ],
+        out_specs=pl.BlockSpec((COLS, many * LEAF), lambda i: (0, i)),
+        scratch_shapes=[
+            pltpu.VMEM((COLS, total), jnp.bfloat16),
+            pltpu.VMEM((total, LANES), jnp.bfloat16),
+        ],
         compiler_params=params(),
         cost_estimate=cost(12),
         name="high_out",
@@ -411,9 +495,14 @@
     lo, hi, w, t, own = tree_call(tree_perm, skel_low, events, coeffs)
 
     low = own
-    for masks in LOW_ROUNDS:
+    selfs = []
+    pieces = None
+    for masks, span in zip(LOW_ROUNDS, SELF_SPANS):
+        if pieces is not None:
+            low = after(jnp.concatenate(pieces, axis=0), selfs[-1])
         pieces = [low] + [swap(low, "inner", m) for m in masks]
-        low = jnp.concatenate(pieces, axis=0) if masks is not LOW_ROUNDS[-1] else low
+        selfs.append(self_call(after(lo, low), after(hi, low), w, t, *span))
+    pieces = [after(p, selfs[-1]) for p in pieces]
 
     both = ("outer", "inner")
     left = lax.ppermute(after(hi, low), both, [(i, i + 1) for i in range(devices - 1)])
@@ -427,7 +516,7 @@
     low_scale = 128.0 / (far_count * RANK) ** 0.5
     ratio = (far_count / group_count) ** 0.5
     part = near_call(
-        (near_scale, low_scale), near_list, near_count, first, lo, hi, left, right, w, t, far
+        (near_scale, low_scale), near_list, near_count, first, lo, hi, left, right, w, t, far, selfs
     )
     group = lax.axis_index("outer").astype(jnp.int32).reshape(1)
     return high_call(low_scale, ratio, group_count, group, after(terms, part), t, part)

time: 143 us -> 137 us (0.958)
  the two profiles are of different devices: /device:TPU:7 before, /device:TPU:1 now
where the time goes in v1:
time: 137 us; the launch traced here: 135 us
  Pallas kernels  87.1 us (64%)
  waiting for transfers between devices  16.5 us (12%)
  starting transfers between devices  15.8 us (12%)
  between operations  13.5 us (10%)
  local copies, waits for them, and re-layouts  1.67 us (1%)
    pallas_call x1, Pallas kernels, near_call(): pl.pallas_call(lambda *refs: near_kernel(scales, *refs), out_shape=jax.Sh...  26.9 us
    pallas_call x1, Pallas kernels, low_call(): pl.pallas_call(low_kernel, out_shape=jax.ShapeDtypeStruct((LEAF_DEV, COLS...  18.7 us
    pallas_call x1, Pallas kernels, tree_call(): pl.pallas_call(tree_kernel, out_shape=(jax.ShapeDtypeStruct((n // 2, LANE...  15.5 us
    all_gather x1, waiting for transfers between devices, per_device(): terms = lax.all_gather(term, both, axis=0, tiled=True)  14.6 us
    pallas_call x4, Pallas kernels, self_call(): pl.pallas_call(lambda *refs: self_kernel(leaves, *refs), out_shape=jax.Sh...  14.1 us
    ppermute x6, starting transfers between devices, swap(): return lax.ppermute(x, axis, [(i, i ^ mask) for i in range(count)])  10.2 us
    pallas_call x1, Pallas kernels, high_call(): pl.pallas_call(lambda *refs: high_kernel(scale, ratio, group_count, *refs...  6.93 us
    pallas_call x1, Pallas kernels, term_call(): pl.pallas_call(lambda *refs: term_kernel(scale, len(pieces), *refs), out_...  4.93 us
  transfers between devices with their start and end apart: 9, of which 3 were waited for; matrix products, arithmetic and copies ran while one was open for 0% of the time, Pallas kernels for 44%

profile of v1, /device:TPU:1, one launch (start us, length us, event | category | flops | bytes accessed | tf_op | source)
XLA Modules:
  0.0 134.6 jit_solution(5639142497706243025)
XLA Ops:
  6.5 15.5 %tree_rows.1 = (bf16[4096,128]{1,0:T(8,128)(2,1)}, bf16[4096,128]{1,0:T(8,128)(2,1)}, bf16[64,8192]{1,0:T(8,128)(2,1)}, bf16[8192,128]{1,0:T(8,128)(2,1)}, bf16[80,128]{1,0:T(8,128)(2,1)}) custom-call(s32[1,8192]{1,0:T(1,128)} %perm_hbm.1, s32[1,128]{1,0:T(1,128)} %skel_hbm.1, bf16[16,8192]{1,0:T(8,128)(2,1)} %events_hbm.1, bf16[64,8192]{1,0:T(8,128)(2,1)} %coeffs_hbm.1), custom_call_target="tpu_custom_call" | custom-call | tf_op jit(solution)/shard_map/tree_rows/pallas_call | solution.py:171
  22.0 1.5 %collective-permute-start = (bf16[80,128]{1,0:T(8,128)(2,1)}, bf16[80,128]{1,0:T(8,128)(2,1)S(1)}, u32[]{:S(2)}, u32[]{:S(2)}) collective-permute-start(bf16[80,128]{1,0:T(8,128)(2,1)} %get-tuple-element.26), channel_id=1, source_target_pairs={{0,1},{1,0},{2,3},{3,2},{4,5},{5,4},{6,7},{7,6},{8,9},{9,8},{10,11... | collective-permute-start | bytes 61448 | tf_op jit(solution)/shard_map/ppermute | solution.py:478
  23.5 2.6 %near_self.4.refs_10_ = f32[2,64,512]{2,1,0:T(8,128)} custom-call(bf16[4096,128]{1,0:T(8,128)(2,1)} %get-tuple-element.43.refs_0_.refs_6_.refs_3_, bf16[64,8192]{1,0:T(8,128)(2,1)} %get-tuple-element.29.refs_1_.refs_8_.refs_7_, bf16[8192,128]{1,0:T(8,128)(2,1)} %get-tuple-element.30.refs_2_.t.refs_8_), custom_call_target="tpu_custom_call" | custom-call | flops 402653184 | bytes 4194304 | tf_op jit(solution)/shard_map/near_self/pallas_call | solution.py:213
  26.1 0.0 collective-permute-done
  26.2 1.5 %collective-permute-start.1 = (bf16[160,128]{1,0:T(8,128)(2,1)S(1)}, bf16[160,128]{1,0:T(8,128)(2,1)S(1)}, u32[]{:S(2)}, u32[]{:S(2)}) collective-permute-start(bf16[160,128]{1,0:T(8,128)(2,1)S(1)} %pad_maximum_fusion.2), channel_id=1, source_target_pairs={{0,2},{1,3},{2,0},{3,1},{4,6},{5,7},{6,4},{7,5},{8,10},{9,11},{10,... | collective-permute-start | bytes 122888 | tf_op jit(solution)/shard_map/ppermute | solution.py:478
  27.6 2.6 %near_self.5.refs_11_ = f32[2,64,512]{2,1,0:T(8,128)} custom-call(bf16[4096,128]{1,0:T(8,128)(2,1)} %get-tuple-element.43.refs_0_.refs_6_.refs_3_, bf16[64,8192]{1,0:T(8,128)(2,1)} %get-tuple-element.29.refs_1_.refs_8_.refs_7_, bf16[8192,128]{1,0:T(8,128)(2,1)} %get-tuple-element.30.refs_2_.t.refs_8_), custom_call_target="tpu_custom_call" | custom-call | flops 402653184 | bytes 4194304 | tf_op jit(solution)/shard_map/near_self/pallas_call | solution.py:213
  30.2 0.0 collective-permute-done.1
  30.2 2.7 %collective-permute-start.2 = (bf16[320,128]{1,0:T(8,128)(2,1)S(1)}, bf16[320,128]{1,0:T(8,128)(2,1)S(1)}, u32[]{:S(2)}, u32[]{:S(2)}) collective-permute-start(bf16[320,128]{1,0:T(8,128)(2,1)S(1)} %pad_maximum_fusion.1), channel_id=1, source_target_pairs={{0,4},{1,5},{2,6},{3,7},{4,0},{5,1},{6,2},{7,3},{8,12},{9,13},{10,... | collective-permute-start | bytes 245768 | tf_op jit(solution)/shard_map/ppermute | solution.py:478
  32.9 3.5 %near_self.6.refs_12_ = f32[4,64,512]{2,1,0:T(8,128)} custom-call(bf16[4096,128]{1,0:T(8,128)(2,1)} %get-tuple-element.43.refs_0_.refs_6_.refs_3_, bf16[64,8192]{1,0:T(8,128)(2,1)} %get-tuple-element.29.refs_1_.refs_8_.refs_7_, bf16[8192,128]{1,0:T(8,128)(2,1)} %get-tuple-element.30.refs_2_.t.refs_8_), custom_call_target="tpu_custom_call" | custom-call | flops 805306368 | bytes 4194304 | tf_op jit(solution)/shard_map/near_self/pallas_call | solution.py:213
  36.4 0.0 collective-permute-done.2
  36.5 0.0 copy-start.2
  36.5 3.8 %collective-permute-start.5 = (bf16[640,128]{1,0:T(8,128)(2,1)S(1)}, bf16[640,128]{1,0:T(8,128)(2,1)S(1)}, u32[]{:S(2)}, u32[]{:S(2)}) collective-permute-start(bf16[640,128]{1,0:T(8,128)(2,1)S(1)} %pad_maximum_fusion.refs_2_), channel_id=1, source_target_pairs={{0,24},{1,25},{2,26},{3,27},{4,28},{5,29},{6,30},{7,31},{8,16},{9,... | collective-permute-start | bytes 491528 | tf_op jit(solution)/shard_map/ppermute | solution.py:478
  40.3 0.0 collective-permute-start.4
  40.3 0.7 collective-permute-start.3
  41.0 5.4 %near_self.7.refs_13_ = f32[8,64,512]{2,1,0:T(8,128)} custom-call(bf16[4096,128]{1,0:T(8,128)(2,1)} %get-tuple-element.37.refs_0_.refs_7_.refs_4_, bf16[64,8192]{1,0:T(8,128)(2,1)} %get-tuple-element.29.refs_1_.refs_8_.refs_7_, bf16[8192,128]{1,0:T(8,128)(2,1)} %get-tuple-element.30.refs_2_.t.refs_8_), custom_call_target="tpu_custom_call" | custom-call | flops 1610612736 | bytes 4194304 | tf_op jit(solution)/shard_map/near_self/pallas_call | solution.py:213
  46.4 0.0 copy-done.2
  46.4 1.0 collective-permute-done.5.refs_5_
  47.3 0.0 collective-permute-done.4.refs_4_
  47.3 0.8 collective-permute-done.3.refs_3_
  48.2 0.0 copy-done.3
  48.2 0.7 copy-done.5
  48.9 4.9 %high_term.1 = (bf16[80,128]{1,0:T(8,128)(2,1)}, bf16[4096,128]{1,0:T(8,128)(2,1)}, bf16[64,4096]{1,0:T(8,128)(2,1)}) custom-call(s32[1]{0:T(128)} %bitcast.1.refs_0_.me, s32[1,128]{1,0:T(1,128)} %refs_1_.2, bf16[640,128]{1,0:T(8,128)(2,1)} %copy-done.2, bf16[640,128]{1,0:T(8,128)(2,1)} %copy-done.5, bf16[640,128]{1,0:T(8,128)(2,1)} %copy-done.4, ...), custom_call_target="tpu_custom_call" | custom-call | flops 805306368 | bytes 4194304 | tf_op jit(solution)/shard_map/high_term/pallas_call | solution.py:266
  53.8 0.0 all-gather.2.cloned.1.call-update
  53.9 3.8 %collective-permute-start.6 = (bf16[4096,128]{1,0:T(8,128)(2,1)S(1)}, bf16[4096,128]{1,0:T(8,128)(2,1)S(1)}, u32[]{:S(2)}, u32[]{:S(2)}) collective-permute-start(bf16[4096,128]{1,0:T(8,128)(2,1)S(1)} %copy-done.1), channel_id=1, source_target_pairs={{0,1},{1,2},{2,3},{3,4},{4,5},{5,6},{6,7},{7,8},{8,9},{9,10},{10,1... | collective-permute-start | bytes 3145736 | tf_op jit(solution)/shard_map/ppermute | solution.py:508
  57.6 1.9 %collective-permute-start.7 = (bf16[4096,128]{1,0:T(8,128)(2,1)S(1)}, bf16[4096,128]{1,0:T(8,128)(2,1)}, u32[]{:S(2)}, u32[]{:S(2)}) collective-permute-start(bf16[4096,128]{1,0:T(8,128)(2,1)S(1)} %copy-done), channel_id=1, source_target_pairs={{1,0},{2,1},{3,2},{4,3},{5,4},{6,5},{7,6},{8,7},{9,8},{10,9},{11,1... | collective-permute-start | bytes 3145736 | tf_op jit(solution)/shard_map/ppermute | solution.py:509
  59.6 18.7 %far_low.1.refs_9_ = f32[16,64,512]{2,1,0:T(8,128)} custom-call(s32[16,16]{1,0:T(8,128)} %far.1, s32[1]{0:T(128)} %bitcast.1.refs_0_.me, bf16[4096,128]{1,0:T(8,128)(2,1)} %get-tuple-element.44.low, bf16[64,4096]{1,0:T(8,128)(2,1)} %get-tuple-element.45.low_w, bf16[8192,128]{1,0:T(8,128)(2,1)} %get-tuple-element.30.refs_2_.t.refs_8_), custom_call_target="tpu_custom_call" | custom-call | flops 12884901888 | bytes 4194304 | tf_op jit(solution)/shard_map/far_low/pallas_call | solution.py:309
  78.3 0.0 collective-permute-done.7.refs_6_
  78.3 0.0 collective-permute-done.6.refs_5_
  78.3 1.0 copy-done.7
  79.3 26.9 %near_sum.1.refs_3_ = f32[64,8192]{1,0:T(8,128)} custom-call(s32[16,32]{1,0:T(8,128)} %refs_0_.1, s32[16]{0:T(128)} %refs_1_.3, s32[1]{0:T(128)} %bitcast.2.refs_2_, bf16[4096,128]{1,0:T(8,128)(2,1)} %get-tuple-element.43.refs_0_.refs_6_.refs_3_, bf16[4096,128]{1,0:T(8,128)(2,1)} %get-tuple-element.37.refs_0_.refs_7_.refs_4_, bf16[4096,128]{1,0:T(8,128)(2,1)} %copy-done.7, ...), custom_call_target="tpu_custom_call" | custom-call | flops 30198988800 | bytes 4194304 | tf_op jit(solution)/shard_map/near_sum/pallas_call | solution.py:407
  106.2 14.6 %all-gather.2.cloned.1.call-done.refs_1_ = bf16[10240,128]{1,0:T(8,128)(2,1)} async-done(((bf16[80,128]{1,0:T(8,128)(2,1)}), bf16[10240,128]{1,0:T(8,128)(2,1)}) %all-gather.2.cloned.1.call-update) | async-done | bytes 2621456 | tf_op jit(solution)/shard_map/all_gather | solution.py:513
  120.8 6.9 %high_out.1 = bf16[64,8192]{1,0:T(8,128)(2,1)} custom-call(s32[1]{0:T(128)} %bitcast.refs_0_, bf16[10240,128]{1,0:T(8,128)(2,1)} %all-gather.2.cloned.1.call-done.refs_1_, bf16[8192,128]{1,0:T(8,128)(2,1)} %get-tuple-element.30.refs_2_.t.refs_8_, f32[64,8192]{1,0:T(8,128)} %near_sum.1.refs_3_), custom_call_target="tpu_custom_call" | custom-call | flops 2415919104 | bytes 4194304 | tf_op jit(solution)/shard_map/high_out/pallas_call | solution.py:455
  (15 shorter events, 0.0 us)
Async XLA Ops:
  6.5 114.3 %all-gather.2.cloned.1.call-start = ((), (), s32[]{:S(2)}) async-start(), calls=%async_computation | async-start | bytes 2641920 | tf_op jit(solution)/shard_map/all_gather | solution.py:513
  22.0 4.1 %collective-permute-start = (bf16[80,128]{1,0:T(8,128)(2,1)}, bf16[80,128]{1,0:T(8,128)(2,1)S(1)}, u32[]{:S(2)}, u32[]{:S(2)}) collective-permute-start(bf16[80,128]{1,0:T(8,128)(2,1)} %get-tuple-element.26), channel_id=1, source_target_pairs={{0,1},{1,0},{2,3},{3,2},{4,5},{5,4},{6,7},{7,6},{8,9},{9,8},{10,11... | collective-permute-start | bytes 61448 | tf_op jit(solution)/shard_map/ppermute | solution.py:478
  23.5 2.6 %copy-start.6 = (bf16[80,128]{1,0:T(8,128)(2,1)S(1)}, bf16[80,128]{1,0:T(8,128)(2,1)}, u32[]{:S(2)}) copy-start(bf16[80,128]{1,0:T(8,128)(2,1)} %get-tuple-element.26) | copy-start | bytes 61444
  26.2 4.1 %collective-permute-start.1 = (bf16[160,128]{1,0:T(8,128)(2,1)S(1)}, bf16[160,128]{1,0:T(8,128)(2,1)S(1)}, u32[]{:S(2)}, u32[]{:S(2)}) collective-permute-start(bf16[160,128]{1,0:T(8,128)(2,1)S(1)} %pad_maximum_fusion.2), channel_id=1, source_target_pairs={{0,2},{1,3},{2,0},{3,1},{4,6},{5,7},{6,4},{7,5},{8,10},{9,11},{10,... | collective-permute-start | bytes 122888 | tf_op jit(solution)/shard_map/ppermute | solution.py:478
  30.2 6.2 %collective-permute-start.2 = (bf16[320,128]{1,0:T(8,128)(2,1)S(1)}, bf16[320,128]{1,0:T(8,128)(2,1)S(1)}, u32[]{:S(2)}, u32[]{:S(2)}) collective-permute-start(bf16[320,128]{1,0:T(8,128)(2,1)S(1)} %pad_maximum_fusion.1), channel_id=1, source_target_pairs={{0,4},{1,5},{2,6},{3,7},{4,0},{5,1},{6,2},{7,3},{8,12},{9,13},{10,... | collective-permute-start | bytes 245768 | tf_op jit(solution)/shard_map/ppermute | solution.py:478
  36.5 9.9 %copy-start.2 = (bf16[640,128]{1,0:T(8,128)(2,1)}, bf16[640,128]{1,0:T(8,128)(2,1)S(1)}, u32[]{:S(2)}) copy-start(bf16[640,128]{1,0:T(8,128)(2,1)S(1)} %pad_maximum_fusion.refs_2_) | copy-start | bytes 491524
  36.5 10.9 %collective-permute-start.5 = (bf16[640,128]{1,0:T(8,128)(2,1)S(1)}, bf16[640,128]{1,0:T(8,128)(2,1)S(1)}, u32[]{:S(2)}, u32[]{:S(2)}) collective-permute-start(bf16[640,128]{1,0:T(8,128)(2,1)S(1)} %pad_maximum_fusion.refs_2_), channel_id=1, source_target_pairs={{0,24},{1,25},{2,26},{3,27},{4,28},{5,29},{6,30},{7,31},{8,16},{9,... | collective-permute-start | bytes 491528 | tf_op jit(solution)/shard_map/ppermute | solution.py:478
  40.3 7.0 %collective-permute-start.4 = (bf16[640,128]{1,0:T(8,128)(2,1)S(1)}, bf16[640,128]{1,0:T(8,128)(2,1)S(1)}, u32[]{:S(2)}, u32[]{:S(2)}) collective-permute-start(bf16[640,128]{1,0:T(8,128)(2,1)S(1)} %pad_maximum_fusion.refs_2_), channel_id=1, source_target_pairs={{0,16},{1,17},{2,18},{3,19},{4,20},{5,21},{6,22},{7,23},{8,24},{9,... | collective-permute-start | bytes 491528 | tf_op jit(solution)/shard_map/ppermute | solution.py:478
  40.3 7.9 %collective-permute-start.3 = (bf16[640,128]{1,0:T(8,128)(2,1)S(1)}, bf16[640,128]{1,0:T(8,128)(2,1)S(1)}, u32[]{:S(2)}, u32[]{:S(2)}) collective-permute-start(bf16[640,128]{1,0:T(8,128)(2,1)S(1)} %pad_maximum_fusion.refs_2_), channel_id=1, source_target_pairs={{0,8},{1,9},{2,10},{3,11},{4,12},{5,13},{6,14},{7,15},{8,0},{9,1},... | collective-permute-start | bytes 491528 | tf_op jit(solution)/shard_map/ppermute | solution.py:478
  46.4 7.5 %copy-start.1 = (bf16[4096,128]{1,0:T(8,128)(2,1)S(1)}, bf16[4096,128]{1,0:T(8,128)(2,1)}, u32[]{:S(2)}) copy-start(bf16[4096,128]{1,0:T(8,128)(2,1)} %get-tuple-element.37.refs_0_.refs_7_.refs_4_) | copy-start | bytes 3145732
  46.4 11.3 %copy-start = (bf16[4096,128]{1,0:T(8,128)(2,1)S(1)}, bf16[4096,128]{1,0:T(8,128)(2,1)}, u32[]{:S(2)}) copy-start(bf16[4096,128]{1,0:T(8,128)(2,1)} %get-tuple-element.43.refs_0_.refs_6_.refs_3_) | copy-start | bytes 3145732
  47.3 0.9 copy-start.3
  47.3 0.9 copy-start.4
  48.2 0.7 copy-start.5
  53.9 24.4 %collective-permute-start.6 = (bf16[4096,128]{1,0:T(8,128)(2,1)S(1)}, bf16[4096,128]{1,0:T(8,128)(2,1)S(1)}, u32[]{:S(2)}, u32[]{:S(2)}) collective-permute-start(bf16[4096,128]{1,0:T(8,128)(2,1)S(1)} %copy-done.1), channel_id=1, source_target_pairs={{0,1},{1,2},{2,3},{3,4},{4,5},{5,6},{6,7},{7,8},{8,9},{9,10},{10,1... | collective-permute-start | bytes 3145736 | tf_op jit(solution)/shard_map/ppermute | solution.py:508
  57.6 20.6 %collective-permute-start.7 = (bf16[4096,128]{1,0:T(8,128)(2,1)S(1)}, bf16[4096,128]{1,0:T(8,128)(2,1)}, u32[]{:S(2)}, u32[]{:S(2)}) collective-permute-start(bf16[4096,128]{1,0:T(8,128)(2,1)S(1)} %copy-done), channel_id=1, source_target_pairs={{1,0},{2,1},{3,2},{4,3},{5,4},{6,5},{7,6},{8,7},{9,8},{10,9},{11,1... | collective-permute-start | bytes 3145736 | tf_op jit(solution)/shard_map/ppermute | solution.py:509
  78.3 1.0 copy-start.7
Sparse Core Ops, SparseCore 0:
  54.0 66.8 all-gather.1

commit v2 on v1

v2 whole, which is shorter than its diff:
```python
import functools

import jax
import jax.numpy as jnp
from jax import lax
from jax.experimental import pallas as pl
from jax.experimental.pallas import tpu as pltpu
from jax.sharding import PartitionSpec as P

LEAF = 512
RANK = 128
NEAR = 32
LEAF_DEV = 16
COLS = 64
FEAT = 16
LANES = 128
REACH = 8
NT = (((1,), (1,)), ((), ()))
NN = (((1,), (0,)), ((), ()))
VMEM_LIMIT = 60 << 20

X0 = COLS
N0 = X0 + FEAT
O0 = N0 + 3


def dot(a, b, dims=NN):
    return lax.dot_general(a, b, dims, preferred_element_type=jnp.float32)


def target_map():
    k = lax.broadcasted_iota(jnp.int32, (LANES, LANES), 0)
    m = lax.broadcasted_iota(jnp.int32, (LANES, LANES), 1)
    quarter = (k == m) & (k >= X0) & (k < N0)
    ones = (k == m + 3) & (m >= N0) & (m < O0)
    pieces = (k + 3 == m) & (k >= N0) & (k < O0)
    return jnp.where(quarter, 0.25, jnp.where(ones | pieces, 1.0, 0.0)).astype(jnp.bfloat16)


def targets(rows):
    return dot(rows, target_map()).astype(jnp.bfloat16)


def weight_map():
    k = lax.broadcasted_iota(jnp.int32, (COLS, LANES), 0)
    m = lax.broadcasted_iota(jnp.int32, (COLS, LANES), 1)
    return jnp.where(k == m, 1.0, 0.0).astype(jnp.bfloat16)


def weights(rows):
    return dot(weight_map(), rows, NT).astype(jnp.bfloat16)


def block(i, size):
    return pl.ds(pl.multiple_of(i * size, size), size)


def cost(pairs):
    return pl.CostEstimate(
        flops=pairs * 2 * LEAF * LEAF * 384, bytes_accessed=4 << 20, transcendentals=pairs * LEAF * LEAF
    )


def features(xb):
    x = xb.astype(jnp.float32)
    n = jnp.sum(x * x, axis=0, keepdims=True) * -0.125
    n1 = n.astype(jnp.bfloat16).astype(jnp.float32)
    n2 = (n - n1).astype(jnp.bfloat16).astype(jnp.float32)
    n3 = (n - n1 - n2).astype(jnp.bfloat16).astype(jnp.float32)
    r = lax.broadcasted_iota(jnp.int32, xb.shape, 0)
    one = jnp.where(r < 6, 1.0, 0.0)
    ext = jnp.where(r == 0, n1, jnp.where(r == 1, n2, jnp.where(r == 2, n3, one)))
    pad = jnp.zeros((LANES - COLS - 2 * FEAT, xb.shape[1]), jnp.bfloat16)
    return [xb, ext.astype(jnp.bfloat16), pad]


def event_table(events, coeffs, store):
    def build(c, _):
        at = block(c, LEAF)
        full = jnp.concatenate([coeffs[:, at]] + features(events[:, at]), axis=0)
        store(at, full.T)
        return 0

    lax.fori_loop(0, events.shape[1] // LEAF, build, 0)


def fetch(table, ids):
    return jnp.concatenate([table[pl.ds(i, 1), :] for i in ids], axis=0)


def start_copies(pairs, sems):
    moves = [pltpu.make_async_copy(src, dst, sems.at[i]) for i, (src, dst) in enumerate(pairs)]
    for m in moves:
        m.start()
    return moves


def own_kernel(
    perm_hbm, skel_hbm, events_hbm, coeffs_hbm, own_out,
    table, rows, spick, perm, skel, events, coeffs, sems,
):
    moves = start_copies(
        [(events_hbm, events), (coeffs_hbm, coeffs), (perm_hbm, perm), (skel_hbm, skel)], sems
    )
    moves[0].wait()
    moves[1].wait()

    def store(at, full):
        rows[at, :] = full
        table[at, :] = full.astype(jnp.float32)

    event_table(events, coeffs, store)
    moves[2].wait()
    moves[3].wait()
    for j in range(0, RANK, 8):
        spick[j : j + 8, :] = fetch(table, [perm[0, skel[0, j + u]] for u in range(8)])
    s = spick[...]
    k = jnp.exp(dot(rows[...], targets(s.astype(jnp.bfloat16)), NT)).astype(jnp.bfloat16)
    su = dot(coeffs[...], k) / events.shape[1] ** 0.5
    own_out[:COLS, :] = su.astype(jnp.bfloat16)
    own_out[COLS : COLS + FEAT, :] = s.T[X0:N0].astype(jnp.bfloat16)
    own_out[COLS + FEAT :, :] = jnp.zeros((LANES - COLS - FEAT, RANK), jnp.bfloat16)


def tree_kernel(
    perm_hbm, events_hbm, coeffs_hbm, lo_hbm, hi_hbm, w_hbm, t_hbm,
    lo_out, hi_out, w_out, t_out, table, picked, perm, events, coeffs, sems,
):
    moves = start_copies([(events_hbm, events), (coeffs_hbm, coeffs), (perm_hbm, perm)], sems)
    moves[0].wait()
    moves[1].wait()

    def store(at, full):
        table[at, :] = full.astype(jnp.float32)

    event_table(events, coeffs, store)
    moves[2].wait()
    step = 64

    def gather(rows_out, base, c, _):
        def some(b, _):
            for v in range(0, step, 8):
                e = (base + c) * LEAF + b * step + v
                picked[block(b * (step // 8) + v // 8, 8), :] = fetch(
                    table, [perm[0, e + u] for u in range(8)]
                )
            return 0

        lax.fori_loop(0, LEAF // step, some, 0)
        at = block(base + c, LEAF)
        r = picked[...]
        rb = r.astype(jnp.bfloat16)
        rows_out[block(c, LEAF), :] = rb
        w_out[:, at] = r.T[:COLS].astype(jnp.bfloat16)
        t_out[at, :] = targets(rb)
        return 0

    half = events.shape[1] // LEAF // 2
    lax.fori_loop(0, half, functools.partial(gather, lo_out, 0), 0)
    outs = [
        pltpu.make_async_copy(src, dst, sems.at[3 + i])
        for i, (src, dst) in enumerate(
            [(lo_out, lo_hbm), (hi_out, hi_hbm), (w_out, w_hbm), (t_out, t_hbm)]
        )
    ]
    outs[0].start()
    lax.fori_loop(0, half, functools.partial(gather, hi_out, half), 0)
    for m in outs[1:]:
        m.start()
    for m in outs:
        m.wait()


def halves_dot(lo, hi, w, ts):
    half = lo.shape[0]
    ka = jnp.exp(dot(lo[...], ts, NT)).astype(jnp.bfloat16)
    kb = jnp.exp(dot(hi[...], ts, NT)).astype(jnp.bfloat16)
    return dot(w[:, :half], ka) + dot(w[:, half:], kb)


SMEM = pl.BlockSpec(memory_space=pltpu.SMEM)
VMEM = pl.BlockSpec(memory_space=pltpu.VMEM)
ANY = pl.BlockSpec(memory_space=pl.ANY)


def params(limit=VMEM_LIMIT):
    return pltpu.CompilerParams(vmem_limit_bytes=limit)


def own_call(perm, skel, events, coeffs):
    n = events.shape[1]
    return pl.pallas_call(
        own_kernel,
        out_shape=jax.ShapeDtypeStruct((LANES, RANK), jnp.bfloat16),
        in_specs=[ANY] * 4,
        out_specs=VMEM,
        scratch_shapes=[
            pltpu.VMEM((n, LANES), jnp.float32),
            pltpu.VMEM((n, LANES), jnp.bfloat16),
            pltpu.VMEM((RANK, LANES), jnp.float32),
            pltpu.SMEM(perm.shape, jnp.int32),
            pltpu.SMEM(skel.shape, jnp.int32),
            pltpu.VMEM(events.shape, jnp.bfloat16),
            pltpu.VMEM(coeffs.shape, jnp.bfloat16),
            pltpu.SemaphoreType.DMA((4,)),
        ],
        compiler_params=params(),
        cost_estimate=cost(4),
        name="own_skeleton",
    )(perm, skel, events, coeffs)


def tree_call(perm, events, coeffs):
    n = events.shape[1]
    shapes = ((n // 2, LANES), (n // 2, LANES), (COLS, n), (n, LANES))
    return pl.pallas_call(
        tree_kernel,
        out_shape=tuple(jax.ShapeDtypeStruct(s, jnp.bfloat16) for s in shapes),
        in_specs=[ANY] * 3,
        out_specs=(ANY,) * 4,
        scratch_shapes=[pltpu.VMEM(s, jnp.bfloat16) for s in shapes]
        + [
            pltpu.VMEM((n, LANES), jnp.float32),
            pltpu.VMEM((LEAF, LANES), jnp.float32),
            pltpu.SMEM(perm.shape, jnp.int32),
            pltpu.VMEM(events.shape, jnp.bfloat16),
            pltpu.VMEM(coeffs.shape, jnp.bfloat16),
            pltpu.SemaphoreType.DMA((7,)),
        ],
        compiler_params=params(),
        cost_estimate=cost(40),
        name="tree_rows",
    )(perm, events, coeffs)


def event_rows(xb):
    none = jnp.zeros((COLS, xb.shape[1]), jnp.bfloat16)
    return jnp.concatenate([none] + features(xb), axis=0).T


def term_kernel(picks, low_all, lo_hbm, hi_hbm, w_hbm, term_out, hx_out, low_out, low_w, low_x, lo, hi, w, sems):
    moves = start_copies([(lo_hbm, lo), (hi_hbm, hi), (w_hbm, w)], sems)
    nodes = low_all.shape[0] // LANES
    for b in range(nodes):
        at = slice(b * RANK, (b + 1) * RANK)
        low_w[:, at] = low_all[b * LANES : b * LANES + COLS, :]
        low_x[:, at] = low_all[b * LANES + COLS : b * LANES + COLS + FEAT, :]
    low_out[...] = event_rows(low_x[...])
    hit = lax.broadcasted_iota(jnp.int32, (nodes * RANK, RANK), 0) == picks[...]
    hx = dot(low_x[...], jnp.where(hit, 1.0, 0.0).astype(jnp.bfloat16)).astype(jnp.bfloat16)
    hx_out[...] = hx
    for m in moves:
        m.wait()
    term_out[...] = halves_dot(lo, hi, w, targets(event_rows(hx)))


def term_call(picks, low_all, lo, hi, w):
    total = low_all.shape[0] // LANES * RANK
    return pl.pallas_call(
        term_kernel,
        out_shape=(
            jax.ShapeDtypeStruct((COLS, RANK), jnp.float32),
            jax.ShapeDtypeStruct((FEAT, RANK), jnp.bfloat16),
            jax.ShapeDtypeStruct((total, LANES), jnp.bfloat16),
            jax.ShapeDtypeStruct((COLS, total), jnp.bfloat16),
        ),
        in_specs=[VMEM] * 2 + [ANY] * 3,
        out_specs=(VMEM,) * 4,
        scratch_shapes=[
            pltpu.VMEM((FEAT, total), jnp.bfloat16),
            pltpu.VMEM(lo.shape, jnp.bfloat16),
            pltpu.VMEM(hi.shape, jnp.bfloat16),
            pltpu.VMEM(w.shape, jnp.bfloat16),
            pltpu.SemaphoreType.DMA((3,)),
        ],
        compiler_params=params(),
        cost_estimate=cost(4),
        name="high_term",
    )(picks, low_all, lo, hi, w)


def low_kernel(far, low, low_w, t, part):
    groups = far.shape[1] // 4
    leaves = part.shape[0]
    ks = []
    for j in range(leaves):
        leaf = pl.program_id(0) * leaves + j
        tl = t[j * LEAF : (j + 1) * LEAF, :]
        for g in range(groups):
            spots = [block(far[leaf, 4 * g + i], RANK) for i in range(4)]
            r = jnp.concatenate([low[s, :] for s in spots], axis=0)
            ks.append((spots, jnp.exp(dot(r, tl, NT)).astype(jnp.bfloat16)))
    for j in range(leaves):
        total = None
        for spots, k in ks[j * groups : (j + 1) * groups]:
            p = dot(jnp.concatenate([low_w[:, s] for s in spots], axis=1), k)
            total = p if total is None else total + p
        part[j] = total


def low_call(far, low, low_w, t):
    each = 2
    return pl.pallas_call(
        low_kernel,
        out_shape=jax.ShapeDtypeStruct((LEAF_DEV, COLS, LEAF), jnp.float32),
        grid=(LEAF_DEV // each,),
        in_specs=[
            SMEM,
            pl.BlockSpec(low.shape, lambda i: (0, 0)),
            pl.BlockSpec(low_w.shape, lambda i: (0, 0)),
            pl.BlockSpec((each * LEAF, LANES), lambda i: (i, 0)),
        ],
        out_specs=pl.BlockSpec((each, COLS, LEAF), lambda i: (i, 0, 0)),
        compiler_params=params(),
        cost_estimate=cost(64),
        name="far_low",
    )(far, low, low_w, t)


def pair_list(near, count, first, pairs, place):
    def leaf_slots(leaf, n):
        def slot(s, n):
            at, takes = place(near[leaf, s] - first[0])
            pairs[n] = leaf * 64 + at
            return n + jnp.where(takes, 1, 0)

        return lax.fori_loop(0, count[leaf], slot, n)

    n = lax.fori_loop(0, LEAF_DEV, leaf_slots, jnp.int32(0))
    for u in range(8):
        pairs[n + u] = LEAF_DEV * 64
    return n


def pair_sums(n, pairs, rows, w, t, acc):
    def step(begin, many):
        ks = []
        for u in range(many):
            e = pairs[begin + u]
            leaf, at = e // 64, e % 64
            tl = t[block(jnp.minimum(leaf, LEAF_DEV - 1), LEAF), :]
            k = jnp.exp(dot(rows[block(at, LEAF), :], tl, NT)).astype(jnp.bfloat16)
            ks.append((leaf, at, k))
        for leaf, at, k in ks:
            acc[leaf] = acc[leaf] + dot(w[:, block(at, LEAF)], k)

    def eight(s, _):
        step(s * 8, 8)
        return 0

    lax.fori_loop(0, n // 8, eight, 0)

    def four(s, _):
        step(n // 8 * 8 + s * 4, 4)
        return 0

    lax.fori_loop(0, (n % 8 + 3) // 4, four, 0)


def near_own_kernel(near, count, first, lo, hi, w_hbm, t_hbm, acc, rows, w, t, pairs, sems):
    half = lo.shape[0]
    moves = start_copies(
        [
            (lo, rows.at[pl.ds(0, half), :]),
            (hi, rows.at[pl.ds(half, half), :]),
            (w_hbm, w),
            (t_hbm, t),
        ],
        sems,
    )
    n = pair_list(near, count, first, pairs, lambda at: (at, (at >= 0) & (at < LEAF_DEV)))
    acc[...] = jnp.zeros_like(acc)
    for m in moves:
        m.wait()
    pair_sums(n, pairs, rows, w, t, acc)


def near_own_call(near, count, first, lo, hi, w, t):
    return pl.pallas_call(
        near_own_kernel,
        out_shape=jax.ShapeDtypeStruct((LEAF_DEV + 1, COLS, LEAF), jnp.float32),
        in_specs=[SMEM] * 3 + [ANY] * 4,
        out_specs=VMEM,
        scratch_shapes=[
            pltpu.VMEM(t.shape, jnp.bfloat16),
            pltpu.VMEM(w.shape, jnp.bfloat16),
            pltpu.VMEM(t.shape, jnp.bfloat16),
            pltpu.SMEM((LEAF_DEV * NEAR + 8,), jnp.int32),
            pltpu.SemaphoreType.DMA((4,)),
        ],
        compiler_params=params(),
        cost_estimate=cost(60),
        name="near_own",
    )(near, count, first, lo, hi, w, t)


def near_side_kernel(
    scales, near, count, first, left, right, t_hbm, acc_hbm, low_hbm, out, rows, w, t, acc, low, pairs, sems
):
    near_scale, low_scale = scales
    side = REACH * LEAF
    moves = start_copies(
        [
            (left, rows.at[pl.ds(0, side), :]),
            (right, rows.at[pl.ds(side, side), :]),
            (t_hbm, t),
            (acc_hbm, acc),
            (low_hbm, low),
        ],
        sems,
    )
    n = pair_list(
        near, count, first, pairs,
        lambda at: (jnp.where(at < 0, at + REACH, at - REACH), (at < 0) | (at >= LEAF_DEV)),
    )
    moves[0].wait()
    moves[1].wait()

    def flip(b, _):
        for at in (block(b, LEAF), block(b + REACH, LEAF)):
            w[:, at] = weights(rows[at, :])
        return 0

    lax.fori_loop(0, REACH, flip, 0)
    for m in moves[2:]:
        m.wait()
    pair_sums(n, pairs, rows, w, t, acc)
    for leaf in range(LEAF_DEV):
        at = slice(leaf * LEAF, (leaf + 1) * LEAF)
        out[:, at] = acc[leaf] * near_scale + low[leaf] * low_scale


def near_side_call(scales, near, count, first, left, right, t, acc, low):
    n = 2 * REACH * LEAF
    return pl.pallas_call(
        lambda *refs: near_side_kernel(scales, *refs),
        out_shape=jax.ShapeDtypeStruct((COLS, LEAF_DEV * LEAF), jnp.float32),
        in_specs=[SMEM] * 3 + [ANY] * 5,
        out_specs=VMEM,
        scratch_shapes=[
            pltpu.VMEM((n, LANES), jnp.bfloat16),
            pltpu.VMEM((COLS, n), jnp.bfloat16),
            pltpu.VMEM(t.shape, jnp.bfloat16),
            pltpu.VMEM(acc.shape, jnp.float32),
            pltpu.VMEM(low.shape, jnp.float32),
            pltpu.SMEM((LEAF_DEV * NEAR + 8,), jnp.int32),
            pltpu.SemaphoreType.DMA((5,)),
        ],
        compiler_params=params(),
        cost_estimate=cost(50),
        name="near_sides",
    )(near, count, first, left, right, t, acc, low)


def upper_kernel(scale, ratio, terms, hx, upper):
    total = terms[:COLS, :]
    for m in range(1, terms.shape[0] // COLS):
        total = total + terms[m * COLS : (m + 1) * COLS, :]
    upper[:COLS, :] = (total * scale).astype(jnp.bfloat16) * jnp.bfloat16(ratio)
    upper[COLS:, :] = hx[...]


def upper_call(scale, ratio, terms, hx):
    return pl.pallas_call(
        lambda *refs: upper_kernel(scale, ratio, *refs),
        out_shape=jax.ShapeDtypeStruct((COLS + FEAT, RANK), jnp.bfloat16),
        in_specs=[VMEM] * 2,
        out_specs=VMEM,
        compiler_params=params(),
        name="high_sum",
    )(terms, hx)


def high_kernel(scale, *refs):
    *ups, t, part, out = refs
    high_w = jnp.concatenate([u[:COLS, :] for u in ups], axis=1)
    high_x = event_rows(jnp.concatenate([u[COLS:, :] for u in ups], axis=1))
    many = out.shape[1] // LEAF
    ats = [slice(j * LEAF, (j + 1) * LEAF) for j in range(many)]
    ks = [jnp.exp(dot(high_x, t[at, :], NT)).astype(jnp.bfloat16) for at in ats]
    for at, k in zip(ats, ks):
        out[:, at] = (part[:, at] + dot(high_w, k) * scale).astype(jnp.bfloat16)


def high_call(scale, ups, t, part):
    many = 4
    return pl.pallas_call(
        lambda *refs: high_kernel(scale, *refs),
        out_shape=jax.ShapeDtypeStruct(part.shape, jnp.bfloat16),
        grid=(LEAF_DEV // many,),
        in_specs=[pl.BlockSpec(u.shape, lambda i: (0, 0)) for u in ups]
        + [
            pl.BlockSpec((many * LEAF, LANES), lambda i: (i, 0)),
            pl.BlockSpec((COLS, many * LEAF), lambda i: (0, i)),
        ],
        out_specs=pl.BlockSpec((COLS, many * LEAF), lambda i: (0, i)),
        compiler_params=params(),
        cost_estimate=cost(12),
        name="high_out",
    )(*ups, t, part)


def swap(x, axis, mask):
    count = lax.axis_size(axis)
    return lax.ppermute(x, axis, [(i, i ^ mask) for i in range(count)])


def after(x, *others):
    return lax.optimization_barrier((x, *others))[0]


def per_device(events, coeffs, tree_perm, near_list, near_count, far_list, skel_low, skel_high):
    group_devs = lax.axis_size("inner")
    group_count = lax.axis_size("outer")
    far_count = far_list.shape[1]
    ev_dev = events.shape[1]
    inner = lax.axis_index("inner").astype(jnp.int32)
    device = lax.axis_index("outer").astype(jnp.int32) * group_devs + inner
    devices = group_devs * group_count
    first = (device * LEAF_DEV).reshape(1)
    own = own_call(tree_perm, skel_low, events, coeffs)
    low_all = lax.all_gather(own, "inner", axis=0, tiled=True)
    lo, hi, w, t = tree_call(after(tree_perm, own), events, coeffs)
    both = ("outer", "inner")
    left = lax.ppermute(hi, both, [(i, i + 1) for i in range(devices - 1)])
    right = lax.ppermute(lo, both, [(i + 1, i) for i in range(devices - 1)])
    acc = near_own_call(near_list, near_count, first, lo, hi, w, t)

    term, hx, low, low_w = term_call(skel_high, after(low_all, acc), lo, hi, w)
    terms = lax.all_gather(term, "inner", axis=0, tiled=True)
    far = low_call(far_list, after(low, term), low_w, t)
    near_scale = 16.0 / (LEAF * NEAR) ** 0.5
    low_scale = 128.0 / (far_count * RANK) ** 0.5
    scales = (near_scale, low_scale)
    part = near_side_call(scales, near_list, near_count, first, left, right, t, acc, far)

    scale = 1.0 / (ev_dev * group_devs) ** 0.5
    upper = upper_call(scale, (far_count / group_count) ** 0.5, after(terms, part), hx)
    ups = [swap(upper, "outer", m) for m in range(1, group_count)]
    return high_call(low_scale, ups, t, part)


def solution(mesh):
    return jax.shard_map(
        per_device,
        mesh=mesh,
        in_specs=(
            P(None, ("outer", "inner")),
            P(None, ("outer", "inner")),
            P(("outer", "inner"), None),
            P(("outer", "inner"), None),
            P(("outer", "inner")),
            P(("outer", "inner"), None),
            P(("outer", "inner"), None),
            P("outer", None),
        ),
        out_specs=P(None, ("outer", "inner")),
        check_vma=False,
    )
```

time: 137 us -> 137 us (level)
  the two profiles are of different devices: /device:TPU:1 before, /device:TPU:0 now
where the time goes in v2:
time: 137 us; the launch traced here: 135 us
  Pallas kernels  89.7 us (65%)
  waiting for transfers between devices  21.5 us (16%)
  between operations  13.5 us (10%)
  starting transfers between devices  7.39 us (5%)
  local copies, waits for them, and re-layouts  2.56 us (2%)
    pallas_call x1, Pallas kernels, near_own_call(): pl.pallas_call(near_own_kernel, out_shape=jax.ShapeDtypeStruct((LEAF_DEV...  22.6 us
    pallas_call x1, Pallas kernels, low_call(): pl.pallas_call(low_kernel, out_shape=jax.ShapeDtypeStruct((LEAF_DEV, COLS...  18.7 us
    pallas_call x1, Pallas kernels, near_side_call(): pl.pallas_call(lambda *refs: near_side_kernel(scales, *refs), out_shape=j...  16 us
    pallas_call x1, Pallas kernels, tree_call(): pl.pallas_call(tree_kernel, out_shape=tuple((jax.ShapeDtypeStruct(s, jnp....  14.7 us
    all_gather x1, waiting for transfers between devices, per_device(): low_all = lax.all_gather(own, 'inner', axis=0, tiled=True)  10.6 us
    all_gather x1, waiting for transfers between devices, per_device(): terms = lax.all_gather(term, 'inner', axis=0, tiled=True)  6.19 us
    pallas_call x1, Pallas kernels, high_call(): pl.pallas_call(lambda *refs: high_kernel(scale, *refs), out_shape=jax.Sha...  5.86 us
    pallas_call x1, Pallas kernels, term_call(): pl.pallas_call(term_kernel, out_shape=(jax.ShapeDtypeStruct((COLS, RANK),...  5.01 us
  transfers between devices with their start and end apart: 7, of which 4 were waited for; matrix products, arithmetic and copies ran while one was open for 0% of the time, Pallas kernels for 57%

profile of v2, /device:TPU:0, one launch (start us, length us, event | category | flops | bytes accessed | tf_op | source)
XLA Modules:
  0.0 134.6 jit_solution(16594419777878359862)
XLA Ops:
  6.5 0.0 all-gather.3.cloned.1.call-start
  6.5 5.0 %own_skeleton.1 = bf16[128,128]{1,0:T(8,128)(2,1)} custom-call(s32[1,8192]{1,0:T(1,128)} %perm_hbm.2, s32[1,128]{1,0:T(1,128)} %skel_hbm.1, bf16[16,8192]{1,0:T(8,128)(2,1)} %events_hbm.3, bf16[64,8192]{1,0:T(8,128)(2,1)} %coeffs_hbm.3), custom_call_target="tpu_custom_call" | custom-call | flops 805306368 | bytes 4194304 | tf_op jit(solution)/shard_map/own_skeleton/pallas_call | solution.py:192
  11.5 0.0 all-gather.3.cloned.1.call-update
  11.5 0.0 all-gather.5.cloned.1.call-start
  11.6 14.7 %tree_rows.1 = (bf16[4096,128]{1,0:T(8,128)(2,1)}, bf16[4096,128]{1,0:T(8,128)(2,1)}, bf16[64,8192]{1,0:T(8,128)(2,1)}, bf16[8192,128]{1,0:T(8,128)(2,1)}) custom-call(s32[1,8192]{1,0:T(1,128)} %perm_hbm.2, bf16[16,8192]{1,0:T(8,128)(2,1)} %events_hbm.3, bf16[64,8192]{1,0:T(8,128)(2,1)} %coeffs_hbm.3), custom_call_target="tpu_custom_call" | custom-call | flops 8053063680 | bytes 4194304 | tf_op jit(solution)/shard_map/tree_rows/pallas_call | solution.py:216
  26.3 1.4 %collective-permute-start = (bf16[4096,128]{1,0:T(8,128)(2,1)}, bf16[4096,128]{1,0:T(8,128)(2,1)S(1)}, u32[]{:S(2)}, u32[]{:S(2)}) collective-permute-start(bf16[4096,128]{1,0:T(8,128)(2,1)} %get-tuple-element.19.hi.hi_hbm), channel_id=1, source_target_pairs={{0,1},{1,2},{2,3},{3,4},{4,5},{5,6},{6,7},{7,8},{8,9},{9,10},{10,1... | collective-permute-start | bytes 3145736 | tf_op jit(solution)/shard_map/ppermute | solution.py:525
  27.6 1.3 collective-permute-start.1
  29.0 22.6 %near_own.1.refs_6_ = f32[17,64,512]{2,1,0:T(8,128)} custom-call(s32[16,32]{1,0:T(8,128)} %refs_0_.1, s32[16]{0:T(128)} %refs_1_.1, s32[1]{0:T(128)} %bitcast.first.refs_2_, bf16[4096,128]{1,0:T(8,128)(2,1)} %get-tuple-element.18.lo.lo_hbm, bf16[4096,128]{1,0:T(8,128)(2,1)} %get-tuple-element.19.hi.hi_hbm, bf16[64,8192]{1,0:T(8,128)(2,1)} %get-tuple-element.20.w_hbm, ...), custom_call_target="tpu_custom_call" | custom-call | flops 12079595520 | bytes 4194304 | tf_op jit(solution)/shard_map/near_own/pallas_call | solution.py:379
  51.6 10.6 %all-gather.3.cloned.1.call-done.low_all = bf16[4096,128]{1,0:T(8,128)(2,1)} async-done(((bf16[128,128]{1,0:T(8,128)(2,1)}), bf16[4096,128]{1,0:T(8,128)(2,1)}) %all-gather.3.cloned.1.call-update) | async-done | bytes 1048592 | tf_op jit(solution)/shard_map/all_gather | solution.py:522
  62.2 5.0 %high_term.1 = (f32[64,128]{1,0:T(8,128)}, bf16[16,128]{1,0:T(8,128)(2,1)}, bf16[4096,128]{1,0:T(8,128)(2,1)}, bf16[64,4096]{1,0:T(8,128)(2,1)}) custom-call(s32[1,128]{1,0:T(1,128)} %picks.1, bf16[4096,128]{1,0:T(8,128)(2,1)} %all-gather.3.cloned.1.call-done.low_all, bf16[4096,128]{1,0:T(8,128)(2,1)} %get-tuple-element.18.lo.lo_hbm, ...), custom_call_target="tpu_custom_call" | custom-call | flops 805306368 | bytes 4194304 | tf_op jit(solution)/shard_map/high_term/pallas_call | solution.py:259
  67.2 0.0 all-gather.5.cloned.1.call-update
  67.2 18.7 %far_low.1.refs_7_ = f32[16,64,512]{2,1,0:T(8,128)} custom-call(s32[16,16]{1,0:T(8,128)} %far.1, bf16[4096,128]{1,0:T(8,128)(2,1)} %get-tuple-element.25.low, bf16[64,4096]{1,0:T(8,128)(2,1)} %get-tuple-element.26.low_w, bf16[8192,128]{1,0:T(8,128)(2,1)} %get-tuple-element.21.t_hbm.t.refs_5_.refs_3_), custom_call_target="tpu_custom_call" | custom-call | flops 12884901888 | bytes 4194304 | tf_op jit(solution)/shard_map/far_low/pallas_call | solution.py:303
  85.9 0.0 collective-permute-done.refs_3_
  85.9 0.0 copy-start
  85.9 0.0 collective-permute-done.1.refs_4_
  85.9 1.0 copy-done
  86.9 0.0 copy-start.1
  86.9 1.0 copy-done.1
  87.9 16.0 %near_sides.1.refs_4_ = f32[64,8192]{1,0:T(8,128)} custom-call(s32[16,32]{1,0:T(8,128)} %refs_0_.1, s32[16]{0:T(128)} %refs_1_.1, s32[1]{0:T(128)} %bitcast.first.refs_2_, bf16[4096,128]{1,0:T(8,128)(2,1)} %copy-done, bf16[4096,128]{1,0:T(8,128)(2,1)} %copy-done.1, bf16[8192,128]{1,0:T(8,128)(2,1)} %get-tuple-element.21.t_hbm.t.refs_5_.refs_3_, ...), custom_call_target="tpu_custom_call" | custom-call | flops 10066329600 | bytes 4194304 | tf_op jit(solution)/shard_map/near_sides/pallas_call | solution.py:435
  103.8 6.2 %all-gather.5.cloned.1.call-done.refs_0_ = f32[2048,128]{1,0:T(8,128)} async-done(((f32[64,128]{1,0:T(8,128)}), f32[2048,128]{1,0:T(8,128)}) %all-gather.5.cloned.1.call-update) | async-done | bytes 1048592 | tf_op jit(solution)/shard_map/all_gather | solution.py:530
  110.0 1.9 %high_sum.1 = bf16[80,128]{1,0:T(8,128)(2,1)} custom-call(f32[2048,128]{1,0:T(8,128)} %all-gather.5.cloned.1.call-done.refs_0_, bf16[16,128]{1,0:T(8,128)(2,1)} %get-tuple-element.28.refs_1_), custom_call_target="tpu_custom_call" | custom-call | tf_op jit(solution)/shard_map/high_sum/pallas_call | solution.py:464
  111.9 1.4 %collective-permute-start.2 = (bf16[80,128]{1,0:T(8,128)(2,1)}, bf16[80,128]{1,0:T(8,128)(2,1)S(1)}, u32[]{:S(2)}, u32[]{:S(2)}) collective-permute-start(bf16[80,128]{1,0:T(8,128)(2,1)} %high_sum.1), channel_id=1, source_target_pairs={{0,32},{32,0},{64,96},{96,64},{1,33},{33,1},{65,97},{97,65},{2,34}... | collective-permute-start | bytes 61448 | tf_op jit(solution)/shard_map/ppermute | solution.py:505
  113.4 2.7 %collective-permute-start.3 = (bf16[80,128]{1,0:T(8,128)(2,1)}, bf16[80,128]{1,0:T(8,128)(2,1)S(1)}, u32[]{:S(2)}, u32[]{:S(2)}) collective-permute-start(bf16[80,128]{1,0:T(8,128)(2,1)} %high_sum.1), channel_id=1, source_target_pairs={{0,64},{32,96},{64,0},{96,32},{1,65},{33,97},{65,1},{97,33},{2,66}... | collective-permute-start | bytes 61448 | tf_op jit(solution)/shard_map/ppermute | solution.py:505
  116.1 0.6 collective-permute-start.4
  116.6 0.0 collective-permute-done.2.refs_0_
  116.6 0.0 copy-start.2
  116.6 2.2 %collective-permute-done.3.refs_1_ = bf16[80,128]{1,0:T(8,128)(2,1)S(1)} collective-permute-done((bf16[80,128]{1,0:T(8,128)(2,1)}, bf16[80,128]{1,0:T(8,128)(2,1)S(1)}, u32[]{:S(2)}, u32[]{:S(2)}) %collective-permute-start.3) | collective-permute-done | bytes 20512 | tf_op jit(solution)/shard_map/ppermute | solution.py:505
  118.9 2.4 %collective-permute-done.4.refs_2_ = bf16[80,128]{1,0:T(8,128)(2,1)S(1)} collective-permute-done((bf16[80,128]{1,0:T(8,128)(2,1)}, bf16[80,128]{1,0:T(8,128)(2,1)S(1)}, u32[]{:S(2)}, u32[]{:S(2)}) %collective-permute-start.4) | collective-permute-done | bytes 20512 | tf_op jit(solution)/shard_map/ppermute | solution.py:505
  121.3 0.0 copy-done.2
  121.3 0.0 copy-done.3
  121.3 0.6 copy-done.4
  121.9 5.9 %high_out.1 = bf16[64,8192]{1,0:T(8,128)(2,1)} custom-call(bf16[80,128]{1,0:T(8,128)(2,1)} %copy-done.2, bf16[80,128]{1,0:T(8,128)(2,1)} %copy-done.3, bf16[80,128]{1,0:T(8,128)(2,1)} %copy-done.4, bf16[8192,128]{1,0:T(8,128)(2,1)} %get-tuple-element.21.t_hbm.t.refs_5_.refs_3_, f32[64,8192]{1,0:T(8,128)} %near_sides.1.refs_4_), custom_call_target="tpu_custom_call" | custom-call | flops 2415919104 | bytes 4194304 | tf_op jit(solution)/shard_map/high_out/pallas_call | solution.py:487
  (2 shorter events, 0.0 us)
Async XLA Ops:
  6.5 55.6 %all-gather.3.cloned.1.call-start = ((), (), s32[]{:S(2)}) async-start(), calls=%async_computation | async-start | bytes 1081344 | tf_op jit(solution)/shard_map/all_gather | solution.py:522
  11.5 98.5 %all-gather.5.cloned.1.call-start = ((), (), s32[]{:S(2)}) async-start(), calls=%async_computation.1 | async-start | bytes 1081344 | tf_op jit(solution)/shard_map/all_gather | solution.py:530
  26.3 59.6 %collective-permute-start = (bf16[4096,128]{1,0:T(8,128)(2,1)}, bf16[4096,128]{1,0:T(8,128)(2,1)S(1)}, u32[]{:S(2)}, u32[]{:S(2)}) collective-permute-start(bf16[4096,128]{1,0:T(8,128)(2,1)} %get-tuple-element.19.hi.hi_hbm), channel_id=1, source_target_pairs={{0,1},{1,2},{2,3},{3,4},{4,5},{5,6},{6,7},{7,8},{8,9},{9,10},{10,1... | collective-permute-start | bytes 3145736 | tf_op jit(solution)/shard_map/ppermute | solution.py:525
  27.6 58.3 %collective-permute-start.1 = (bf16[4096,128]{1,0:T(8,128)(2,1)}, bf16[4096,128]{1,0:T(8,128)(2,1)S(1)}, u32[]{:S(2)}, u32[]{:S(2)}) collective-permute-start(bf16[4096,128]{1,0:T(8,128)(2,1)} %get-tuple-element.18.lo.lo_hbm), channel_id=1, source_target_pairs={{1,0},{2,1},{3,2},{4,3},{5,4},{6,5},{7,6},{8,7},{9,8},{10,9},{11,1... | collective-permute-start | bytes 3145736 | tf_op jit(solution)/shard_map/ppermute | solution.py:526
  85.9 1.0 copy-start
  86.9 1.0 copy-start.1
  111.9 4.7 %collective-permute-start.2 = (bf16[80,128]{1,0:T(8,128)(2,1)}, bf16[80,128]{1,0:T(8,128)(2,1)S(1)}, u32[]{:S(2)}, u32[]{:S(2)}) collective-permute-start(bf16[80,128]{1,0:T(8,128)(2,1)} %high_sum.1), channel_id=1, source_target_pairs={{0,32},{32,0},{64,96},{96,64},{1,33},{33,1},{65,97},{97,65},{2,34}... | collective-permute-start | bytes 61448 | tf_op jit(solution)/shard_map/ppermute | solution.py:505
  113.4 5.5 %collective-permute-start.3 = (bf16[80,128]{1,0:T(8,128)(2,1)}, bf16[80,128]{1,0:T(8,128)(2,1)S(1)}, u32[]{:S(2)}, u32[]{:S(2)}) collective-permute-start(bf16[80,128]{1,0:T(8,128)(2,1)} %high_sum.1), channel_id=1, source_target_pairs={{0,64},{32,96},{64,0},{96,32},{1,65},{33,97},{65,1},{97,33},{2,66}... | collective-permute-start | bytes 61448 | tf_op jit(solution)/shard_map/ppermute | solution.py:505
  116.1 5.2 %collective-permute-start.4 = (bf16[80,128]{1,0:T(8,128)(2,1)}, bf16[80,128]{1,0:T(8,128)(2,1)S(1)}, u32[]{:S(2)}, u32[]{:S(2)}) collective-permute-start(bf16[80,128]{1,0:T(8,128)(2,1)} %high_sum.1), channel_id=1, source_target_pairs={{0,96},{32,64},{64,32},{96,0},{1,97},{33,65},{65,33},{97,1},{2,98}... | collective-permute-start | bytes 61448 | tf_op jit(solution)/shard_map/ppermute | solution.py:505
  116.6 4.6 %copy-start.2 = (bf16[80,128]{1,0:T(8,128)(2,1)}, bf16[80,128]{1,0:T(8,128)(2,1)S(1)}, u32[]{:S(2)}) copy-start(bf16[80,128]{1,0:T(8,128)(2,1)S(1)} %collective-permute-done.2.refs_0_) | copy-start | bytes 61444
  118.9 2.4 %copy-start.3 = (bf16[80,128]{1,0:T(8,128)(2,1)}, bf16[80,128]{1,0:T(8,128)(2,1)S(1)}, u32[]{:S(2)}) copy-start(bf16[80,128]{1,0:T(8,128)(2,1)S(1)} %collective-permute-done.3.refs_1_) | copy-start | bytes 61444
  121.3 0.6 copy-start.4
Sparse Core Ops, SparseCore 0:
  11.7 50.4 all-gather.2
  67.3 42.6 all-gather.4

commit v3 on v2

--- a/solution.py
+++ b/solution.py
@@ -74,14 +74,26 @@
     return [xb, ext.astype(jnp.bfloat16), pad]
 
 
-def event_table(events, coeffs, store):
+QUARTERS = 4
+
+
+def quarters(src, dst):
+    size = src.shape[1] // QUARTERS
+    return [(src.at[:, pl.ds(i * size, size)], dst.at[:, pl.ds(i * size, size)]) for i in range(QUARTERS)]
+
+
+def event_table(events, coeffs, event_moves, coeff_moves, store):
     def build(c, _):
         at = block(c, LEAF)
         full = jnp.concatenate([coeffs[:, at]] + features(events[:, at]), axis=0)
         store(at, full.T)
         return 0
 
-    lax.fori_loop(0, events.shape[1] // LEAF, build, 0)
+    each = events.shape[1] // LEAF // QUARTERS
+    for i in range(QUARTERS):
+        event_moves[i].wait()
+        coeff_moves[i].wait()
+        lax.fori_loop(i * each, (i + 1) * each, build, 0)
 
 
 def fetch(table, ids):
@@ -100,18 +112,19 @@
     table, rows, spick, perm, skel, events, coeffs, sems,
 ):
     moves = start_copies(
-        [(events_hbm, events), (coeffs_hbm, coeffs), (perm_hbm, perm), (skel_hbm, skel)], sems
+        quarters(events_hbm, events)
+        + quarters(coeffs_hbm, coeffs)
+        + [(perm_hbm, perm), (skel_hbm, skel)],
+        sems,
     )
-    moves[0].wait()
-    moves[1].wait()
 
     def store(at, full):
         rows[at, :] = full
         table[at, :] = full.astype(jnp.float32)
 
-    event_table(events, coeffs, store)
-    moves[2].wait()
-    moves[3].wait()
+    event_table(events, coeffs, moves[:QUARTERS], moves[QUARTERS : 2 * QUARTERS], store)
+    moves[-2].wait()
+    moves[-1].wait()
     for j in range(0, RANK, 8):
         spick[j : j + 8, :] = fetch(table, [perm[0, skel[0, j + u]] for u in range(8)])
     s = spick[...]
@@ -126,15 +139,15 @@
     perm_hbm, events_hbm, coeffs_hbm, lo_hbm, hi_hbm, w_hbm, t_hbm,
     lo_out, hi_out, w_out, t_out, table, picked, perm, events, coeffs, sems,
 ):
-    moves = start_copies([(events_hbm, events), (coeffs_hbm, coeffs), (perm_hbm, perm)], sems)
-    moves[0].wait()
-    moves[1].wait()
+    moves = start_copies(
+        quarters(events_hbm, events) + quarters(coeffs_hbm, coeffs) + [(perm_hbm, perm)], sems
+    )
 
     def store(at, full):
         table[at, :] = full.astype(jnp.float32)
 
-    event_table(events, coeffs, store)
-    moves[2].wait()
+    event_table(events, coeffs, moves[:QUARTERS], moves[QUARTERS : 2 * QUARTERS], store)
+    moves[-1].wait()
     step = 64
 
     def gather(rows_out, base, c, _):
@@ -158,7 +171,7 @@
     half = events.shape[1] // LEAF // 2
     lax.fori_loop(0, half, functools.partial(gather, lo_out, 0), 0)
     outs = [
-        pltpu.make_async_copy(src, dst, sems.at[3 + i])
+        pltpu.make_async_copy(src, dst, sems.at[2 * QUARTERS + 1 + i])
         for i, (src, dst) in enumerate(
             [(lo_out, lo_hbm), (hi_out, hi_hbm), (w_out, w_hbm), (t_out, t_hbm)]
         )
@@ -202,7 +215,7 @@
             pltpu.SMEM(skel.shape, jnp.int32),
             pltpu.VMEM(events.shape, jnp.bfloat16),
             pltpu.VMEM(coeffs.shape, jnp.bfloat16),
-            pltpu.SemaphoreType.DMA((4,)),
+            pltpu.SemaphoreType.DMA((2 * QUARTERS + 2,)),
         ],
         compiler_params=params(),
         cost_estimate=cost(4),
@@ -225,7 +238,7 @@
             pltpu.SMEM(perm.shape, jnp.int32),
             pltpu.VMEM(events.shape, jnp.bfloat16),
             pltpu.VMEM(coeffs.shape, jnp.bfloat16),
-            pltpu.SemaphoreType.DMA((7,)),
+            pltpu.SemaphoreType.DMA((2 * QUARTERS + 5,)),
         ],
         compiler_params=params(),
         cost_estimate=cost(40),
@@ -238,20 +251,19 @@
     return jnp.concatenate([none] + features(xb), axis=0).T
 
 
-def term_kernel(picks, low_all, lo_hbm, hi_hbm, w_hbm, term_out, hx_out, low_out, low_w, low_x, lo, hi, w, sems):
+def term_kernel(picks, low_all, lo_hbm, hi_hbm, w_hbm, term_out, hx_out, low_x, lo, hi, w, sems):
     moves = start_copies([(lo_hbm, lo), (hi_hbm, hi), (w_hbm, w)], sems)
     nodes = low_all.shape[0] // LANES
     for b in range(nodes):
-        at = slice(b * RANK, (b + 1) * RANK)
-        low_w[:, at] = low_all[b * LANES : b * LANES + COLS, :]
-        low_x[:, at] = low_all[b * LANES + COLS : b * LANES + COLS + FEAT, :]
-    low_out[...] = event_rows(low_x[...])
+        x = low_all[b * LANES + COLS : b * LANES + COLS + FEAT, :]
+        low_x[:, b * RANK : (b + 1) * RANK] = x
     hit = lax.broadcasted_iota(jnp.int32, (nodes * RANK, RANK), 0) == picks[...]
     hx = dot(low_x[...], jnp.where(hit, 1.0, 0.0).astype(jnp.bfloat16)).astype(jnp.bfloat16)
     hx_out[...] = hx
+    ts = targets(event_rows(hx))
     for m in moves:
         m.wait()
-    term_out[...] = halves_dot(lo, hi, w, targets(event_rows(hx)))
+    term_out[...] = halves_dot(lo, hi, w, ts)
 
 
 def term_call(picks, low_all, lo, hi, w):
@@ -261,11 +273,9 @@
         out_shape=(
             jax.ShapeDtypeStruct((COLS, RANK), jnp.float32),
             jax.ShapeDtypeStruct((FEAT, RANK), jnp.bfloat16),
-            jax.ShapeDtypeStruct((total, LANES), jnp.bfloat16),
-            jax.ShapeDtypeStruct((COLS, total), jnp.bfloat16),
         ),
         in_specs=[VMEM] * 2 + [ANY] * 3,
-        out_specs=(VMEM,) * 4,
+        out_specs=(VMEM,) * 2,
         scratch_shapes=[
             pltpu.VMEM((FEAT, total), jnp.bfloat16),
             pltpu.VMEM(lo.shape, jnp.bfloat16),
@@ -279,7 +289,18 @@
     )(picks, low_all, lo, hi, w)
 
 
-def low_kernel(far, low, low_w, t, part):
+def low_kernel(far, low_all, t, part, low, low_w):
+    nodes = low_all.shape[0] // LANES
+
+    @pl.when(pl.program_id(0) == 0)
+    def _():
+        for b in range(0, nodes, 4):
+            xs = []
+            for j in range(b, b + 4):
+                low_w[:, j * RANK : (j + 1) * RANK] = low_all[j * LANES : j * LANES + COLS, :]
+                xs.append(low_all[j * LANES + COLS : j * LANES + COLS + FEAT, :])
+            low[b * RANK : (b + 4) * RANK, :] = event_rows(jnp.concatenate(xs, axis=1))
+
     groups = far.shape[1] // 4
     leaves = part.shape[0]
     ks = []
@@ -298,23 +319,27 @@
         part[j] = total
 
 
-def low_call(far, low, low_w, t):
+def low_call(far, low_all, t):
     each = 2
+    total = low_all.shape[0] // LANES * RANK
     return pl.pallas_call(
         low_kernel,
         out_shape=jax.ShapeDtypeStruct((LEAF_DEV, COLS, LEAF), jnp.float32),
         grid=(LEAF_DEV // each,),
         in_specs=[
             SMEM,
-            pl.BlockSpec(low.shape, lambda i: (0, 0)),
-            pl.BlockSpec(low_w.shape, lambda i: (0, 0)),
+            pl.BlockSpec(low_all.shape, lambda i: (0, 0)),
             pl.BlockSpec((each * LEAF, LANES), lambda i: (i, 0)),
         ],
         out_specs=pl.BlockSpec((each, COLS, LEAF), lambda i: (i, 0, 0)),
+        scratch_shapes=[
+            pltpu.VMEM((total, LANES), jnp.bfloat16),
+            pltpu.VMEM((COLS, total), jnp.bfloat16),
+        ],
         compiler_params=params(),
         cost_estimate=cost(64),
         name="far_low",
-    )(far, low, low_w, t)
+    )(far, low_all, t)
 
 
 def pair_list(near, count, first, pairs, place):
@@ -471,29 +496,51 @@
     )(terms, hx)
 
 
-def high_kernel(scale, *refs):
-    *ups, t, part, out = refs
-    high_w = jnp.concatenate([u[:COLS, :] for u in ups], axis=1)
-    high_x = event_rows(jnp.concatenate([u[COLS:, :] for u in ups], axis=1))
+def high_kernel(scale, n_up, *refs):
+    sources, (t, part, out, ups, high_w, high_x, sems) = refs[:n_up], refs[n_up:]
+    each = COLS + FEAT
+
+    @pl.when(pl.program_id(0) == 0)
+    def _():
+        sizes = [u.shape[0] for u in sources]
+        starts = [sum(sizes[:i]) for i in range(n_up)]
+        moves = start_copies(
+            [(u, ups.at[pl.ds(at, n), :]) for u, at, n in zip(sources, starts, sizes)], sems
+        )
+        for m in moves:
+            m.wait()
+        others = range(0, ups.shape[0], each)
+        high_w[...] = jnp.concatenate([ups[i : i + COLS, :] for i in others], axis=1)
+        xs = [ups[i + COLS : i + each, :] for i in others]
+        high_x[...] = event_rows(jnp.concatenate(xs, axis=1))
+
     many = out.shape[1] // LEAF
     ats = [slice(j * LEAF, (j + 1) * LEAF) for j in range(many)]
-    ks = [jnp.exp(dot(high_x, t[at, :], NT)).astype(jnp.bfloat16) for at in ats]
+    ks = [jnp.exp(dot(high_x[...], t[at, :], NT)).astype(jnp.bfloat16) for at in ats]
     for at, k in zip(ats, ks):
-        out[:, at] = (part[:, at] + dot(high_w, k) * scale).astype(jnp.bfloat16)
+        out[:, at] = (part[:, at] + dot(high_w[...], k) * scale).astype(jnp.bfloat16)
 
 
 def high_call(scale, ups, t, part):
     many = 4
-    return pl.pallas_call(
-        lambda *refs: high_kernel(scale, *refs),
+    rows = sum(u.shape[0] for u in ups)
+    total = rows // (COLS + FEAT) * RANK
+    return pl.pallas_call(
+        lambda *refs: high_kernel(scale, len(ups), *refs),
         out_shape=jax.ShapeDtypeStruct(part.shape, jnp.bfloat16),
         grid=(LEAF_DEV // many,),
-        in_specs=[pl.BlockSpec(u.shape, lambda i: (0, 0)) for u in ups]
+        in_specs=[ANY] * len(ups)
         + [
             pl.BlockSpec((many * LEAF, LANES), lambda i: (i, 0)),
             pl.BlockSpec((COLS, many * LEAF), lambda i: (0, i)),
         ],
         out_specs=pl.BlockSpec((COLS, many * LEAF), lambda i: (0, i)),
+        scratch_shapes=[
+            pltpu.VMEM((rows, RANK), jnp.bfloat16),
+            pltpu.VMEM((COLS, total), jnp.bfloat16),
+            pltpu.VMEM((total, LANES), jnp.bfloat16),
+            pltpu.SemaphoreType.DMA((len(ups),)),
+        ],
         compiler_params=params(),
         cost_estimate=cost(12),
         name="high_out",
@@ -526,9 +573,10 @@
     right = lax.ppermute(lo, both, [(i + 1, i) for i in range(devices - 1)])
     acc = near_own_call(near_list, near_count, first, lo, hi, w, t)
 
-    term, hx, low, low_w = term_call(skel_high, after(low_all, acc), lo, hi, w)
+    low_all = after(low_all, acc)
+    term, hx = term_call(skel_high, low_all, lo, hi, w)
     terms = lax.all_gather(term, "inner", axis=0, tiled=True)
-    far = low_call(far_list, after(low, term), low_w, t)
+    far = low_call(far_list, after(low_all, term), t)
     near_scale = 16.0 / (LEAF * NEAR) ** 0.5
     low_scale = 128.0 / (far_count * RANK) ** 0.5
     scales = (near_scale, low_scale)
@@ -536,7 +584,11 @@
 
     scale = 1.0 / (ev_dev * group_devs) ** 0.5
     upper = upper_call(scale, (far_count / group_count) ** 0.5, after(terms, part), hx)
-    ups = [swap(upper, "outer", m) for m in range(1, group_count)]
+    ups, mask = [], 1
+    while mask < group_count:
+        ups.append(swap(upper, "outer", mask))
+        upper = jnp.concatenate([upper, ups[-1]], axis=0)
+        mask *= 2
     return high_call(low_scale, ups, t, part)
 
 

time: 137 us -> 143 us (1.044); the launches traced: 135 us -> 143 us
  waiting for transfers between devices: 21.5 us -> 27.9 us
  starting transfers between devices: 7.39 us -> 9.22 us
    pallas_call x1, Pallas kernels: 16 us -> 12.9 us  [near_side_call(): pl.pallas_call(lambda *refs: near_side_kernel(scales, *refs), out_shape=j...]
    ppermute x3 -> x2, waiting for transfers between devices: 4.63 us -> 7.62 us  [swap(): return lax.ppermute(x, axis, [(i, i ^ mask) for i in range(count)])]
    all_gather x1, waiting for transfers between devices: 6.19 us -> 8.41 us  [per_device(): terms = lax.all_gather(term, 'inner', axis=0, tiled=True)]
    pallas_call x1, Pallas kernels: 22.6 us -> 24.5 us  [near_own_call(): pl.pallas_call(near_own_kernel, out_shape=jax.ShapeDtypeStruct((LEAF_DEV...]
    ppermute x3 -> x2, starting transfers between devices: 4.7 us -> 6.52 us  [swap(): return lax.ppermute(x, axis, [(i, i ^ mask) for i in range(count)])]
  transfers between devices with their start and end apart: 7 -> 6, of which waited for: 4 -> 4; matrix products, arithmetic and copies ran while one was open for 0% -> 0% of each run, Pallas kernels for 57% -> 53%
where the time goes in v3:
time: 143 us
  Pallas kernels  89.1 us (62%)
  waiting for transfers between devices  27.9 us (20%)
  between operations  13.5 us (9%)
  starting transfers between devices  9.22 us (6%)
  local copies, waits for them, and re-layouts  2.58 us (2%)
    pallas_call x1, Pallas kernels, near_own_call(): pl.pallas_call(near_own_kernel, out_shape=jax.ShapeDtypeStruct((LEAF_DEV...  24.5 us
    pallas_call x1, Pallas kernels, low_call(): pl.pallas_call(low_kernel, out_shape=jax.ShapeDtypeStruct((LEAF_DEV, COLS...  19 us
    pallas_call x1, Pallas kernels, tree_call(): pl.pallas_call(tree_kernel, out_shape=tuple((jax.ShapeDtypeStruct(s, jnp....  14.5 us
    pallas_call x1, Pallas kernels, near_side_call(): pl.pallas_call(lambda *refs: near_side_kernel(scales, *refs), out_shape=j...  12.9 us
    all_gather x1, waiting for transfers between devices, per_device(): low_all = lax.all_gather(own, 'inner', axis=0, tiled=True)  11.8 us
    all_gather x1, waiting for transfers between devices, per_device(): terms = lax.all_gather(term, 'inner', axis=0, tiled=True)  8.41 us
    ppermute x2, waiting for transfers between devices, swap(): return lax.ppermute(x, axis, [(i, i ^ mask) for i in range(count)])  7.62 us
    pallas_call x1, Pallas kernels, high_call(): pl.pallas_call(lambda *refs: high_kernel(scale, len(ups), *refs), out_sha...  6.73 us
  transfers between devices with their start and end apart: 6, of which 4 were waited for; matrix products, arithmetic and copies ran while one was open for 0% of the time, Pallas kernels for 53%

profile of v3, /device:TPU:0, one launch (start us, length us, event | category | flops | bytes accessed | tf_op | source)
XLA Modules:
  0.0 143.0 jit_solution(17500564113535752497)
XLA Ops:
  6.5 0.0 all-gather.3.cloned.1.call-start
  6.5 4.8 %own_skeleton.1 = bf16[128,128]{1,0:T(8,128)(2,1)} custom-call(s32[1,8192]{1,0:T(1,128)} %perm_hbm.2, s32[1,128]{1,0:T(1,128)} %skel_hbm.1, bf16[16,8192]{1,0:T(8,128)(2,1)} %events_hbm.3, bf16[64,8192]{1,0:T(8,128)(2,1)} %coeffs_hbm.3), custom_call_target="tpu_custom_call" | custom-call | flops 805306368 | bytes 4194304 | tf_op jit(solution)/shard_map/own_skeleton/pallas_call | solution.py:205
  11.3 0.0 all-gather.3.cloned.1.call-update
  11.4 0.0 all-gather.5.cloned.1.call-start
  11.4 14.5 %tree_rows.1 = (bf16[4096,128]{1,0:T(8,128)(2,1)}, bf16[4096,128]{1,0:T(8,128)(2,1)}, bf16[64,8192]{1,0:T(8,128)(2,1)}, bf16[8192,128]{1,0:T(8,128)(2,1)}) custom-call(s32[1,8192]{1,0:T(1,128)} %perm_hbm.2, bf16[16,8192]{1,0:T(8,128)(2,1)} %events_hbm.3, bf16[64,8192]{1,0:T(8,128)(2,1)} %coeffs_hbm.3), custom_call_target="tpu_custom_call" | custom-call | flops 8053063680 | bytes 4194304 | tf_op jit(solution)/shard_map/tree_rows/pallas_call | solution.py:229
  25.9 1.4 collective-permute-start
  27.3 1.3 collective-permute-start.1
  28.6 24.5 %near_own.1.refs_6_ = f32[17,64,512]{2,1,0:T(8,128)} custom-call(s32[16,32]{1,0:T(8,128)} %refs_0_.1, s32[16]{0:T(128)} %refs_1_.1, s32[1]{0:T(128)} %bitcast.first.refs_2_, bf16[4096,128]{1,0:T(8,128)(2,1)} %get-tuple-element.16.lo.lo_hbm, bf16[4096,128]{1,0:T(8,128)(2,1)} %get-tuple-element.17.hi.hi_hbm, bf16[64,8192]{1,0:T(8,128)(2,1)} %get-tuple-element.18.w_hbm, ...), custom_call_target="tpu_custom_call" | custom-call | flops 12079595520 | bytes 4194304 | tf_op jit(solution)/shard_map/near_own/pallas_call | solution.py:404
  53.1 11.8 %all-gather.3.cloned.1.call-done.low_all = bf16[4096,128]{1,0:T(8,128)(2,1)} async-done(((bf16[128,128]{1,0:T(8,128)(2,1)}), bf16[4096,128]{1,0:T(8,128)(2,1)}) %all-gather.3.cloned.1.call-update) | async-done | bytes 1048592 | tf_op jit(solution)/shard_map/all_gather | solution.py:569
  64.9 4.7 %high_term.1 = (f32[64,128]{1,0:T(8,128)}, bf16[16,128]{1,0:T(8,128)(2,1)}) custom-call(s32[1,128]{1,0:T(1,128)} %picks.1, bf16[4096,128]{1,0:T(8,128)(2,1)} %all-gather.3.cloned.1.call-done.low_all, bf16[4096,128]{1,0:T(8,128)(2,1)} %get-tuple-element.16.lo.lo_hbm, bf16[4096,128]{1,0:T(8,128)(2,1)} %get-tuple-element.17.hi.hi_hbm, ...), custom_call_target="tpu_custom_call" | custom-call | flops 805306368 | bytes 4194304 | tf_op jit(solution)/shard_map/high_term/pallas_call | solution.py:271
  69.7 0.0 all-gather.5.cloned.1.call-update
  69.7 19.0 %far_low.1.refs_7_ = f32[16,64,512]{2,1,0:T(8,128)} custom-call(s32[16,16]{1,0:T(8,128)} %far.1, bf16[4096,128]{1,0:T(8,128)(2,1)} %all-gather.3.cloned.1.call-done.low_all, bf16[8192,128]{1,0:T(8,128)(2,1)} %get-tuple-element.19.t_hbm.t.refs_5_.refs_2_), custom_call_target="tpu_custom_call" | custom-call | flops 12884901888 | bytes 4194304 | tf_op jit(solution)/shard_map/far_low/pallas_call | solution.py:325
  88.7 0.0 collective-permute-done.refs_3_
  88.7 0.0 copy-start.1
  88.7 0.0 collective-permute-done.1.refs_4_
  88.7 1.0 copy-done.1
  89.7 0.0 copy-start.2
  89.7 1.0 copy-done.2
  90.7 12.9 %near_sides.1.refs_3_ = f32[64,8192]{1,0:T(8,128)} custom-call(s32[16,32]{1,0:T(8,128)} %refs_0_.1, s32[16]{0:T(128)} %refs_1_.1, s32[1]{0:T(128)} %bitcast.first.refs_2_, bf16[4096,128]{1,0:T(8,128)(2,1)} %copy-done.1, bf16[4096,128]{1,0:T(8,128)(2,1)} %copy-done.2, bf16[8192,128]{1,0:T(8,128)(2,1)} %get-tuple-element.19.t_hbm.t.refs_5_.refs_2_, ...), custom_call_target="tpu_custom_call" | custom-call | flops 10066329600 | bytes 4194304 | tf_op jit(solution)/shard_map/near_sides/pallas_call | solution.py:460
  103.6 8.4 %all-gather.5.cloned.1.call-done.refs_0_ = f32[2048,128]{1,0:T(8,128)} async-done(((f32[64,128]{1,0:T(8,128)}), f32[2048,128]{1,0:T(8,128)}) %all-gather.5.cloned.1.call-update) | async-done | bytes 1048592 | tf_op jit(solution)/shard_map/all_gather | solution.py:578
  112.0 1.9 %high_sum.1 = bf16[80,128]{1,0:T(8,128)(2,1)} custom-call(f32[2048,128]{1,0:T(8,128)} %all-gather.5.cloned.1.call-done.refs_0_, bf16[16,128]{1,0:T(8,128)(2,1)} %get-tuple-element.24.refs_1_), custom_call_target="tpu_custom_call" | custom-call | tf_op jit(solution)/shard_map/high_sum/pallas_call | solution.py:489
  113.9 6.5 %collective-permute-start.2 = (bf16[80,128]{1,0:T(8,128)(2,1)}, bf16[80,128]{1,0:T(8,128)(2,1)S(1)}, u32[]{:S(2)}, u32[]{:S(2)}) collective-permute-start(bf16[80,128]{1,0:T(8,128)(2,1)} %high_sum.1), channel_id=1, source_target_pairs={{0,32},{32,0},{64,96},{96,64},{1,33},{33,1},{65,97},{97,65},{2,34}... | collective-permute-start | bytes 61448 | tf_op jit(solution)/shard_map/ppermute | solution.py:552
  120.4 2.1 %collective-permute-done.2.refs_0_ = bf16[80,128]{1,0:T(8,128)(2,1)S(1)} collective-permute-done((bf16[80,128]{1,0:T(8,128)(2,1)}, bf16[80,128]{1,0:T(8,128)(2,1)S(1)}, u32[]{:S(2)}, u32[]{:S(2)}) %collective-permute-start.2) | collective-permute-done | bytes 20512 | tf_op jit(solution)/shard_map/ppermute | solution.py:552
  122.5 0.0 copy-start
  122.5 0.7 pad_maximum_fusion
  123.3 0.0 collective-permute-start.3
  123.3 5.5 %collective-permute-done.3.refs_1_ = bf16[160,128]{1,0:T(8,128)(2,1)S(1)} collective-permute-done((bf16[160,128]{1,0:T(8,128)(2,1)S(1)}, bf16[160,128]{1,0:T(8,128)(2,1)S(1)}, u32[]{:S(2)}, u32[]{:S(2)}) %collective-permute-start.3) | collective-permute-done | bytes 40992 | tf_op jit(solution)/shard_map/ppermute | solution.py:552
  128.8 0.0 copy-done
  128.8 0.0 copy-start.3
  128.8 0.6 copy-done.3
  129.4 6.7 %high_out.1 = bf16[64,8192]{1,0:T(8,128)(2,1)} custom-call(bf16[80,128]{1,0:T(8,128)(2,1)} %copy-done, bf16[160,128]{1,0:T(8,128)(2,1)} %copy-done.3, bf16[8192,128]{1,0:T(8,128)(2,1)} %get-tuple-element.19.t_hbm.t.refs_5_.refs_2_, f32[64,8192]{1,0:T(8,128)} %near_sides.1.refs_3_), custom_call_target="tpu_custom_call" | custom-call | flops 2415919104 | bytes 4194304 | tf_op jit(solution)/shard_map/high_out/pallas_call | solution.py:528
Async XLA Ops:
  6.5 58.4 %all-gather.3.cloned.1.call-start = ((), (), s32[]{:S(2)}) async-start(), calls=%async_computation | async-start | bytes 1081344 | tf_op jit(solution)/shard_map/all_gather | solution.py:569
  11.4 100.6 %all-gather.5.cloned.1.call-start = ((), (), s32[]{:S(2)}) async-start(), calls=%async_computation.1 | async-start | bytes 1081344 | tf_op jit(solution)/shard_map/all_gather | solution.py:578
  25.9 62.8 %collective-permute-start = (bf16[4096,128]{1,0:T(8,128)(2,1)}, bf16[4096,128]{1,0:T(8,128)(2,1)S(1)}, u32[]{:S(2)}, u32[]{:S(2)}) collective-permute-start(bf16[4096,128]{1,0:T(8,128)(2,1)} %get-tuple-element.17.hi.hi_hbm), channel_id=1, source_target_pairs={{0,1},{1,2},{2,3},{3,4},{4,5},{5,6},{6,7},{7,8},{8,9},{9,10},{10,1... | collective-permute-start | bytes 3145736 | tf_op jit(solution)/shard_map/ppermute | solution.py:572
  27.3 61.4 %collective-permute-start.1 = (bf16[4096,128]{1,0:T(8,128)(2,1)}, bf16[4096,128]{1,0:T(8,128)(2,1)S(1)}, u32[]{:S(2)}, u32[]{:S(2)}) collective-permute-start(bf16[4096,128]{1,0:T(8,128)(2,1)} %get-tuple-element.16.lo.lo_hbm), channel_id=1, source_target_pairs={{1,0},{2,1},{3,2},{4,3},{5,4},{6,5},{7,6},{8,7},{9,8},{10,9},{11,1... | collective-permute-start | bytes 3145736 | tf_op jit(solution)/shard_map/ppermute | solution.py:573
  88.7 1.0 copy-start.1
  89.7 1.0 copy-start.2
  113.9 8.6 %collective-permute-start.2 = (bf16[80,128]{1,0:T(8,128)(2,1)}, bf16[80,128]{1,0:T(8,128)(2,1)S(1)}, u32[]{:S(2)}, u32[]{:S(2)}) collective-permute-start(bf16[80,128]{1,0:T(8,128)(2,1)} %high_sum.1), channel_id=1, source_target_pairs={{0,32},{32,0},{64,96},{96,64},{1,33},{33,1},{65,97},{97,65},{2,34}... | collective-permute-start | bytes 61448 | tf_op jit(solution)/shard_map/ppermute | solution.py:552
  122.5 6.3 %copy-start = (bf16[80,128]{1,0:T(8,128)(2,1)}, bf16[80,128]{1,0:T(8,128)(2,1)S(1)}, u32[]{:S(2)}) copy-start(bf16[80,128]{1,0:T(8,128)(2,1)S(1)} %collective-permute-done.2.refs_0_) | copy-start | bytes 61444
  123.3 5.5 %collective-permute-start.3 = (bf16[160,128]{1,0:T(8,128)(2,1)S(1)}, bf16[160,128]{1,0:T(8,128)(2,1)S(1)}, u32[]{:S(2)}, u32[]{:S(2)}) collective-permute-start(bf16[160,128]{1,0:T(8,128)(2,1)S(1)} %pad_maximum_fusion), channel_id=1, source_target_pairs={{0,64},{32,96},{64,0},{96,32},{1,65},{33,97},{65,1},{97,33},{2,66}... | collective-permute-start | bytes 122888 | tf_op jit(solution)/shard_map/ppermute | solution.py:552
  128.8 0.6 copy-start.3
Sparse Core Ops, SparseCore 0:
  11.5 53.3 all-gather.2
  69.8 42.1 all-gather.4

commit v4 on v3

--- a/solution.py
+++ b/solution.py
@@ -41,16 +41,6 @@
     return dot(rows, target_map()).astype(jnp.bfloat16)
 
 
-def weight_map():
-    k = lax.broadcasted_iota(jnp.int32, (COLS, LANES), 0)
-    m = lax.broadcasted_iota(jnp.int32, (COLS, LANES), 1)
-    return jnp.where(k == m, 1.0, 0.0).astype(jnp.bfloat16)
-
-
-def weights(rows):
-    return dot(weight_map(), rows, NT).astype(jnp.bfloat16)
-
-
 def block(i, size):
     return pl.ds(pl.multiple_of(i * size, size), size)
 
@@ -107,6 +97,13 @@
     return moves
 
 
+def weight_copies(wx_lo, wx_hi, w):
+    half = wx_lo.shape[1]
+    return [
+        (wx.at[pl.ds(0, COLS), :], w.at[:, pl.ds(i * half, half)]) for i, wx in enumerate((wx_lo, wx_hi))
+    ]
+
+
 def own_kernel(
     perm_hbm, skel_hbm, events_hbm, coeffs_hbm, own_out,
     table, rows, spick, perm, skel, events, coeffs, sems,
@@ -136,8 +133,8 @@
 
 
 def tree_kernel(
-    perm_hbm, events_hbm, coeffs_hbm, lo_hbm, hi_hbm, w_hbm, t_hbm,
-    lo_out, hi_out, w_out, t_out, table, picked, perm, events, coeffs, sems,
+    perm_hbm, events_hbm, coeffs_hbm, lo_hbm, hi_hbm, wx_lo_hbm, wx_hi_hbm, t_hbm,
+    lo_out, hi_out, wx_lo, wx_hi, t_out, table, picked, perm, events, coeffs, sems,
 ):
     moves = start_copies(
         quarters(events_hbm, events) + quarters(coeffs_hbm, coeffs) + [(perm_hbm, perm)], sems
@@ -150,7 +147,7 @@
     moves[-1].wait()
     step = 64
 
-    def gather(rows_out, base, c, _):
+    def gather(rows_out, wx_out, base, c, _):
         def some(b, _):
             for v in range(0, step, 8):
                 e = (base + c) * LEAF + b * step + v
@@ -160,25 +157,25 @@
             return 0
 
         lax.fori_loop(0, LEAF // step, some, 0)
-        at = block(base + c, LEAF)
         r = picked[...]
         rb = r.astype(jnp.bfloat16)
         rows_out[block(c, LEAF), :] = rb
-        w_out[:, at] = r.T[:COLS].astype(jnp.bfloat16)
-        t_out[at, :] = targets(rb)
+        wx_out[:, block(c, LEAF)] = r.T[:N0].astype(jnp.bfloat16)
+        t_out[block(base + c, LEAF), :] = targets(rb)
         return 0
 
     half = events.shape[1] // LEAF // 2
-    lax.fori_loop(0, half, functools.partial(gather, lo_out, 0), 0)
+    lax.fori_loop(0, half, functools.partial(gather, lo_out, wx_lo, 0), 0)
     outs = [
         pltpu.make_async_copy(src, dst, sems.at[2 * QUARTERS + 1 + i])
         for i, (src, dst) in enumerate(
-            [(lo_out, lo_hbm), (hi_out, hi_hbm), (w_out, w_hbm), (t_out, t_hbm)]
+            [(lo_out, lo_hbm), (wx_lo, wx_lo_hbm), (hi_out, hi_hbm), (wx_hi, wx_hi_hbm), (t_out, t_hbm)]
         )
     ]
-    outs[0].start()
-    lax.fori_loop(0, half, functools.partial(gather, hi_out, half), 0)
-    for m in outs[1:]:
+    for m in outs[:2]:
+        m.start()
+    lax.fori_loop(0, half, functools.partial(gather, hi_out, wx_hi, half), 0)
+    for m in outs[2:]:
         m.start()
     for m in outs:
         m.wait()
@@ -225,12 +222,12 @@
 
 def tree_call(perm, events, coeffs):
     n = events.shape[1]
-    shapes = ((n // 2, LANES), (n // 2, LANES), (COLS, n), (n, LANES))
+    shapes = ((n // 2, LANES), (n // 2, LANES), (N0, n // 2), (N0, n // 2), (n, LANES))
     return pl.pallas_call(
         tree_kernel,
         out_shape=tuple(jax.ShapeDtypeStruct(s, jnp.bfloat16) for s in shapes),
         in_specs=[ANY] * 3,
-        out_specs=(ANY,) * 4,
+        out_specs=(ANY,) * 5,
         scratch_shapes=[pltpu.VMEM(s, jnp.bfloat16) for s in shapes]
         + [
             pltpu.VMEM((n, LANES), jnp.float32),
@@ -238,7 +235,7 @@
             pltpu.SMEM(perm.shape, jnp.int32),
             pltpu.VMEM(events.shape, jnp.bfloat16),
             pltpu.VMEM(coeffs.shape, jnp.bfloat16),
-            pltpu.SemaphoreType.DMA((2 * QUARTERS + 5,)),
+            pltpu.SemaphoreType.DMA((2 * QUARTERS + 6,)),
         ],
         compiler_params=params(),
         cost_estimate=cost(40),
@@ -251,8 +248,8 @@
     return jnp.concatenate([none] + features(xb), axis=0).T
 
 
-def term_kernel(picks, low_all, lo_hbm, hi_hbm, w_hbm, term_out, hx_out, low_x, lo, hi, w, sems):
-    moves = start_copies([(lo_hbm, lo), (hi_hbm, hi), (w_hbm, w)], sems)
+def term_kernel(picks, low_all, lo_hbm, hi_hbm, wx_lo, wx_hi, term_out, hx_out, low_x, lo, hi, w, sems):
+    moves = start_copies([(lo_hbm, lo), (hi_hbm, hi)] + weight_copies(wx_lo, wx_hi, w), sems)
     nodes = low_all.shape[0] // LANES
     for b in range(nodes):
         x = low_all[b * LANES + COLS : b * LANES + COLS + FEAT, :]
@@ -266,7 +263,7 @@
     term_out[...] = halves_dot(lo, hi, w, ts)
 
 
-def term_call(picks, low_all, lo, hi, w):
+def term_call(picks, low_all, lo, hi, wx_lo, wx_hi):
     total = low_all.shape[0] // LANES * RANK
     return pl.pallas_call(
         term_kernel,
@@ -274,19 +271,19 @@
             jax.ShapeDtypeStruct((COLS, RANK), jnp.float32),
             jax.ShapeDtypeStruct((FEAT, RANK), jnp.bfloat16),
         ),
-        in_specs=[VMEM] * 2 + [ANY] * 3,
+        in_specs=[VMEM] * 2 + [ANY] * 4,
         out_specs=(VMEM,) * 2,
         scratch_shapes=[
             pltpu.VMEM((FEAT, total), jnp.bfloat16),
             pltpu.VMEM(lo.shape, jnp.bfloat16),
             pltpu.VMEM(hi.shape, jnp.bfloat16),
-            pltpu.VMEM(w.shape, jnp.bfloat16),
-            pltpu.SemaphoreType.DMA((3,)),
+            pltpu.VMEM((COLS, 2 * wx_lo.shape[1]), jnp.bfloat16),
+            pltpu.SemaphoreType.DMA((4,)),
         ],
         compiler_params=params(),
         cost_estimate=cost(4),
         name="high_term",
-    )(picks, low_all, lo, hi, w)
+    )(picks, low_all, lo, hi, wx_lo, wx_hi)
 
 
 def low_kernel(far, low_all, t, part, low, low_w):
@@ -382,15 +379,15 @@
     lax.fori_loop(0, (n % 8 + 3) // 4, four, 0)
 
 
-def near_own_kernel(near, count, first, lo, hi, w_hbm, t_hbm, acc, rows, w, t, pairs, sems):
+def near_own_kernel(near, count, first, lo, hi, wx_lo, wx_hi, t_hbm, acc, rows, w, t, pairs, sems):
     half = lo.shape[0]
     moves = start_copies(
         [
             (lo, rows.at[pl.ds(0, half), :]),
             (hi, rows.at[pl.ds(half, half), :]),
-            (w_hbm, w),
             (t_hbm, t),
-        ],
+        ]
+        + weight_copies(wx_lo, wx_hi, w),
         sems,
     )
     n = pair_list(near, count, first, pairs, lambda at: (at, (at >= 0) & (at < LEAF_DEV)))
@@ -400,38 +397,39 @@
     pair_sums(n, pairs, rows, w, t, acc)
 
 
-def near_own_call(near, count, first, lo, hi, w, t):
+def near_own_call(near, count, first, lo, hi, wx_lo, wx_hi, t):
     return pl.pallas_call(
         near_own_kernel,
         out_shape=jax.ShapeDtypeStruct((LEAF_DEV + 1, COLS, LEAF), jnp.float32),
-        in_specs=[SMEM] * 3 + [ANY] * 4,
+        in_specs=[SMEM] * 3 + [ANY] * 5,
         out_specs=VMEM,
         scratch_shapes=[
             pltpu.VMEM(t.shape, jnp.bfloat16),
-            pltpu.VMEM(w.shape, jnp.bfloat16),
+            pltpu.VMEM((COLS, t.shape[0]), jnp.bfloat16),
             pltpu.VMEM(t.shape, jnp.bfloat16),
             pltpu.SMEM((LEAF_DEV * NEAR + 8,), jnp.int32),
-            pltpu.SemaphoreType.DMA((4,)),
+            pltpu.SemaphoreType.DMA((5,)),
         ],
         compiler_params=params(),
         cost_estimate=cost(60),
         name="near_own",
-    )(near, count, first, lo, hi, w, t)
+    )(near, count, first, lo, hi, wx_lo, wx_hi, t)
 
 
 def near_side_kernel(
-    scales, near, count, first, left, right, t_hbm, acc_hbm, low_hbm, out, rows, w, t, acc, low, pairs, sems
+    scales, near, count, first, left, right, t_hbm, acc_hbm, low_hbm, out, rows, w, x, t, acc, low, pairs, sems
 ):
     near_scale, low_scale = scales
     side = REACH * LEAF
     moves = start_copies(
         [
-            (left, rows.at[pl.ds(0, side), :]),
-            (right, rows.at[pl.ds(side, side), :]),
+            (left.at[pl.ds(COLS, FEAT), :], x.at[:, pl.ds(0, side)]),
+            (right.at[pl.ds(COLS, FEAT), :], x.at[:, pl.ds(side, side)]),
             (t_hbm, t),
             (acc_hbm, acc),
             (low_hbm, low),
-        ],
+        ]
+        + weight_copies(left, right, w),
         sems,
     )
     n = pair_list(
@@ -441,12 +439,12 @@
     moves[0].wait()
     moves[1].wait()
 
-    def flip(b, _):
-        for at in (block(b, LEAF), block(b + REACH, LEAF)):
-            w[:, at] = weights(rows[at, :])
+    def build(b, _):
+        at = block(b, LEAF)
+        rows[at, :] = event_rows(x[:, at])
         return 0
 
-    lax.fori_loop(0, REACH, flip, 0)
+    lax.fori_loop(0, 2 * REACH, build, 0)
     for m in moves[2:]:
         m.wait()
     pair_sums(n, pairs, rows, w, t, acc)
@@ -465,11 +463,12 @@
         scratch_shapes=[
             pltpu.VMEM((n, LANES), jnp.bfloat16),
             pltpu.VMEM((COLS, n), jnp.bfloat16),
+            pltpu.VMEM((FEAT, n), jnp.bfloat16),
             pltpu.VMEM(t.shape, jnp.bfloat16),
             pltpu.VMEM(acc.shape, jnp.float32),
             pltpu.VMEM(low.shape, jnp.float32),
             pltpu.SMEM((LEAF_DEV * NEAR + 8,), jnp.int32),
-            pltpu.SemaphoreType.DMA((5,)),
+            pltpu.SemaphoreType.DMA((7,)),
         ],
         compiler_params=params(),
         cost_estimate=cost(50),
@@ -496,51 +495,29 @@
     )(terms, hx)
 
 
-def high_kernel(scale, n_up, *refs):
-    sources, (t, part, out, ups, high_w, high_x, sems) = refs[:n_up], refs[n_up:]
-    each = COLS + FEAT
-
-    @pl.when(pl.program_id(0) == 0)
-    def _():
-        sizes = [u.shape[0] for u in sources]
-        starts = [sum(sizes[:i]) for i in range(n_up)]
-        moves = start_copies(
-            [(u, ups.at[pl.ds(at, n), :]) for u, at, n in zip(sources, starts, sizes)], sems
-        )
-        for m in moves:
-            m.wait()
-        others = range(0, ups.shape[0], each)
-        high_w[...] = jnp.concatenate([ups[i : i + COLS, :] for i in others], axis=1)
-        xs = [ups[i + COLS : i + each, :] for i in others]
-        high_x[...] = event_rows(jnp.concatenate(xs, axis=1))
-
+def high_kernel(scale, *refs):
+    *ups, t, part, out = refs
+    high_w = jnp.concatenate([u[:COLS, :] for u in ups], axis=1)
+    high_x = event_rows(jnp.concatenate([u[COLS:, :] for u in ups], axis=1))
     many = out.shape[1] // LEAF
     ats = [slice(j * LEAF, (j + 1) * LEAF) for j in range(many)]
-    ks = [jnp.exp(dot(high_x[...], t[at, :], NT)).astype(jnp.bfloat16) for at in ats]
+    ks = [jnp.exp(dot(high_x, t[at, :], NT)).astype(jnp.bfloat16) for at in ats]
     for at, k in zip(ats, ks):
-        out[:, at] = (part[:, at] + dot(high_w[...], k) * scale).astype(jnp.bfloat16)
+        out[:, at] = (part[:, at] + dot(high_w, k) * scale).astype(jnp.bfloat16)
 
 
 def high_call(scale, ups, t, part):
     many = 4
-    rows = sum(u.shape[0] for u in ups)
-    total = rows // (COLS + FEAT) * RANK
-    return pl.pallas_call(
-        lambda *refs: high_kernel(scale, len(ups), *refs),
+    return pl.pallas_call(
+        lambda *refs: high_kernel(scale, *refs),
         out_shape=jax.ShapeDtypeStruct(part.shape, jnp.bfloat16),
         grid=(LEAF_DEV // many,),
-        in_specs=[ANY] * len(ups)
+        in_specs=[pl.BlockSpec(u.shape, lambda i: (0, 0)) for u in ups]
         + [
             pl.BlockSpec((many * LEAF, LANES), lambda i: (i, 0)),
             pl.BlockSpec((COLS, many * LEAF), lambda i: (0, i)),
         ],
         out_specs=pl.BlockSpec((COLS, many * LEAF), lambda i: (0, i)),
-        scratch_shapes=[
-            pltpu.VMEM((rows, RANK), jnp.bfloat16),
-            pltpu.VMEM((COLS, total), jnp.bfloat16),
-            pltpu.VMEM((total, LANES), jnp.bfloat16),
-            pltpu.SemaphoreType.DMA((len(ups),)),
-        ],
         compiler_params=params(),
         cost_estimate=cost(12),
         name="high_out",
@@ -567,14 +544,14 @@
     first = (device * LEAF_DEV).reshape(1)
     own = own_call(tree_perm, skel_low, events, coeffs)
     low_all = lax.all_gather(own, "inner", axis=0, tiled=True)
-    lo, hi, w, t = tree_call(after(tree_perm, own), events, coeffs)
+    lo, hi, wx_lo, wx_hi, t = tree_call(after(tree_perm, own), events, coeffs)
     both = ("outer", "inner")
-    left = lax.ppermute(hi, both, [(i, i + 1) for i in range(devices - 1)])
-    right = lax.ppermute(lo, both, [(i + 1, i) for i in range(devices - 1)])
-    acc = near_own_call(near_list, near_count, first, lo, hi, w, t)
+    left = lax.ppermute(wx_hi, both, [(i, i + 1) for i in range(devices - 1)])
+    right = lax.ppermute(wx_lo, both, [(i + 1, i) for i in range(devices - 1)])
+    acc = near_own_call(near_list, near_count, first, lo, hi, wx_lo, wx_hi, t)
 
     low_all = after(low_all, acc)
-    term, hx = term_call(skel_high, low_all, lo, hi, w)
+    term, hx = term_call(skel_high, low_all, lo, hi, wx_lo, wx_hi)
     terms = lax.all_gather(term, "inner", axis=0, tiled=True)
     far = low_call(far_list, after(low_all, term), t)
     near_scale = 16.0 / (LEAF * NEAR) ** 0.5
@@ -584,11 +561,7 @@
 
     scale = 1.0 / (ev_dev * group_devs) ** 0.5
     upper = upper_call(scale, (far_count / group_count) ** 0.5, after(terms, part), hx)
-    ups, mask = [], 1
-    while mask < group_count:
-        ups.append(swap(upper, "outer", mask))
-        upper = jnp.concatenate([upper, ups[-1]], axis=0)
-        mask *= 2
+    ups = [swap(upper, "outer", m) for m in range(1, group_count)]
     return high_call(low_scale, ups, t, part)
 
 

time: 143 us -> 135 us (0.944); the launches traced: 143 us -> 132 us
  Pallas kernels: 89.1 us -> 80 us
  starting transfers between devices: 9.22 us -> 7.76 us
    pallas_call x1, Pallas kernels: 24.5 us -> 17.5 us  [near_own_call(): pl.pallas_call(near_own_kernel, out_shape=jax.ShapeDtypeStruct((LEAF_DEV...]
    ppermute x2 -> x3, waiting for transfers between devices: 7.62 us -> 4.25 us  [swap(): return lax.ppermute(x, axis, [(i, i ^ mask) for i in range(count)])]
    all_gather x1, waiting for transfers between devices: 11.8 us -> 14.7 us  [per_device(): low_all = lax.all_gather(own, 'inner', axis=0, tiled=True)]
    ppermute x2 -> x3, starting transfers between devices: 6.52 us -> 5.1 us  [swap(): return lax.ppermute(x, axis, [(i, i ^ mask) for i in range(count)])]
  transfers between devices with their start and end apart: 6 -> 7, of which waited for: 4 -> 4; matrix products, arithmetic and copies ran while one was open for 0% -> 0% of each run, Pallas kernels for 53% -> 51%
where the time goes in v4:
time: 135 us; the launch traced here: 132 us
  Pallas kernels  80 us (59%)
  waiting for transfers between devices  28.8 us (21%)
  between operations  13.5 us (10%)
  starting transfers between devices  7.76 us (6%)
  local copies, waits for them, and re-layouts  2.29 us (2%)
    pallas_call x1, Pallas kernels, low_call(): pl.pallas_call(low_kernel, out_shape=jax.ShapeDtypeStruct((LEAF_DEV, COLS...  19 us
    pallas_call x1, Pallas kernels, near_own_call(): pl.pallas_call(near_own_kernel, out_shape=jax.ShapeDtypeStruct((LEAF_DEV...  17.5 us
    all_gather x1, waiting for transfers between devices, per_device(): low_all = lax.all_gather(own, 'inner', axis=0, tiled=True)  14.7 us
    pallas_call x1, Pallas kernels, tree_call(): pl.pallas_call(tree_kernel, out_shape=tuple((jax.ShapeDtypeStruct(s, jnp....  14.4 us
    pallas_call x1, Pallas kernels, near_side_call(): pl.pallas_call(lambda *refs: near_side_kernel(scales, *refs), out_shape=j...  11.8 us
    all_gather x1, waiting for transfers between devices, per_device(): terms = lax.all_gather(term, 'inner', axis=0, tiled=True)  9.84 us
    pallas_call x1, Pallas kernels, high_call(): pl.pallas_call(lambda *refs: high_kernel(scale, *refs), out_shape=jax.Sha...  5.86 us
    ppermute x3, starting transfers between devices, swap(): return lax.ppermute(x, axis, [(i, i ^ mask) for i in range(count)])  5.1 us
  transfers between devices with their start and end apart: 7, of which 4 were waited for; matrix products, arithmetic and copies ran while one was open for 0% of the time, Pallas kernels for 51%

profile of v4, /device:TPU:0, one launch (start us, length us, event | category | flops | bytes accessed | tf_op | source)
XLA Modules:
  0.0 132.3 jit_solution(12944377843092278611)
XLA Ops:
  6.5 0.0 all-gather.3.cloned.1.call-start
  6.5 4.8 %own_skeleton.1 = bf16[128,128]{1,0:T(8,128)(2,1)} custom-call(s32[1,8192]{1,0:T(1,128)} %perm_hbm.2, s32[1,128]{1,0:T(1,128)} %skel_hbm.1, bf16[16,8192]{1,0:T(8,128)(2,1)} %events_hbm.3, bf16[64,8192]{1,0:T(8,128)(2,1)} %coeffs_hbm.3), custom_call_target="tpu_custom_call" | custom-call | flops 805306368 | bytes 4194304 | tf_op jit(solution)/shard_map/own_skeleton/pallas_call | solution.py:202
  11.3 0.0 all-gather.3.cloned.1.call-update
  11.4 0.0 all-gather.5.cloned.1.call-start
  11.4 14.4 %tree_rows.1 = (bf16[4096,128]{1,0:T(8,128)(2,1)}, bf16[4096,128]{1,0:T(8,128)(2,1)}, bf16[80,4096]{1,0:T(8,128)(2,1)}, bf16[80,4096]{1,0:T(8,128)(2,1)}, bf16[8192,128]{1,0:T(8,128)(2,1)}) custom-call(s32[1,8192]{1,0:T(1,128)} %perm_hbm.2, bf16[16,8192]{1,0:T(8,128)(2,1)} %events_hbm.3, bf16[64,8192]{1,0:T(8,128)(2,1)} %coeffs_hbm.3), custom_call_target="tpu_custom_call" | custom-call | flops 8053063680 | bytes 4194304 | tf_op jit(solution)/shard_map/tree_rows/pallas_call | solution.py:226
  25.9 1.3 %collective-permute-start = (bf16[80,4096]{1,0:T(8,128)(2,1)}, bf16[80,4096]{1,0:T(8,128)(2,1)S(1)}, u32[]{:S(2)}, u32[]{:S(2)}) collective-permute-start(bf16[80,4096]{1,0:T(8,128)(2,1)} %get-tuple-element.20.wx_hi), channel_id=1, source_target_pairs={{0,1},{1,2},{2,3},{3,4},{4,5},{5,6},{6,7},{7,8},{8,9},{9,10},{10,1... | collective-permute-start | bytes 1966088 | tf_op jit(solution)/shard_map/ppermute | solution.py:549
  27.2 1.3 collective-permute-start.1
  28.5 17.5 %near_own.1.refs_6_ = f32[17,64,512]{2,1,0:T(8,128)} custom-call(s32[16,32]{1,0:T(8,128)} %refs_0_.1, s32[16]{0:T(128)} %refs_1_.1, s32[1]{0:T(128)} %bitcast.first.refs_2_, bf16[4096,128]{1,0:T(8,128)(2,1)} %get-tuple-element.17.lo.lo_hbm, bf16[4096,128]{1,0:T(8,128)(2,1)} %get-tuple-element.18.hi.hi_hbm, bf16[80,4096]{1,0:T(8,128)(2,1)} %get-tuple-element.19.wx_lo, ...), custom_call_target="tpu_custom_call" | custom-call | flops 12079595520 | bytes 4194304 | tf_op jit(solution)/shard_map/near_own/pallas_call | solution.py:401
  46.0 14.7 %all-gather.3.cloned.1.call-done.low_all = bf16[4096,128]{1,0:T(8,128)(2,1)} async-done(((bf16[128,128]{1,0:T(8,128)(2,1)}), bf16[4096,128]{1,0:T(8,128)(2,1)}) %all-gather.3.cloned.1.call-update) | async-done | bytes 1048592 | tf_op jit(solution)/shard_map/all_gather | solution.py:546
  60.7 4.7 %high_term.1 = (f32[64,128]{1,0:T(8,128)}, bf16[16,128]{1,0:T(8,128)(2,1)}) custom-call(s32[1,128]{1,0:T(1,128)} %picks.1, bf16[4096,128]{1,0:T(8,128)(2,1)} %all-gather.3.cloned.1.call-done.low_all, bf16[4096,128]{1,0:T(8,128)(2,1)} %get-tuple-element.17.lo.lo_hbm, bf16[4096,128]{1,0:T(8,128)(2,1)} %get-tuple-element.18.hi.hi_hbm, ...), custom_call_target="tpu_custom_call" | custom-call | flops 805306368 | bytes 4194304 | tf_op jit(solution)/shard_map/high_term/pallas_call | solution.py:268
  65.4 0.0 all-gather.5.cloned.1.call-update
  65.4 19.0 %far_low.1.refs_7_ = f32[16,64,512]{2,1,0:T(8,128)} custom-call(s32[16,16]{1,0:T(8,128)} %far.1, bf16[4096,128]{1,0:T(8,128)(2,1)} %all-gather.3.cloned.1.call-done.low_all, bf16[8192,128]{1,0:T(8,128)(2,1)} %get-tuple-element.21.t_hbm.t.refs_5_.refs_3_), custom_call_target="tpu_custom_call" | custom-call | flops 12884901888 | bytes 4194304 | tf_op jit(solution)/shard_map/far_low/pallas_call | solution.py:322
  84.4 0.0 collective-permute-done.refs_3_
  84.4 0.0 copy-start
  84.4 0.0 collective-permute-done.1.refs_4_
  84.4 0.8 copy-done
  85.3 0.0 copy-start.1
  85.3 0.9 copy-done.1
  86.1 11.8 %near_sides.1.refs_4_ = f32[64,8192]{1,0:T(8,128)} custom-call(s32[16,32]{1,0:T(8,128)} %refs_0_.1, s32[16]{0:T(128)} %refs_1_.1, s32[1]{0:T(128)} %bitcast.first.refs_2_, bf16[80,4096]{1,0:T(8,128)(2,1)} %copy-done, bf16[80,4096]{1,0:T(8,128)(2,1)} %copy-done.1, bf16[8192,128]{1,0:T(8,128)(2,1)} %get-tuple-element.21.t_hbm.t.refs_5_.refs_3_, ...), custom_call_target="tpu_custom_call" | custom-call | flops 10066329600 | bytes 4194304 | tf_op jit(solution)/shard_map/near_sides/pallas_call | solution.py:458
  97.9 9.8 %all-gather.5.cloned.1.call-done.refs_0_ = f32[2048,128]{1,0:T(8,128)} async-done(((f32[64,128]{1,0:T(8,128)}), f32[2048,128]{1,0:T(8,128)}) %all-gather.5.cloned.1.call-update) | async-done | bytes 1048592 | tf_op jit(solution)/shard_map/all_gather | solution.py:555
  107.8 1.9 %high_sum.1 = bf16[80,128]{1,0:T(8,128)(2,1)} custom-call(f32[2048,128]{1,0:T(8,128)} %all-gather.5.cloned.1.call-done.refs_0_, bf16[16,128]{1,0:T(8,128)(2,1)} %get-tuple-element.26.refs_1_), custom_call_target="tpu_custom_call" | custom-call | tf_op jit(solution)/shard_map/high_sum/pallas_call | solution.py:488
  109.7 2.4 %collective-permute-start.2 = (bf16[80,128]{1,0:T(8,128)(2,1)}, bf16[80,128]{1,0:T(8,128)(2,1)S(1)}, u32[]{:S(2)}, u32[]{:S(2)}) collective-permute-start(bf16[80,128]{1,0:T(8,128)(2,1)} %high_sum.1), channel_id=1, source_target_pairs={{0,32},{32,0},{64,96},{96,64},{1,33},{33,1},{65,97},{97,65},{2,34}... | collective-permute-start | bytes 61448 | tf_op jit(solution)/shard_map/ppermute | solution.py:529
  112.1 1.7 %collective-permute-start.3 = (bf16[80,128]{1,0:T(8,128)(2,1)}, bf16[80,128]{1,0:T(8,128)(2,1)S(1)}, u32[]{:S(2)}, u32[]{:S(2)}) collective-permute-start(bf16[80,128]{1,0:T(8,128)(2,1)} %high_sum.1), channel_id=1, source_target_pairs={{0,64},{32,96},{64,0},{96,32},{1,65},{33,97},{65,1},{97,33},{2,66}... | collective-permute-start | bytes 61448 | tf_op jit(solution)/shard_map/ppermute | solution.py:529
  113.8 0.9 collective-permute-start.4
  114.8 0.0 collective-permute-done.2.refs_0_
  114.8 0.0 copy-start.2
  114.8 2.8 %collective-permute-done.3.refs_1_ = bf16[80,128]{1,0:T(8,128)(2,1)S(1)} collective-permute-done((bf16[80,128]{1,0:T(8,128)(2,1)}, bf16[80,128]{1,0:T(8,128)(2,1)S(1)}, u32[]{:S(2)}, u32[]{:S(2)}) %collective-permute-start.3) | collective-permute-done | bytes 20512 | tf_op jit(solution)/shard_map/ppermute | solution.py:529
  117.6 1.4 %collective-permute-done.4.refs_2_ = bf16[80,128]{1,0:T(8,128)(2,1)S(1)} collective-permute-done((bf16[80,128]{1,0:T(8,128)(2,1)}, bf16[80,128]{1,0:T(8,128)(2,1)S(1)}, u32[]{:S(2)}, u32[]{:S(2)}) %collective-permute-start.4) | collective-permute-done | bytes 20512 | tf_op jit(solution)/shard_map/ppermute | solution.py:529
  119.0 0.0 copy-done.2
  119.0 0.0 copy-done.3
  119.1 0.6 copy-done.4
  119.6 5.9 %high_out.1 = bf16[64,8192]{1,0:T(8,128)(2,1)} custom-call(bf16[80,128]{1,0:T(8,128)(2,1)} %copy-done.2, bf16[80,128]{1,0:T(8,128)(2,1)} %copy-done.3, bf16[80,128]{1,0:T(8,128)(2,1)} %copy-done.4, bf16[8192,128]{1,0:T(8,128)(2,1)} %get-tuple-element.21.t_hbm.t.refs_5_.refs_3_, f32[64,8192]{1,0:T(8,128)} %near_sides.1.refs_4_), custom_call_target="tpu_custom_call" | custom-call | flops 2415919104 | bytes 4194304 | tf_op jit(solution)/shard_map/high_out/pallas_call | solution.py:511
  (2 shorter events, 0.0 us)
Async XLA Ops:
  6.5 54.1 %all-gather.3.cloned.1.call-start = ((), (), s32[]{:S(2)}) async-start(), calls=%async_computation | async-start | bytes 1081344 | tf_op jit(solution)/shard_map/all_gather | solution.py:546
  11.4 96.4 %all-gather.5.cloned.1.call-start = ((), (), s32[]{:S(2)}) async-start(), calls=%async_computation.1 | async-start | bytes 1081344 | tf_op jit(solution)/shard_map/all_gather | solution.py:555
  25.9 58.6 %collective-permute-start = (bf16[80,4096]{1,0:T(8,128)(2,1)}, bf16[80,4096]{1,0:T(8,128)(2,1)S(1)}, u32[]{:S(2)}, u32[]{:S(2)}) collective-permute-start(bf16[80,4096]{1,0:T(8,128)(2,1)} %get-tuple-element.20.wx_hi), channel_id=1, source_target_pairs={{0,1},{1,2},{2,3},{3,4},{4,5},{5,6},{6,7},{7,8},{8,9},{9,10},{10,1... | collective-permute-start | bytes 1966088 | tf_op jit(solution)/shard_map/ppermute | solution.py:549
  27.2 57.2 %collective-permute-start.1 = (bf16[80,4096]{1,0:T(8,128)(2,1)}, bf16[80,4096]{1,0:T(8,128)(2,1)S(1)}, u32[]{:S(2)}, u32[]{:S(2)}) collective-permute-start(bf16[80,4096]{1,0:T(8,128)(2,1)} %get-tuple-element.19.wx_lo), channel_id=1, source_target_pairs={{1,0},{2,1},{3,2},{4,3},{5,4},{6,5},{7,6},{8,7},{9,8},{10,9},{11,1... | collective-permute-start | bytes 1966088 | tf_op jit(solution)/shard_map/ppermute | solution.py:550
  84.4 0.8 copy-start
  85.3 0.9 copy-start.1
  109.7 5.1 %collective-permute-start.2 = (bf16[80,128]{1,0:T(8,128)(2,1)}, bf16[80,128]{1,0:T(8,128)(2,1)S(1)}, u32[]{:S(2)}, u32[]{:S(2)}) collective-permute-start(bf16[80,128]{1,0:T(8,128)(2,1)} %high_sum.1), channel_id=1, source_target_pairs={{0,32},{32,0},{64,96},{96,64},{1,33},{33,1},{65,97},{97,65},{2,34}... | collective-permute-start | bytes 61448 | tf_op jit(solution)/shard_map/ppermute | solution.py:529
  112.1 5.5 %collective-permute-start.3 = (bf16[80,128]{1,0:T(8,128)(2,1)}, bf16[80,128]{1,0:T(8,128)(2,1)S(1)}, u32[]{:S(2)}, u32[]{:S(2)}) collective-permute-start(bf16[80,128]{1,0:T(8,128)(2,1)} %high_sum.1), channel_id=1, source_target_pairs={{0,64},{32,96},{64,0},{96,32},{1,65},{33,97},{65,1},{97,33},{2,66}... | collective-permute-start | bytes 61448 | tf_op jit(solution)/shard_map/ppermute | solution.py:529
  113.8 5.2 %collective-permute-start.4 = (bf16[80,128]{1,0:T(8,128)(2,1)}, bf16[80,128]{1,0:T(8,128)(2,1)S(1)}, u32[]{:S(2)}, u32[]{:S(2)}) collective-permute-start(bf16[80,128]{1,0:T(8,128)(2,1)} %high_sum.1), channel_id=1, source_target_pairs={{0,96},{32,64},{64,32},{96,0},{1,97},{33,65},{65,33},{97,1},{2,98}... | collective-permute-start | bytes 61448 | tf_op jit(solution)/shard_map/ppermute | solution.py:529
  114.8 4.3 %copy-start.2 = (bf16[80,128]{1,0:T(8,128)(2,1)}, bf16[80,128]{1,0:T(8,128)(2,1)S(1)}, u32[]{:S(2)}) copy-start(bf16[80,128]{1,0:T(8,128)(2,1)S(1)} %collective-permute-done.2.refs_0_) | copy-start | bytes 61444
  117.6 1.4 %copy-start.3 = (bf16[80,128]{1,0:T(8,128)(2,1)}, bf16[80,128]{1,0:T(8,128)(2,1)S(1)}, u32[]{:S(2)}) copy-start(bf16[80,128]{1,0:T(8,128)(2,1)S(1)} %collective-permute-done.3.refs_1_) | copy-start | bytes 61444
  119.0 0.6 copy-start.4
Sparse Core Ops, SparseCore 0:
  11.5 49.1 all-gather.2
  65.5 42.1 all-gather.4

commit v5 on v4

--- a/solution.py
+++ b/solution.py
@@ -249,16 +249,21 @@
 
 
 def term_kernel(picks, low_all, lo_hbm, hi_hbm, wx_lo, wx_hi, term_out, hx_out, low_x, lo, hi, w, sems):
-    moves = start_copies([(lo_hbm, lo), (hi_hbm, hi)] + weight_copies(wx_lo, wx_hi, w), sems)
     nodes = low_all.shape[0] // LANES
-    for b in range(nodes):
-        x = low_all[b * LANES + COLS : b * LANES + COLS + FEAT, :]
-        low_x[:, b * RANK : (b + 1) * RANK] = x
+    features_of = [
+        (low_all.at[pl.ds(b * LANES + COLS, FEAT), :], low_x.at[:, pl.ds(b * RANK, RANK)])
+        for b in range(nodes)
+    ]
+    moves = start_copies(
+        features_of + [(lo_hbm, lo), (hi_hbm, hi)] + weight_copies(wx_lo, wx_hi, w), sems
+    )
+    for m in moves[:nodes]:
+        m.wait()
     hit = lax.broadcasted_iota(jnp.int32, (nodes * RANK, RANK), 0) == picks[...]
     hx = dot(low_x[...], jnp.where(hit, 1.0, 0.0).astype(jnp.bfloat16)).astype(jnp.bfloat16)
     hx_out[...] = hx
     ts = targets(event_rows(hx))
-    for m in moves:
+    for m in moves[nodes:]:
         m.wait()
     term_out[...] = halves_dot(lo, hi, w, ts)
 
@@ -271,14 +276,14 @@
             jax.ShapeDtypeStruct((COLS, RANK), jnp.float32),
             jax.ShapeDtypeStruct((FEAT, RANK), jnp.bfloat16),
         ),
-        in_specs=[VMEM] * 2 + [ANY] * 4,
+        in_specs=[VMEM] + [ANY] * 5,
         out_specs=(VMEM,) * 2,
         scratch_shapes=[
             pltpu.VMEM((FEAT, total), jnp.bfloat16),
             pltpu.VMEM(lo.shape, jnp.bfloat16),
             pltpu.VMEM(hi.shape, jnp.bfloat16),
             pltpu.VMEM((COLS, 2 * wx_lo.shape[1]), jnp.bfloat16),
-            pltpu.SemaphoreType.DMA((4,)),
+            pltpu.SemaphoreType.DMA((4 + total // RANK,)),
         ],
         compiler_params=params(),
         cost_estimate=cost(4),
@@ -317,7 +322,7 @@
 
 
 def low_call(far, low_all, t):
-    each = 2
+    each = 4
     total = low_all.shape[0] // LANES * RANK
     return pl.pallas_call(
         low_kernel,
@@ -476,20 +481,38 @@
     )(near, count, first, left, right, t, acc, low)
 
 
-def upper_kernel(scale, ratio, terms, hx, upper):
-    total = terms[:COLS, :]
+def upper_kernel(scale, ratio, terms, hx, upper, total):
+    here = terms[:COLS, :]
     for m in range(1, terms.shape[0] // COLS):
-        total = total + terms[m * COLS : (m + 1) * COLS, :]
-    upper[:COLS, :] = (total * scale).astype(jnp.bfloat16) * jnp.bfloat16(ratio)
-    upper[COLS:, :] = hx[...]
+        here = here + terms[m * COLS : (m + 1) * COLS, :]
+    step = pl.program_id(0)
+
+    @pl.when(step == 0)
+    def _():
+        total[...] = here
+
+    @pl.when(step > 0)
+    def _():
+        total[...] += here
+
+    @pl.when(step == pl.num_programs(0) - 1)
+    def _():
+        upper[:COLS, :] = (total[...] * scale).astype(jnp.bfloat16) * jnp.bfloat16(ratio)
+        upper[COLS:, :] = hx[...]
 
 
 def upper_call(scale, ratio, terms, hx):
+    steps = 2
     return pl.pallas_call(
         lambda *refs: upper_kernel(scale, ratio, *refs),
         out_shape=jax.ShapeDtypeStruct((COLS + FEAT, RANK), jnp.bfloat16),
-        in_specs=[VMEM] * 2,
-        out_specs=VMEM,
+        grid=(steps,),
+        in_specs=[
+            pl.BlockSpec((terms.shape[0] // steps, RANK), lambda i: (i, 0)),
+            pl.BlockSpec(hx.shape, lambda i: (0, 0)),
+        ],
+        out_specs=pl.BlockSpec((COLS + FEAT, RANK), lambda i: (0, 0)),
+        scratch_shapes=[pltpu.VMEM((COLS, RANK), jnp.float32)],
         compiler_params=params(),
         name="high_sum",
     )(terms, hx)

time: 135 us -> 133 us (0.985); the launches traced: 132 us -> 132 us
  Pallas kernels: 80 us -> 86.9 us
  waiting for transfers between devices: 28.8 us -> 22 us
    all_gather x1, waiting for transfers between devices: 14.7 us -> 8.76 us  [per_device(): low_all = lax.all_gather(own, 'inner', axis=0, tiled=True)]
    pallas_call x1, Pallas kernels: 17.5 us -> 23.4 us  [near_own_call(): pl.pallas_call(near_own_kernel, out_shape=jax.ShapeDtypeStruct((LEAF_DEV...]
    pallas_call x1, Pallas kernels: 11.8 us -> 13.8 us  [near_side_call(): pl.pallas_call(lambda *refs: near_side_kernel(scales, *refs), out_shape=j...]
  transfers between devices with their start and end apart: 7 -> 7, of which waited for: 4 -> 4; matrix products, arithmetic and copies ran while one was open for 0% -> 0% of each run, Pallas kernels for 51% -> 56%
where the time goes in v5:
time: 133 us; the launch traced here: 132 us
  Pallas kernels  86.9 us (65%)
  waiting for transfers between devices  22 us (17%)
  between operations  13.5 us (10%)
  starting transfers between devices  7.36 us (6%)
  local copies, waits for them, and re-layouts  2.29 us (2%)
    pallas_call x1, Pallas kernels, near_own_call(): pl.pallas_call(near_own_kernel, out_shape=jax.ShapeDtypeStruct((LEAF_DEV...  23.4 us
    pallas_call x1, Pallas kernels, low_call(): pl.pallas_call(low_kernel, out_shape=jax.ShapeDtypeStruct((LEAF_DEV, COLS...  18.2 us
    pallas_call x1, Pallas kernels, tree_call(): pl.pallas_call(tree_kernel, out_shape=tuple((jax.ShapeDtypeStruct(s, jnp....  14.4 us
    pallas_call x1, Pallas kernels, near_side_call(): pl.pallas_call(lambda *refs: near_side_kernel(scales, *refs), out_shape=j...  13.8 us
    all_gather x1, waiting for transfers between devices, per_device(): low_all = lax.all_gather(own, 'inner', axis=0, tiled=True)  8.76 us
    all_gather x1, waiting for transfers between devices, per_device(): terms = lax.all_gather(term, 'inner', axis=0, tiled=True)  8.58 us
    pallas_call x1, Pallas kernels, high_call(): pl.pallas_call(lambda *refs: high_kernel(scale, *refs), out_shape=jax.Sha...  5.86 us
    pallas_call x1, Pallas kernels, own_call(): pl.pallas_call(own_kernel, out_shape=jax.ShapeDtypeStruct((LANES, RANK),...  4.81 us
  transfers between devices with their start and end apart: 7, of which 4 were waited for; matrix products, arithmetic and copies ran while one was open for 0% of the time, Pallas kernels for 56%

profile of v5, /device:TPU:0, one launch (start us, length us, event | category | flops | bytes accessed | tf_op | source)
XLA Modules:
  0.0 132.0 jit_solution(9937932889356295860)
XLA Ops:
  6.5 0.0 all-gather.3.cloned.1.call-start
  6.5 4.8 %own_skeleton.1 = bf16[128,128]{1,0:T(8,128)(2,1)} custom-call(s32[1,8192]{1,0:T(1,128)} %perm_hbm.2, s32[1,128]{1,0:T(1,128)} %skel_hbm.1, bf16[16,8192]{1,0:T(8,128)(2,1)} %events_hbm.3, bf16[64,8192]{1,0:T(8,128)(2,1)} %coeffs_hbm.3), custom_call_target="tpu_custom_call" | custom-call | flops 805306368 | bytes 4194304 | tf_op jit(solution)/shard_map/own_skeleton/pallas_call | solution.py:202
  11.4 0.0 all-gather.3.cloned.1.call-update
  11.4 0.0 all-gather.5.cloned.1.call-start
  11.4 14.4 %tree_rows.1 = (bf16[4096,128]{1,0:T(8,128)(2,1)}, bf16[4096,128]{1,0:T(8,128)(2,1)}, bf16[80,4096]{1,0:T(8,128)(2,1)}, bf16[80,4096]{1,0:T(8,128)(2,1)}, bf16[8192,128]{1,0:T(8,128)(2,1)}) custom-call(s32[1,8192]{1,0:T(1,128)} %perm_hbm.2, bf16[16,8192]{1,0:T(8,128)(2,1)} %events_hbm.3, bf16[64,8192]{1,0:T(8,128)(2,1)} %coeffs_hbm.3), custom_call_target="tpu_custom_call" | custom-call | flops 8053063680 | bytes 4194304 | tf_op jit(solution)/shard_map/tree_rows/pallas_call | solution.py:226
  25.9 1.3 %collective-permute-start = (bf16[80,4096]{1,0:T(8,128)(2,1)}, bf16[80,4096]{1,0:T(8,128)(2,1)S(1)}, u32[]{:S(2)}, u32[]{:S(2)}) collective-permute-start(bf16[80,4096]{1,0:T(8,128)(2,1)} %get-tuple-element.20.wx_hi), channel_id=1, source_target_pairs={{0,1},{1,2},{2,3},{3,4},{4,5},{5,6},{6,7},{7,8},{8,9},{9,10},{10,1... | collective-permute-start | bytes 1966088 | tf_op jit(solution)/shard_map/ppermute | solution.py:572
  27.2 1.3 collective-permute-start.1
  28.5 23.4 %near_own.1.refs_6_ = f32[17,64,512]{2,1,0:T(8,128)} custom-call(s32[16,32]{1,0:T(8,128)} %refs_0_.1, s32[16]{0:T(128)} %refs_1_.1, s32[1]{0:T(128)} %bitcast.first.refs_2_, bf16[4096,128]{1,0:T(8,128)(2,1)} %get-tuple-element.17.lo.lo_hbm, bf16[4096,128]{1,0:T(8,128)(2,1)} %get-tuple-element.18.hi.hi_hbm, bf16[80,4096]{1,0:T(8,128)(2,1)} %get-tuple-element.19.wx_lo, ...), custom_call_target="tpu_custom_call" | custom-call | flops 12079595520 | bytes 4194304 | tf_op jit(solution)/shard_map/near_own/pallas_call | solution.py:406
  51.9 8.8 %all-gather.3.cloned.1.call-done.low_all = bf16[4096,128]{1,0:T(8,128)(2,1)} async-done(((bf16[128,128]{1,0:T(8,128)(2,1)}), bf16[4096,128]{1,0:T(8,128)(2,1)}) %all-gather.3.cloned.1.call-update) | async-done | bytes 1048592 | tf_op jit(solution)/shard_map/all_gather | solution.py:569
  60.7 4.5 %high_term.1 = (f32[64,128]{1,0:T(8,128)}, bf16[16,128]{1,0:T(8,128)(2,1)}) custom-call(s32[1,128]{1,0:T(1,128)} %picks.1, bf16[4096,128]{1,0:T(8,128)(2,1)} %all-gather.3.cloned.1.call-done.low_all, bf16[4096,128]{1,0:T(8,128)(2,1)} %get-tuple-element.17.lo.lo_hbm, bf16[4096,128]{1,0:T(8,128)(2,1)} %get-tuple-element.18.hi.hi_hbm, ...), custom_call_target="tpu_custom_call" | custom-call | flops 805306368 | bytes 4194304 | tf_op jit(solution)/shard_map/high_term/pallas_call | solution.py:273
  65.2 0.0 all-gather.5.cloned.1.call-update
  65.2 18.2 %far_low.1.refs_7_ = f32[16,64,512]{2,1,0:T(8,128)} custom-call(s32[16,16]{1,0:T(8,128)} %far.1, bf16[4096,128]{1,0:T(8,128)(2,1)} %all-gather.3.cloned.1.call-done.low_all, bf16[8192,128]{1,0:T(8,128)(2,1)} %get-tuple-element.21.t_hbm.t.refs_5_.refs_3_), custom_call_target="tpu_custom_call" | custom-call | flops 12884901888 | bytes 4194304 | tf_op jit(solution)/shard_map/far_low/pallas_call | solution.py:327
  83.5 0.0 collective-permute-done.refs_3_
  83.5 0.0 copy-start
  83.5 0.0 collective-permute-done.1.refs_4_
  83.5 0.8 copy-done
  84.3 0.0 copy-start.1
  84.3 0.9 copy-done.1
  85.2 13.8 %near_sides.1.refs_4_ = f32[64,8192]{1,0:T(8,128)} custom-call(s32[16,32]{1,0:T(8,128)} %refs_0_.1, s32[16]{0:T(128)} %refs_1_.1, s32[1]{0:T(128)} %bitcast.first.refs_2_, bf16[80,4096]{1,0:T(8,128)(2,1)} %copy-done, bf16[80,4096]{1,0:T(8,128)(2,1)} %copy-done.1, bf16[8192,128]{1,0:T(8,128)(2,1)} %get-tuple-element.21.t_hbm.t.refs_5_.refs_3_, ...), custom_call_target="tpu_custom_call" | custom-call | flops 10066329600 | bytes 4194304 | tf_op jit(solution)/shard_map/near_sides/pallas_call | solution.py:463
  98.9 8.6 %all-gather.5.cloned.1.call-done.refs_0_ = f32[2048,128]{1,0:T(8,128)} async-done(((f32[64,128]{1,0:T(8,128)}), f32[2048,128]{1,0:T(8,128)}) %all-gather.5.cloned.1.call-update) | async-done | bytes 1048592 | tf_op jit(solution)/shard_map/all_gather | solution.py:578
  107.5 1.8 %high_sum.1 = bf16[80,128]{1,0:T(8,128)(2,1)} custom-call(f32[2048,128]{1,0:T(8,128)} %all-gather.5.cloned.1.call-done.refs_0_, bf16[16,128]{1,0:T(8,128)(2,1)} %get-tuple-element.26.refs_1_), custom_call_target="tpu_custom_call" | custom-call | tf_op jit(solution)/shard_map/high_sum/pallas_call | solution.py:506
  109.4 1.5 %collective-permute-start.2 = (bf16[80,128]{1,0:T(8,128)(2,1)}, bf16[80,128]{1,0:T(8,128)(2,1)S(1)}, u32[]{:S(2)}, u32[]{:S(2)}) collective-permute-start(bf16[80,128]{1,0:T(8,128)(2,1)} %high_sum.1), channel_id=1, source_target_pairs={{0,32},{32,0},{64,96},{96,64},{1,33},{33,1},{65,97},{97,65},{2,34}... | collective-permute-start | bytes 61448 | tf_op jit(solution)/shard_map/ppermute | solution.py:552
  110.8 2.7 %collective-permute-start.3 = (bf16[80,128]{1,0:T(8,128)(2,1)}, bf16[80,128]{1,0:T(8,128)(2,1)S(1)}, u32[]{:S(2)}, u32[]{:S(2)}) collective-permute-start(bf16[80,128]{1,0:T(8,128)(2,1)} %high_sum.1), channel_id=1, source_target_pairs={{0,64},{32,96},{64,0},{96,32},{1,65},{33,97},{65,1},{97,33},{2,66}... | collective-permute-start | bytes 61448 | tf_op jit(solution)/shard_map/ppermute | solution.py:552
  113.5 0.5 collective-permute-start.4
  114.1 0.0 collective-permute-done.2.refs_0_
  114.1 0.0 copy-start.2
  114.1 2.3 %collective-permute-done.3.refs_1_ = bf16[80,128]{1,0:T(8,128)(2,1)S(1)} collective-permute-done((bf16[80,128]{1,0:T(8,128)(2,1)}, bf16[80,128]{1,0:T(8,128)(2,1)S(1)}, u32[]{:S(2)}, u32[]{:S(2)}) %collective-permute-start.3) | collective-permute-done | bytes 20512 | tf_op jit(solution)/shard_map/ppermute | solution.py:552
  116.3 2.4 %collective-permute-done.4.refs_2_ = bf16[80,128]{1,0:T(8,128)(2,1)S(1)} collective-permute-done((bf16[80,128]{1,0:T(8,128)(2,1)}, bf16[80,128]{1,0:T(8,128)(2,1)S(1)}, u32[]{:S(2)}, u32[]{:S(2)}) %collective-permute-start.4) | collective-permute-done | bytes 20512 | tf_op jit(solution)/shard_map/ppermute | solution.py:552
  118.7 0.0 copy-done.2
  118.7 0.0 copy-done.3
  118.7 0.6 copy-done.4
  119.3 5.9 %high_out.1 = bf16[64,8192]{1,0:T(8,128)(2,1)} custom-call(bf16[80,128]{1,0:T(8,128)(2,1)} %copy-done.2, bf16[80,128]{1,0:T(8,128)(2,1)} %copy-done.3, bf16[80,128]{1,0:T(8,128)(2,1)} %copy-done.4, bf16[8192,128]{1,0:T(8,128)(2,1)} %get-tuple-element.21.t_hbm.t.refs_5_.refs_3_, f32[64,8192]{1,0:T(8,128)} %near_sides.1.refs_4_), custom_call_target="tpu_custom_call" | custom-call | flops 2415919104 | bytes 4194304 | tf_op jit(solution)/shard_map/high_out/pallas_call | solution.py:534
  (2 shorter events, 0.0 us)
Async XLA Ops:
  6.5 54.1 %all-gather.3.cloned.1.call-start = ((), (), s32[]{:S(2)}) async-start(), calls=%async_computation | async-start | bytes 1081344 | tf_op jit(solution)/shard_map/all_gather | solution.py:569
  11.4 96.1 %all-gather.5.cloned.1.call-start = ((), (), s32[]{:S(2)}) async-start(), calls=%async_computation.1 | async-start | bytes 1081344 | tf_op jit(solution)/shard_map/all_gather | solution.py:578
  25.9 57.6 %collective-permute-start = (bf16[80,4096]{1,0:T(8,128)(2,1)}, bf16[80,4096]{1,0:T(8,128)(2,1)S(1)}, u32[]{:S(2)}, u32[]{:S(2)}) collective-permute-start(bf16[80,4096]{1,0:T(8,128)(2,1)} %get-tuple-element.20.wx_hi), channel_id=1, source_target_pairs={{0,1},{1,2},{2,3},{3,4},{4,5},{5,6},{6,7},{7,8},{8,9},{9,10},{10,1... | collective-permute-start | bytes 1966088 | tf_op jit(solution)/shard_map/ppermute | solution.py:572
  27.2 56.3 %collective-permute-start.1 = (bf16[80,4096]{1,0:T(8,128)(2,1)}, bf16[80,4096]{1,0:T(8,128)(2,1)S(1)}, u32[]{:S(2)}, u32[]{:S(2)}) collective-permute-start(bf16[80,4096]{1,0:T(8,128)(2,1)} %get-tuple-element.19.wx_lo), channel_id=1, source_target_pairs={{1,0},{2,1},{3,2},{4,3},{5,4},{6,5},{7,6},{8,7},{9,8},{10,9},{11,1... | collective-permute-start | bytes 1966088 | tf_op jit(solution)/shard_map/ppermute | solution.py:573
  83.5 0.8 copy-start
  84.3 0.9 copy-start.1
  109.4 4.7 %collective-permute-start.2 = (bf16[80,128]{1,0:T(8,128)(2,1)}, bf16[80,128]{1,0:T(8,128)(2,1)S(1)}, u32[]{:S(2)}, u32[]{:S(2)}) collective-permute-start(bf16[80,128]{1,0:T(8,128)(2,1)} %high_sum.1), channel_id=1, source_target_pairs={{0,32},{32,0},{64,96},{96,64},{1,33},{33,1},{65,97},{97,65},{2,34}... | collective-permute-start | bytes 61448 | tf_op jit(solution)/shard_map/ppermute | solution.py:552
  110.8 5.5 %collective-permute-start.3 = (bf16[80,128]{1,0:T(8,128)(2,1)}, bf16[80,128]{1,0:T(8,128)(2,1)S(1)}, u32[]{:S(2)}, u32[]{:S(2)}) collective-permute-start(bf16[80,128]{1,0:T(8,128)(2,1)} %high_sum.1), channel_id=1, source_target_pairs={{0,64},{32,96},{64,0},{96,32},{1,65},{33,97},{65,1},{97,33},{2,66}... | collective-permute-start | bytes 61448 | tf_op jit(solution)/shard_map/ppermute | solution.py:552
  113.5 5.2 %collective-permute-start.4 = (bf16[80,128]{1,0:T(8,128)(2,1)}, bf16[80,128]{1,0:T(8,128)(2,1)S(1)}, u32[]{:S(2)}, u32[]{:S(2)}) collective-permute-start(bf16[80,128]{1,0:T(8,128)(2,1)} %high_sum.1), channel_id=1, source_target_pairs={{0,96},{32,64},{64,32},{96,0},{1,97},{33,65},{65,33},{97,1},{2,98}... | collective-permute-start | bytes 61448 | tf_op jit(solution)/shard_map/ppermute | solution.py:552
  114.1 4.7 %copy-start.2 = (bf16[80,128]{1,0:T(8,128)(2,1)}, bf16[80,128]{1,0:T(8,128)(2,1)S(1)}, u32[]{:S(2)}) copy-start(bf16[80,128]{1,0:T(8,128)(2,1)S(1)} %collective-permute-done.2.refs_0_) | copy-start | bytes 61444
  116.3 2.4 %copy-start.3 = (bf16[80,128]{1,0:T(8,128)(2,1)}, bf16[80,128]{1,0:T(8,128)(2,1)S(1)}, u32[]{:S(2)}) copy-start(bf16[80,128]{1,0:T(8,128)(2,1)S(1)} %collective-permute-done.3.refs_1_) | copy-start | bytes 61444
  118.7 0.6 copy-start.4
Sparse Core Ops, SparseCore 0:
  11.5 49.1 all-gather.2
  65.4 42.1 all-gather.4
